TPU v7x, 32 devices: a whole 2x2x4 slice. The times are simulated.
32 devices in a mesh: lat: 4 (over y, x), lon: 8 (over z, core).
Axes of the slice: x: 2, y: 2, z: 4, core: 2. Of those that a mesh axis runs over, the one named last changes fastest.
Arguments:
- grid_field: bfloat16 [128, 1024, 192], P('lat', 'lon'), may hold values from -6 to 6
- conv_weight: bfloat16 [9, 192, 192], replicated, may hold values from -0.15625 to 0.15625
- observed: float32 [8192, 128], P(('lat', 'lon')), may hold values from -6 to 6
- hidden_mask: int32 [8192, 128], P(('lat', 'lon')), may hold values 0 or 1
- tile_route: int32 [8192, 1], P(('lat', 'lon')), may hold values from 0 to 31; in each aligned block of 256 rows (0 to 255, 256 to 511, ...) at most 16 rows name the same one
- station_spot: int32 [8192], P(('lat', 'lon')), may hold values from 0 to 62991
- neighbours: int32 [8192, 16], P(('lat', 'lon')), may hold values from 0 to 255
- neighbour_count: int32 [8192], P(('lat', 'lon')), may hold values from 2 to 16
- edge_bias: float32 [8192, 16], P(('lat', 'lon')), may hold values from -9 to 300
- live_count: int32 [32], P(('lat', 'lon')), may hold values from 32 to 256, as said below
- in_weight: bfloat16 [448, 192], replicated, may hold values from -0.25 to 0.25
- norm_gain: float32 [192], replicated, may hold values from 0.1 to 1.9
- qkv_weight: bfloat16 [192, 576], replicated, may hold values from -0.4375 to 0.4375
- out_weight: bfloat16 [192, 192], replicated, may hold values from -0.4375 to 0.4375
- final_gain: float32 [192], replicated, may hold values from 0.1 to 1.9
- head_weight: bfloat16 [192, 128], replicated, may hold values from -0.4375 to 0.4375
Outputs:
- predicted: float32 [8192, 128], P(('lat', 'lon'))
- grid_gradient: float32 [128, 1024, 192], P('lat', 'lon')
Inputs may be any that keep to these rules, and one draw needn't show every extreme that they name: `tile_route`: within the stations of one region no tile is named by more than 16 stations, and some tile reaches 16 in every draw. `neighbours`: entries at positions j >= neighbour_count are padding. Stations 0 to live_count - 1 of a region are present; some region has all 256 in every draw.
All inputs are finite; a program needn't handle non-finite values. No bound on the sum of `hidden_mask` on one device may be relied on, other than what follows from the above.
Results may differ from a plain program's by a relative error of at most 0.02.
Values may be sent and summed in bfloat16 or wider, within the bound.
No kernel may reach another device: no remote copies, remote signals or barrier semaphores. Data moves between devices by JAX's collectives and lax.ppermute only.
A program may use at most 192 MiB of HBM per device.

v0:
```python
import functools
import math

import jax
import jax.numpy as jnp
from jax import lax
from jax.experimental import pallas as pl
from jax.experimental.pallas import tpu as pltpu
from jax.sharding import PartitionSpec as P

HEADS = 3
EPS = 1e-06
NEG = -1e30
AXES = ("lat", "lon")
F32 = jnp.float32
BF16 = jnp.bfloat16
VMEM = pltpu.VMEM


def nn(a, b):
    return lax.dot_general(a, b, (((1,), (0,)), ((), ())), preferred_element_type=F32)


def nt(a, b):
    return lax.dot_general(a, b, (((1,), (1,)), ((), ())), preferred_element_type=F32)


def tn(a, b):
    return lax.dot_general(a, b, (((0,), (0,)), ((), ())), preferred_element_type=F32)


def iota(shape, dim):
    return lax.broadcasted_iota(jnp.int32, shape, dim)


def iota_f(shape, dim):
    return iota(shape, dim).astype(F32)


def onehot(test):
    return jnp.where(test, 1.0, 0.0).astype(BF16)


def up(n, m):
    return -(-n // m) * m


def whole(count):
    return [pl.BlockSpec(memory_space=VMEM)] * count


def route_parts(route, wide):
    stations = route.shape[0]
    member = onehot(route == iota((stations, wide), 1))
    same = nt(member, member)
    row, col = iota((stations, stations), 0), iota((stations, stations), 1)
    rank_col = jnp.sum(jnp.where(col < row, same, 0.0), axis=1, keepdims=True)
    rank_row = jnp.sum(jnp.where(row < col, same, 0.0), axis=0, keepdims=True)
    names = jnp.where(iota((8, wide), 0) >= 0, iota((8, wide), 1), 0).astype(BF16)
    route_row = nt(names, member)[0:1]
    return rank_col, rank_row, route_row


def request_kernel(capacity, route_ref, spot_ref, req_ref):
    regions = req_ref.shape[0]
    stations = route_ref.shape[0]
    rank_col, _, route_row = route_parts(route_ref[...], up(regions, 128))
    spot = spot_ref[...].astype(F32)
    high = jnp.floor(spot * (1.0 / 256.0))
    low = spot - 256.0 * high
    member_t = route_row == iota_f((regions, stations), 0)
    ranked = onehot(rank_col == iota_f((stations, 128), 1))
    req = 256.0 * nn(jnp.where(member_t, high, 0.0).astype(BF16), ranked) + nn(
        jnp.where(member_t, low, 0.0).astype(BF16), ranked
    )
    req_ref[...] = req[:, :capacity].astype(jnp.int32)


def make_requests(route, spot, regions, capacity):
    return pl.pallas_call(
        functools.partial(request_kernel, capacity),
        out_shape=jax.ShapeDtypeStruct((regions, capacity), jnp.int32),
        in_specs=whole(2),
        out_specs=pl.BlockSpec(memory_space=VMEM),
        name="requests",
    )(route, spot.reshape(1, -1))


def conv_weights(w_ref, wc, back):
    ch = w_ref.shape[1]
    deep = up(ch, 128)
    wc[...] = jnp.zeros_like(wc)
    for dy in range(3):
        for dx in range(3):
            if back:
                wc[dx, :, dy * deep : dy * deep + ch] = w_ref[8 - (3 * dy + dx)]
            else:
                wc[dx, dy * deep : dy * deep + ch, :] = w_ref[3 * dy + dx]


def conv_kernel(back, block, x_ref, w_ref, *refs):
    add_ref = refs[0] if back else None
    o_ref, xs, wc = refs[-3:]
    rows, cols, ch = x_ref.shape
    deep = xs.shape[2]
    step = pl.program_id(0)

    @pl.when(step == 0)
    def _():
        conv_weights(w_ref, wc, back)
        xs[0] = jnp.zeros((cols, deep), BF16)
        xs[rows + 1] = jnp.zeros((cols, deep), BF16)
        pad = jnp.zeros((block, cols, deep - ch), BF16)

        def fill(i, carry):
            r = i * block
            xs[pl.ds(r + 1, block)] = jnp.concatenate([x_ref[pl.ds(r, block)], pad], axis=2)
            return carry

        lax.fori_loop(0, rows // block, fill, 0)

    r0 = step * block
    lhs = jnp.concatenate(
        [xs[pl.ds(r0 + dy, block)].reshape(block * cols, deep) for dy in range(3)], axis=1
    )
    dot = nt if back else nn
    col = iota((block * cols, ch), 0) % cols
    total = dot(lhs, wc[1])
    total = total + jnp.where(col == 0, 0.0, pltpu.roll(dot(lhs, wc[0]), 1, 0))
    total = total + jnp.where(
        col == cols - 1, 0.0, pltpu.roll(dot(lhs, wc[2]), block * cols - 1, 0)
    )
    total = total.reshape(block, cols, ch)
    if back:
        total = total + add_ref[...]
    o_ref[...] = total


def conv_core(x, taps, add=None, block=8):
    rows, cols, ch = x.shape
    back = add is not None
    deep = up(ch, 128)
    wc = (3, ch, 3 * deep) if back else (3, 3 * deep, ch)
    rolling = pl.BlockSpec((block, cols, ch), lambda i: (i, 0, 0))
    return pl.pallas_call(
        functools.partial(conv_kernel, back, block),
        grid=(rows // block,),
        out_shape=jax.ShapeDtypeStruct((rows, cols, ch), F32),
        in_specs=whole(2) + ([rolling] if back else []),
        out_specs=rolling,
        scratch_shapes=[VMEM((rows + 2, cols, deep), BF16), VMEM(wc, BF16)],
        name="conv_back" if back else "conv_core",
    )(*((x, taps, add) if back else (x, taps)))


def border_rows(top, w_ref, dy, back):
    cols, ch = top.shape
    dot = nt if back else nn
    tap = lambda dx: w_ref[8 - (3 * dy + dx)] if back else w_ref[3 * dy + dx]
    col = iota((cols, ch), 0)
    total = dot(top, tap(1))
    total = total + jnp.where(col == 0, 0.0, pltpu.roll(dot(top, tap(0)), 1, 0))
    return total + jnp.where(col == cols - 1, 0.0, pltpu.roll(dot(top, tap(2)), cols - 1, 0))


def border_cols(side, w_ref, dx, back, rows):
    dot = nt if back else nn
    total = None
    for dy in range(3):
        tap = w_ref[8 - (3 * dy + dx)] if back else w_ref[3 * dy + dx]
        term = dot(side, tap)[dy : dy + rows]
        total = term if total is None else total + term
    return total


def fine_cell(spot, cols):
    fine = float(4 * (cols - 1))
    fr = jnp.floor((spot + 0.5) * (1.0 / fine))
    fc = spot - fine * fr
    r, c = jnp.floor(fr * 0.25), jnp.floor(fc * 0.25)
    return r, c, (fr - 4.0 * r + 0.5) * 0.25, (fc - 4.0 * c + 0.5) * 0.25


def hat(cell, at, frac):
    return jnp.where(cell == at, 1.0 - frac, jnp.where(cell == at + 1.0, frac, 0.0))


def split_spots(asked):
    high = jnp.floor(asked * (1.0 / 256.0))
    return high.astype(BF16), (asked - 256.0 * high).astype(BF16)


def spots_column(asked, slots):
    regions, capacity = asked.shape
    high, low = split_spots(asked)
    k, t = iota((slots, regions), 0), iota((slots, regions), 1)
    pick = onehot((k >= t * capacity) & (k < (t + 1) * capacity))
    both = 256.0 * nn(pick, high) + nn(pick, low)
    k, c = iota((slots, capacity), 0), iota((slots, capacity), 1)
    return jnp.sum(jnp.where(k % capacity == c, both, 0.0), axis=1, keepdims=True)


def spots_row(asked, slots):
    regions, capacity = asked.shape
    high, low = split_spots(asked)
    t, k = iota((regions, slots), 0), iota((regions, slots), 1)
    pick = onehot((k >= t * capacity) & (k < (t + 1) * capacity))
    both = 256.0 * tn(high, pick) + tn(low, pick)
    c, k = iota((capacity, slots), 0), iota((capacity, slots), 1)
    return jnp.sum(jnp.where(k % capacity == c, both, 0.0), axis=0, keepdims=True)


def sample_kernel(
    y_ref, x_ref, w_ref, asked_ref, top_ref, bot_ref, left_ref, right_ref, ans_ref, gate_ref, field, fix
):
    rows, cols, ch = x_ref.shape
    slots = ans_ref.shape[0] * ans_ref.shape[1]
    y_top = border_rows(top_ref[...], w_ref, 0, False)
    y_bot = border_rows(bot_ref[...], w_ref, 2, False)
    fix[0] = border_cols(left_ref[...], w_ref, 0, False, rows)
    fix[1] = border_cols(right_ref[...], w_ref, 2, False, rows)
    col = iota((cols, ch), 0)

    def gates(r, carry):
        pre = y_ref[r]
        pre = pre + jnp.where(r == 0, y_top, 0.0) + jnp.where(r == rows - 1, y_bot, 0.0)
        pre = pre + jnp.where(col == 0, fix[0, pl.ds(r, 1)], 0.0)
        pre = pre + jnp.where(col == cols - 1, fix[1, pl.ds(r, 1)], 0.0)
        sg = 1.0 / (1.0 + jnp.exp(-pre))
        field[pl.ds(r * cols, cols), :] = (x_ref[r].astype(F32) + pre * sg).astype(BF16)
        gate_ref[r] = (sg * (1.0 + pre * (1.0 - sg))).astype(BF16)
        return carry

    lax.fori_loop(0, rows, gates, 0)

    spot = spots_column(asked_ref[...].astype(F32), slots)
    r, c, a, b = fine_cell(spot, cols)
    by_row = hat(iota_f((slots, rows), 1), r, a)
    by_col = hat(iota_f((slots, cols), 1), c, b)
    total = jnp.zeros((slots, ch), F32)
    for pair in range(0, rows, 2):
        weights = jnp.concatenate(
            [(by_row[:, pair + k : pair + k + 1] * by_col).astype(BF16) for k in range(2)], axis=1
        )
        total = total + nn(weights, field[pair * cols : (pair + 2) * cols, :])
    ans_ref[...] = total.astype(BF16).reshape(ans_ref.shape)


def sample(y, x, taps, asked, top, bot, left, right):
    rows, cols, ch = x.shape
    return pl.pallas_call(
        sample_kernel,
        out_shape=(
            jax.ShapeDtypeStruct(asked.shape + (ch,), BF16),
            jax.ShapeDtypeStruct((rows, cols, ch), BF16),
        ),
        in_specs=whole(8),
        out_specs=(pl.BlockSpec(memory_space=VMEM),) * 2,
        scratch_shapes=[VMEM((rows * cols, ch), BF16), VMEM((2, rows, ch), F32)],
        name="sample",
    )(y, x, taps, asked, top, bot, left, right)


def spread_kernel(asked_ref, inc_ref, gate_ref, df_ref, dp_ref, by_row):
    rows, cols, ch = gate_ref.shape
    slots = inc_ref.shape[0] * inc_ref.shape[1]
    spot = spots_row(asked_ref[...].astype(F32), slots)
    r, c, a, b = fine_cell(spot, cols)
    by_row[...] = hat(iota_f((rows, slots), 0), r, a)
    by_col = hat(iota_f((cols, slots), 0), c, b)
    incoming = inc_ref[...].reshape(slots, ch)

    def body(i, carry):
        weights = (by_row[pl.ds(i, 1)] * by_col).astype(BF16)
        d_field = nn(weights, incoming)
        df_ref[i] = d_field
        dp_ref[i] = (d_field * gate_ref[i].astype(F32)).astype(BF16)
        return carry

    lax.fori_loop(0, rows, body, 0)


def spread(asked, incoming, gate):
    rows, cols, ch = gate.shape
    slots = incoming.shape[0] * incoming.shape[1]
    return pl.pallas_call(
        spread_kernel,
        out_shape=(
            jax.ShapeDtypeStruct(gate.shape, F32),
            jax.ShapeDtypeStruct(gate.shape, BF16),
        ),
        in_specs=whole(3),
        out_specs=(pl.BlockSpec(memory_space=VMEM),) * 2,
        scratch_shapes=[VMEM((rows, slots), F32)],
        name="spread",
    )(asked, incoming, gate)


def edge_kernel(g_ref, w_ref, top_ref, bot_ref, left_ref, right_ref, o_ref, line, side, sem):
    rows, cols, ch = g_ref.shape
    tail = cols - side.shape[2]
    spots = (
        (o_ref.at[0], line.at[0]),
        (o_ref.at[rows - 1], line.at[1]),
        (o_ref.at[pl.ds(1, rows - 2), pl.ds(0, 8)], side.at[0]),
        (o_ref.at[pl.ds(1, rows - 2), pl.ds(tail, 8)], side.at[1]),
    )
    loads = [pltpu.make_async_copy(there, here, sem.at[i]) for i, (there, here) in enumerate(spots)]
    for load in loads:
        load.start()
    y_left = border_cols(left_ref[...], w_ref, 0, True, rows)
    y_right = border_cols(right_ref[...], w_ref, 2, True, rows)
    col = iota((cols, ch), 0)
    near = iota((rows - 2, 8, ch), 1)
    y_lines = []
    for at, ref, dy in ((0, top_ref, 0), (rows - 1, bot_ref, 2)):
        y = border_rows(ref[...], w_ref, dy, True)
        y = y + jnp.where(col == 0, y_left[at : at + 1], 0.0)
        y_lines.append(y + jnp.where(col == cols - 1, y_right[at : at + 1], 0.0))
    for load in loads:
        load.wait()
    for k in range(2):
        line[k] = line[k] + y_lines[k]
    side[0] = side[0] + jnp.where(near == 0, y_left[1 : rows - 1][:, None, :], 0.0)
    side[1] = side[1] + jnp.where(near == 7, y_right[1 : rows - 1][:, None, :], 0.0)
    stores = [pltpu.make_async_copy(here, there, sem.at[i]) for i, (there, here) in enumerate(spots)]
    for store in stores:
        store.start()
    for store in stores:
        store.wait()


def add_edges(grad, taps, top, bot, left, right):
    rows, cols, ch = grad.shape
    return pl.pallas_call(
        edge_kernel,
        out_shape=jax.ShapeDtypeStruct(grad.shape, F32),
        in_specs=[pl.BlockSpec(memory_space=pl.ANY)] + whole(5),
        out_specs=pl.BlockSpec(memory_space=pl.ANY),
        scratch_shapes=[
            VMEM((2, cols, ch), F32),
            VMEM((2, rows - 2, 8, ch), F32),
            pltpu.SemaphoreType.DMA((4,)),
        ],
        input_output_aliases={0: 0},
        name="edges",
    )(grad, taps, top, bot, left, right)


def prepare_kernel(
    capacity, live_ref, route_ref, near_ref, count_ref, bias_ref, obs_ref, mask_ref, w_ref,
    to_ref, from_ref, bias_out, part_ref,
):
    stations, slots = to_ref.shape
    features = obs_ref.shape[1]
    regions = slots // capacity
    rank_col, rank_row, route_row = route_parts(route_ref[...], up(regions, 128))
    slot_col = route_ref[...].astype(F32) * capacity + rank_col
    slot_row = route_row * capacity + rank_row
    to_ref[...] = onehot(slot_col == iota_f((stations, slots), 1))
    from_ref[...] = onehot(slot_row == iota_f((slots, stations), 0))

    live = live_ref[0]
    width = near_ref.shape[1]
    pad = jnp.zeros((stations, 128 - width), F32)
    turn = lambda v: jnp.concatenate([v, pad], axis=1).T[:width]
    near = turn(near_ref[...].astype(F32))
    bias = turn(bias_ref[...])
    live_f = live.astype(F32)
    valid = (iota((width, stations), 0) < count_ref[...]) & (near < live_f)
    near = jnp.where(valid, near, -1.0)
    bias = jnp.where(valid, bias, NEG)
    me = iota_f((width, stations), 1)
    own = near == me
    top = jnp.where(own, jnp.maximum(bias, 0.0), bias)
    for d in range(1, width):
        same = pltpu.roll(near, d, 0) == near
        top = jnp.maximum(top, jnp.where(same, pltpu.roll(bias, d, 0), NEG))
    mass = jnp.exp(bias - top) + jnp.where(own, jnp.exp(jnp.minimum(-top, 0.0)), 0.0)
    for d in range(1, width):
        same = pltpu.roll(near, d, 0) == near
        other = jnp.exp(jnp.minimum(pltpu.roll(bias, d, 0) - top, 0.0))
        mass = mass + jnp.where(same, other, 0.0)
    merged = top + jnp.log(mass)
    own_top = jnp.max(jnp.where(own, jnp.maximum(bias, 0.0), 0.0), axis=0, keepdims=True)
    own_mass = jnp.exp(-own_top) + jnp.sum(
        jnp.where(own, jnp.exp(jnp.minimum(bias - own_top, 0.0)), 0.0), axis=0, keepdims=True
    )
    own_bias = own_top + jnp.log(own_mass)
    key = iota_f((stations, stations), 0)
    table = jnp.full((stations, stations), NEG, F32)
    for j in range(width):
        table = jnp.where(key == near[j : j + 1], merged[j : j + 1], table)
    bias_out[...] = jnp.where(key == iota_f((stations, stations), 1), own_bias, table)

    mask = mask_ref[...].astype(F32)
    part_ref[...] = nn((obs_ref[...] * (1.0 - mask)).astype(BF16), w_ref[:features]) + nn(
        mask.astype(BF16), w_ref[features : 2 * features]
    )


def prepare(route, near, count, bias, live, obs, mask, w_in, slots, capacity):
    stations = obs.shape[0]
    return pl.pallas_call(
        functools.partial(prepare_kernel, capacity),
        out_shape=(
            jax.ShapeDtypeStruct((stations, slots), BF16),
            jax.ShapeDtypeStruct((slots, stations), BF16),
            jax.ShapeDtypeStruct((stations, stations), F32),
            jax.ShapeDtypeStruct((stations, w_in.shape[1]), F32),
        ),
        in_specs=[pl.BlockSpec(memory_space=pltpu.SMEM)] + whole(7),
        out_specs=(pl.BlockSpec(memory_space=VMEM),) * 4,
        name="prepare",
    )(live, route, near, count.reshape(1, -1), bias, obs, mask, w_in)


def station_kernel(
    live_ref, ans_ref, to_ref, from_ref, bias_ref, part_ref, obs_ref, mask_ref, w_in, g1_ref, w_qkv, w_out,
    g2_ref, w_head, pred_ref, out_ref, prob, d_qkv,
):
    stations, slots = to_ref.shape
    ch = part_ref.shape[1]
    dim = ch // HEADS
    scale = 1.0 / math.sqrt(dim)
    below = w_in.shape[0] - ch
    inv = 1.0 / ch
    g1, g2 = g1_ref[...], g2_ref[...]

    interp = nn(to_ref[...], ans_ref[...].reshape(slots, ch)).astype(BF16)
    embedded = part_ref[...] + nn(interp, w_in[below:])
    r1 = lax.rsqrt(jnp.sum(embedded * embedded, axis=1, keepdims=True) * inv + EPS)
    unit1 = embedded * r1
    projected = nn((unit1 * g1).astype(BF16), w_qkv[...]).astype(BF16)
    cut = lambda block, h: projected[:, block * ch + h * dim : block * ch + (h + 1) * dim]
    residual = embedded
    for h in range(HEADS):
        score = nt(cut(1, h), cut(0, h)) * scale + bias_ref[...]
        weight = jnp.exp(score - jnp.max(score, axis=0, keepdims=True))
        p = weight * (1.0 / jnp.sum(weight, axis=0, keepdims=True))
        prob[h] = p
        mixed = tn(p.astype(BF16), cut(2, h))
        residual = residual + nn(mixed.astype(BF16), w_out[h * dim : (h + 1) * dim])
    r2 = lax.rsqrt(jnp.sum(residual * residual, axis=1, keepdims=True) * inv + EPS)
    unit2 = residual * r2
    alive = jnp.where(iota((stations, 1), 0) < live_ref[0], 1.0, 0.0)
    predicted = nn((unit2 * g2).astype(BF16), w_head[...]) * alive
    pred_ref[...] = predicted

    d_pred = (2.0 * alive) * mask_ref[...].astype(F32) * (predicted - obs_ref[...])
    u2 = nt(d_pred.astype(BF16), w_head[...]).astype(BF16).astype(F32) * g2
    d_res = r2 * (u2 - unit2 * (jnp.sum(u2 * unit2, axis=1, keepdims=True) * inv))
    d_res_b = d_res.astype(BF16)
    for h in range(HEADS):
        p = prob[h]
        d_mixed = nt(d_res_b, w_out[h * dim : (h + 1) * dim]).astype(BF16)
        d_p = nt(cut(2, h), d_mixed)
        d_score = p * (d_p - jnp.sum(p * d_p, axis=0, keepdims=True))
        d_score = (d_score * scale).astype(BF16)
        d_qkv[:, h * dim : (h + 1) * dim] = tn(d_score, cut(1, h)).astype(BF16)
        d_qkv[:, ch + h * dim : ch + (h + 1) * dim] = nn(d_score, cut(0, h)).astype(BF16)
        d_qkv[:, 2 * ch + h * dim : 2 * ch + (h + 1) * dim] = nn(p.astype(BF16), d_mixed).astype(BF16)
    u1 = nt(d_qkv[...], w_qkv[...]).astype(BF16).astype(F32) * g1
    d_emb = d_res + r1 * (u1 - unit1 * (jnp.sum(u1 * unit1, axis=1, keepdims=True) * inv))
    d_interp = nt(d_emb.astype(BF16), w_in[below:]).astype(BF16)
    out_ref[...] = nn(from_ref[...], d_interp).astype(BF16).reshape(out_ref.shape)


def stations_pass(live, answer, prepared, obs, mask, w_in, g1, w_qkv, w_out, g2, w_head):
    to, back, table, part = prepared
    n, ch = part.shape
    return pl.pallas_call(
        station_kernel,
        out_shape=(
            jax.ShapeDtypeStruct(obs.shape, F32),
            jax.ShapeDtypeStruct(answer.shape, BF16),
        ),
        in_specs=[pl.BlockSpec(memory_space=pltpu.SMEM)] + whole(13),
        out_specs=(pl.BlockSpec(memory_space=VMEM),) * 2,
        scratch_shapes=[VMEM((HEADS, n, n), F32), VMEM((n, 3 * ch), BF16)],
        name="stations",
    )(
        live, answer, to, back, table, part, obs, mask, w_in, g1.reshape(1, -1), w_qkv, w_out,
        g2.reshape(1, -1), w_head,
    )


def shift(x, axis, step, wrap):
    n = lax.axis_size(axis)
    pairs = [(i, (i + step) % n) for i in range(n) if wrap or 0 <= i + step < n]
    return lax.ppermute(x, axis, pairs)


def halo(x):
    rows, cols, ch = x.shape
    left = shift(x[:, cols - 1], "lon", 1, True)
    right = shift(x[:, 0], "lon", -1, True)
    low = jnp.concatenate([x[rows - 1], left[rows - 1 :], right[rows - 1 :]])
    high = jnp.concatenate([x[0], left[:1], right[:1]])
    top = shift(low, "lat", 1, False)
    bot = shift(high, "lat", -1, False)
    left = jnp.concatenate([top[cols : cols + 1], left, bot[cols : cols + 1]])
    right = jnp.concatenate([top[cols + 1 :], right, bot[cols + 1 :]])
    return top[:cols], bot[:cols], left, right


def exchange(x):
    return lax.all_to_all(x, AXES, split_axis=0, concat_axis=0, tiled=True)


def on_device(
    grid_field,
    conv_weight,
    observed,
    hidden_mask,
    tile_route,
    station_spot,
    neighbours,
    neighbour_count,
    edge_bias,
    live_count,
    in_weight,
    norm_gain,
    qkv_weight,
    out_weight,
    final_gain,
    head_weight,
):
    regions = lax.axis_size("lat") * lax.axis_size("lon")
    capacity = max(2, 2 * observed.shape[0] // regions)
    slots = regions * capacity
    asked = exchange(make_requests(tile_route, station_spot, regions, capacity))
    borders = halo(grid_field)
    y = conv_core(grid_field, conv_weight)
    answer, gate = sample(y, grid_field, conv_weight, asked, *borders)
    answer = exchange(answer)
    prepared = prepare(
        tile_route, neighbours, neighbour_count, edge_bias, live_count, observed, hidden_mask, in_weight,
        slots, capacity,
    )
    predicted, outgoing = stations_pass(
        live_count, answer, prepared, observed, hidden_mask, in_weight, norm_gain, qkv_weight, out_weight,
        final_gain, head_weight,
    )
    d_field, d_pre = spread(asked, exchange(outgoing), gate)
    borders = halo(d_pre)
    grad = conv_core(d_pre, conv_weight, d_field)
    return predicted, add_edges(grad, conv_weight, *borders)


def solution(mesh):
    split = P(AXES, None)
    one = P(AXES)
    in_specs = (
        P("lat", "lon", None), P(), split, split, split, one, split, one, split, one,
        P(), P(), P(), P(), P(), P(),
    )
    out_specs = (split, P("lat", "lon", None))
    return jax.shard_map(
        on_device, mesh=mesh, in_specs=in_specs, out_specs=out_specs, check_vma=False
    )
```

profile of v0, /device:TPU:0, one launch (start us, length us, event | category | flops | bytes accessed | tf_op | source)
XLA Modules:
  0.0 137.6 jit_solution(6343679786915091871)
XLA Ops:
  0.6 1.5 %copy.35.route_ref = s32[256,1]{1,0:T(8,128)} copy(s32[256,1]{0,1:T(1,128)} %param.20) | data formatting | bytes 2048 | tf_op args[4]
  2.1 2.0 %requests.1 = s32[32,16]{1,0:T(8,128)} custom-call(s32[256,1]{1,0:T(8,128)} %copy.35.route_ref, s32[1,256]{1,0:T(1,128)} %bitcast.27), custom_call_target="tpu_custom_call" | custom-call | tf_op jit(solution)/shard_map/requests/pallas_call | solution.py:80
  4.1 7.3 %all-to-all-start = ((s32[32,1,16]{2,1,0:T(1,128)}), s32[32,1,16]{2,1,0:T(1,128)S(1)}, u32[]{:S(2)}, u32[]{:S(2)}) async-start(s32[32,1,16]{2,1,0:T(1,128)} %bitcast.24), calls=%async_computation | async-start | bytes 32768 | tf_op jit(solution)/shard_map/all_to_all | solution.py:508
  11.5 2.5 %fusion = (bf16[32,1,192]{1,2,0:T(8,128)(2,1)S(1)}, bf16[32,1,192]{1,2,0:T(8,128)(2,1)S(1)}) fusion(bf16[32,128,192]{1,2,0:T(8,128)(2,1)} %param.16), kind=kLoop, calls=%fused_computation.14 | loop fusion | bytes 49152 | tf_op jit(solution)/shard_map/slice | solution.py:496
  14.0 0.9 copy.51
  14.9 3.4 %collective-permute-start.1 = (bf16[32,192]{1,0:T(8,128)(2,1)S(1)}, bf16[32,192]{1,0:T(8,128)(2,1)S(1)}, u32[]{:S(2)}, u32[]{:S(2)}) collective-permute-start(bf16[32,192]{1,0:T(8,128)(2,1)S(1)} %bitcast.25), channel_id=1, source_target_pairs={{0,7},{1,0},{2,1},{3,2},{4,3},{5,4},{6,5},{7,6},{8,15},{9,8},{10,9... | collective-permute-start | bytes 36872 | tf_op jit(solution)/shard_map/ppermute | solution.py:491
  18.3 0.9 copy.50
  19.1 0.1 collective-permute-start
  19.2 3.2 %copy.34.x_ref = bf16[32,128,192]{2,1,0:T(8,128)(2,1)S(1)} copy(bf16[32,128,192]{1,2,0:T(8,128)(2,1)} %param.16) | data formatting | bytes 3145728 | tf_op args[0]
  22.4 0.0 copy-start
  22.4 1.3 copy-done
  23.7 8.7 %conv_core.1.y_ref = f32[32,128,192]{2,1,0:T(8,128)} custom-call(bf16[32,128,192]{2,1,0:T(8,128)(2,1)} %copy-done, bf16[9,192,192]{2,1,0:T(8,128)(2,1)} %w_ref.8), custom_call_target="tpu_custom_call" | custom-call | tf_op jit(solution)/shard_map/conv_core/pallas_call | solution.py:145
  32.4 0.0 collective-permute-done.1
  32.4 0.0 collective-permute-done
  32.4 3.4 %collective-permute-start.2 = (bf16[130,192]{1,0:T(8,128)(2,1)S(1)}, bf16[130,192]{1,0:T(8,128)(2,1)S(1)}, u32[]{:S(2)}, u32[]{:S(2)}) collective-permute-start(bf16[130,192]{1,0:T(8,128)(2,1)S(1)} %pad_maximum_fusion), channel_id=1, source_target_pairs={{0,8},{8,16},{16,24},{1,9},{9,17},{17,25},{2,10},{10,18},{18,26},{... | collective-permute-start | bytes 149768 | tf_op jit(solution)/shard_map/ppermute | solution.py:491
  35.9 1.3 collective-permute-start.3
  37.2 0.6 collective-permute-done.2
  37.8 4.3 %collective-permute-done.3 = bf16[130,192]{1,0:T(8,128)(2,1)S(1)} collective-permute-done((bf16[130,192]{1,0:T(8,128)(2,1)S(1)}, bf16[130,192]{1,0:T(8,128)(2,1)S(1)}, u32[]{:S(2)}, u32[]{:S(2)}) %collective-permute-start.3) | collective-permute-done | bytes 49952 | tf_op jit(solution)/shard_map/ppermute | solution.py:491
  42.1 0.6 pad_maximum_fusion.4
  42.7 0.6 slice.115.top_ref
  43.3 0.6 slice.119.bot_ref
  44.0 0.0 all-to-all-done
  44.0 0.0 copy-start.3
  44.0 0.6 copy-done.3
  44.6 0.0 copy-start.4
  44.6 0.0 copy-start.5
  44.6 0.0 copy-start.2
  44.6 9.5 %sample.1 = (bf16[32,16,192]{2,1,0:T(8,128)(2,1)}, bf16[32,128,192]{2,1,0:T(8,128)(2,1)}) custom-call(f32[32,128,192]{2,1,0:T(8,128)} %conv_core.1.y_ref, bf16[32,128,192]{2,1,0:T(8,128)(2,1)} %copy-done, bf16[9,192,192]{2,1,0:T(8,128)(2,1)} %w_ref.8, s32[32,16]{1,0:T(8,128)} %bitcast.22, bf16[128,192]{1,0:T(8,128)(2,1)} %slice.115.top_ref, ...), custom_call_target="tpu_custom_call" | custom-call | tf_op jit(solution)/shard_map/sample/pallas_call | solution.py:251
  54.1 4.3 %all-to-all-start.1 = ((bf16[32,16,192]{2,1,0:T(8,128)(2,1)}), bf16[32,16,192]{2,1,0:T(8,128)(2,1)S(1)}, u32[]{:S(2)}, u32[]{:S(2)}) async-start(bf16[32,16,192]{2,1,0:T(8,128)(2,1)} %get-tuple-element.12), calls=%async_computation.1 | async-start | bytes 524288 | tf_op jit(solution)/shard_map/all_to_all | solution.py:508
  59.0 0.0 copy-done.4
  59.0 0.8 copy.43.near_ref
  59.8 0.0 copy-done.5
  59.8 0.7 copy.44.bias_ref
  60.5 0.0 copy-done.2
  60.5 0.8 copy.45.w_ref.w_in
  61.4 2.8 %prepare.1 = (bf16[256,512]{1,0:T(8,128)(2,1)}, bf16[512,256]{1,0:T(8,128)(2,1)}, f32[256,256]{1,0:T(8,128)}, f32[256,192]{1,0:T(8,128)}) custom-call(s32[1]{0:T(128)S(6)} %copy.53.live_ref, s32[256,1]{1,0:T(8,128)} %copy.35.route_ref, s32[256,16]{1,0:T(8,128)} %copy.43.near_ref, s32[1,256]{1,0:T(1,128)} %bitcast.30, f32[256,16]{1,0:T(8,128)} %copy.44.bias_ref, ...), custom_call_target="tpu_custom_call" | custom-call | tf_op jit(solution)/shard_map/prepare/pallas_call | solution.py:404
  64.2 4.2 %all-to-all-done.1.ans_ref = bf16[32,16,192]{2,1,0:T(8,128)(2,1)S(1)} async-done(((bf16[32,16,192]{2,1,0:T(8,128)(2,1)}), bf16[32,16,192]{2,1,0:T(8,128)(2,1)S(1)}, u32[]{:S(2)}, u32[]{:S(2)}) %all-to-all-start.1) | async-done | bytes 196640 | tf_op jit(solution)/shard_map/all_to_all | solution.py:508
  68.4 0.0 copy-start.1
  68.4 0.7 copy-done.1
  69.1 6.6 %stations.1 = (f32[256,128]{1,0:T(8,128)}, bf16[32,16,192]{2,1,0:T(8,128)(2,1)}) custom-call(s32[1]{0:T(128)S(6)} %copy.53.live_ref, bf16[32,16,192]{2,1,0:T(8,128)(2,1)} %copy-done.1, bf16[256,512]{1,0:T(8,128)(2,1)} %get-tuple-element.13.to_ref, bf16[512,256]{1,0:T(8,128)(2,1)} %get-tuple-element.14.from_ref, f32[256,256]{1,0:T(8,128)} %get-tuple-element.15.bias_ref, ...), custom_call_target="tpu_custom_call" | custom-call | tf_op jit(solution)/shard_map/stations/pallas_call | solution.py:472
  75.7 13.3 %all_to_all.21.inc_ref = bf16[32,16,192]{2,1,0:T(8,128)(2,1)} all-to-all(bf16[32,16,192]{2,1,0:T(8,128)(2,1)} %get-tuple-element.18), channel_id=1, replica_groups=mesh['lat'=4,'lon'=8] {'lat','lon'}, dimensions={0} | all-to-all | bytes 393216 | tf_op jit(solution)/shard_map/all_to_all | solution.py:508
  89.0 11.0 %spread.1 = (f32[32,128,192]{2,1,0:T(8,128)}, bf16[32,128,192]{2,1,0:T(8,128)(2,1)}) custom-call(s32[32,16]{1,0:T(8,128)} %bitcast.23, bf16[32,16,192]{2,1,0:T(8,128)(2,1)} %all_to_all.21.inc_ref, bf16[32,128,192]{2,1,0:T(8,128)(2,1)} %get-tuple-element.19.gate_ref), custom_call_target="tpu_custom_call" | custom-call | tf_op jit(solution)/shard_map/spread/pallas_call | solution.py:286
  99.9 2.8 %copy.47 = bf16[32,128,192]{2,0,1:T(8,128)(2,1)S(1)} copy(bf16[32,128,192]{2,1,0:T(8,128)(2,1)} %get-tuple-element.20.x_ref) | data formatting | bytes 3145728 | tf_op jit(solution)/shard_map/spread/pallas_call | solution.py:286
  102.7 0.8 collective-permute-start.4
  103.5 0.9 slice_bitcast_fusion.2
  104.4 9.3 %conv_back.1.g_ref = f32[32,128,192]{2,1,0:T(8,128)} custom-call(bf16[32,128,192]{2,1,0:T(8,128)(2,1)} %get-tuple-element.20.x_ref, bf16[9,192,192]{2,1,0:T(8,128)(2,1)} %w_ref.8, f32[32,128,192]{2,1,0:T(8,128)} %get-tuple-element.21.refs_0_), custom_call_target="tpu_custom_call" | custom-call | tf_op jit(solution)/shard_map/conv_back/pallas_call | solution.py:145
  113.7 2.8 %collective-permute-start.5 = (bf16[32,192]{1,0:T(8,128)(2,1)S(1)}, bf16[32,192]{1,0:T(8,128)(2,1)S(1)}, u32[]{:S(2)}, u32[]{:S(2)}) collective-permute-start(bf16[32,192]{1,0:T(8,128)(2,1)S(1)} %get-tuple-element.29), channel_id=1, source_target_pairs={{0,7},{1,0},{2,1},{3,2},{4,3},{5,4},{6,5},{7,6},{8,15},{9,8},{10,9... | collective-permute-start | bytes 36872 | tf_op jit(solution)/shard_map/ppermute | solution.py:491
  116.5 0.0 collective-permute-done.4
  116.5 1.4 %collective-permute-done.5 = bf16[32,192]{1,0:T(8,128)(2,1)S(1)} collective-permute-done((bf16[32,192]{1,0:T(8,128)(2,1)S(1)}, bf16[32,192]{1,0:T(8,128)(2,1)S(1)}, u32[]{:S(2)}, u32[]{:S(2)}) %collective-permute-start.5) | collective-permute-done | bytes 12320 | tf_op jit(solution)/shard_map/ppermute | solution.py:491
  118.0 2.8 %collective-permute-start.6 = (bf16[130,192]{1,0:T(8,128)(2,1)S(1)}, bf16[130,192]{1,0:T(8,128)(2,1)S(1)}, u32[]{:S(2)}, u32[]{:S(2)}) collective-permute-start(bf16[130,192]{1,0:T(8,128)(2,1)S(1)} %pad_maximum_fusion.2), channel_id=1, source_target_pairs={{0,8},{8,16},{16,24},{1,9},{9,17},{17,25},{2,10},{10,18},{18,26},{... | collective-permute-start | bytes 149768 | tf_op jit(solution)/shard_map/ppermute | solution.py:491
  120.8 1.3 collective-permute-start.7
  122.1 0.6 collective-permute-done.6
  122.7 0.6 slice.128.top_ref
  123.3 3.7 %collective-permute-done.7 = bf16[130,192]{1,0:T(8,128)(2,1)S(1)} collective-permute-done((bf16[130,192]{1,0:T(8,128)(2,1)S(1)}, bf16[130,192]{1,0:T(8,128)(2,1)S(1)}, u32[]{:S(2)}, u32[]{:S(2)}) %collective-permute-start.7) | collective-permute-done | bytes 49952 | tf_op jit(solution)/shard_map/ppermute | solution.py:491
  127.0 0.6 slice.131.bot_ref
  127.6 0.6 pad_maximum_fusion.7.right_ref
  128.2 0.6 pad_maximum_fusion.6.left_ref
  128.8 3.4 %edges.1 = f32[32,128,192]{2,1,0:T(8,128)} custom-call(f32[32,128,192]{2,1,0:T(8,128)} %conv_back.1.g_ref, bf16[9,192,192]{2,1,0:T(8,128)(2,1)} %w_ref.8, bf16[128,192]{1,0:T(8,128)(2,1)} %slice.128.top_ref, bf16[128,192]{1,0:T(8,128)(2,1)} %slice.131.bot_ref, bf16[34,192]{1,0:T(8,128)(2,1)} %pad_maximum_fusion.6.left_ref, ...), custom_call_target="tpu_custom_call", output_to_operand_aliasing={{}: (0, {})} | custom-call | tf_op jit(solution)/shard_map/edges/pallas_call | solution.py:335
  132.3 5.3 %copy.49 = f32[32,128,192]{1,2,0:T(8,128)} copy(f32[32,128,192]{2,1,0:T(8,128)} %edges.1) | data formatting | bytes 6291456
  (14 shorter events, 0.1 us)
Async XLA Ops:
  4.1 39.8 %all-to-all-start = ((s32[32,1,16]{2,1,0:T(1,128)}), s32[32,1,16]{2,1,0:T(1,128)S(1)}, u32[]{:S(2)}, u32[]{:S(2)}) async-start(s32[32,1,16]{2,1,0:T(1,128)} %bitcast.24), calls=%async_computation | async-start | bytes 32768 | tf_op jit(solution)/shard_map/all_to_all | solution.py:508
  14.9 17.5 %collective-permute-start.1 = (bf16[32,192]{1,0:T(8,128)(2,1)S(1)}, bf16[32,192]{1,0:T(8,128)(2,1)S(1)}, u32[]{:S(2)}, u32[]{:S(2)}) collective-permute-start(bf16[32,192]{1,0:T(8,128)(2,1)S(1)} %bitcast.25), channel_id=1, source_target_pairs={{0,7},{1,0},{2,1},{3,2},{4,3},{5,4},{6,5},{7,6},{8,15},{9,8},{10,9... | collective-permute-start | bytes 36872 | tf_op jit(solution)/shard_map/ppermute | solution.py:491
  19.1 13.3 %collective-permute-start = (bf16[32,192]{1,0:T(8,128)(2,1)S(1)}, bf16[32,192]{1,0:T(8,128)(2,1)S(1)}, u32[]{:S(2)}, u32[]{:S(2)}) collective-permute-start(bf16[32,192]{1,0:T(8,128)(2,1)S(1)} %bitcast.26), channel_id=1, source_target_pairs={{0,1},{1,2},{2,3},{3,4},{4,5},{5,6},{6,7},{7,0},{8,9},{9,10},{10,1... | collective-permute-start | bytes 36872 | tf_op jit(solution)/shard_map/ppermute | solution.py:491
  22.4 1.3 copy-start
  32.4 5.3 %collective-permute-start.2 = (bf16[130,192]{1,0:T(8,128)(2,1)S(1)}, bf16[130,192]{1,0:T(8,128)(2,1)S(1)}, u32[]{:S(2)}, u32[]{:S(2)}) collective-permute-start(bf16[130,192]{1,0:T(8,128)(2,1)S(1)} %pad_maximum_fusion), channel_id=1, source_target_pairs={{0,8},{8,16},{16,24},{1,9},{9,17},{17,25},{2,10},{10,18},{18,26},{... | collective-permute-start | bytes 149768 | tf_op jit(solution)/shard_map/ppermute | solution.py:491
  35.9 6.2 %collective-permute-start.3 = (bf16[130,192]{1,0:T(8,128)(2,1)S(1)}, bf16[130,192]{1,0:T(8,128)(2,1)S(1)}, u32[]{:S(2)}, u32[]{:S(2)}) collective-permute-start(bf16[130,192]{1,0:T(8,128)(2,1)S(1)} %pad_maximum_fusion.1), channel_id=1, source_target_pairs={{8,0},{16,8},{24,16},{9,1},{17,9},{25,17},{10,2},{18,10},{26,18},{... | collective-permute-start | bytes 149768 | tf_op jit(solution)/shard_map/ppermute | solution.py:491
  44.0 0.6 copy-start.3
  44.6 14.5 %copy-start.4 = (s32[256,16]{0,1:T(8,128)S(1)}, s32[256,16]{0,1:T(8,128)}, u32[]{:S(2)}) copy-start(s32[256,16]{0,1:T(8,128)} %param.22) | copy-start | bytes 49156
  44.6 15.2 %copy-start.5 = (f32[256,16]{0,1:T(8,128)S(1)}, f32[256,16]{0,1:T(8,128)}, u32[]{:S(2)}) copy-start(f32[256,16]{0,1:T(8,128)} %param.24) | copy-start | bytes 49156
  44.6 16.0 %copy-start.2 = (bf16[448,192]{0,1:T(8,128)(2,1)S(1)}, bf16[448,192]{0,1:T(8,128)(2,1)}, u32[]{:S(2)}) copy-start(bf16[448,192]{0,1:T(8,128)(2,1)} %param.26) | copy-start | bytes 516100
  54.1 14.3 %all-to-all-start.1 = ((bf16[32,16,192]{2,1,0:T(8,128)(2,1)}), bf16[32,16,192]{2,1,0:T(8,128)(2,1)S(1)}, u32[]{:S(2)}, u32[]{:S(2)}) async-start(bf16[32,16,192]{2,1,0:T(8,128)(2,1)} %get-tuple-element.12), calls=%async_computation.1 | async-start | bytes 524288 | tf_op jit(solution)/shard_map/all_to_all | solution.py:508
  68.4 0.7 copy-start.1
  102.7 13.8 %collective-permute-start.4 = (bf16[32,192]{1,0:T(8,128)(2,1)S(1)}, bf16[32,192]{1,0:T(8,128)(2,1)S(1)}, u32[]{:S(2)}, u32[]{:S(2)}) collective-permute-start(bf16[32,192]{1,0:T(8,128)(2,1)S(1)} %get-tuple-element.28), channel_id=1, source_target_pairs={{0,1},{1,2},{2,3},{3,4},{4,5},{5,6},{6,7},{7,0},{8,9},{9,10},{10,1... | collective-permute-start | bytes 36872 | tf_op jit(solution)/shard_map/ppermute | solution.py:491
  113.7 4.2 %collective-permute-start.5 = (bf16[32,192]{1,0:T(8,128)(2,1)S(1)}, bf16[32,192]{1,0:T(8,128)(2,1)S(1)}, u32[]{:S(2)}, u32[]{:S(2)}) collective-permute-start(bf16[32,192]{1,0:T(8,128)(2,1)S(1)} %get-tuple-element.29), channel_id=1, source_target_pairs={{0,7},{1,0},{2,1},{3,2},{4,3},{5,4},{6,5},{7,6},{8,15},{9,8},{10,9... | collective-permute-start | bytes 36872 | tf_op jit(solution)/shard_map/ppermute | solution.py:491
  118.0 4.7 %collective-permute-start.6 = (bf16[130,192]{1,0:T(8,128)(2,1)S(1)}, bf16[130,192]{1,0:T(8,128)(2,1)S(1)}, u32[]{:S(2)}, u32[]{:S(2)}) collective-permute-start(bf16[130,192]{1,0:T(8,128)(2,1)S(1)} %pad_maximum_fusion.2), channel_id=1, source_target_pairs={{0,8},{8,16},{16,24},{1,9},{9,17},{17,25},{2,10},{10,18},{18,26},{... | collective-permute-start | bytes 149768 | tf_op jit(solution)/shard_map/ppermute | solution.py:491
  120.8 6.2 %collective-permute-start.7 = (bf16[130,192]{1,0:T(8,128)(2,1)S(1)}, bf16[130,192]{1,0:T(8,128)(2,1)S(1)}, u32[]{:S(2)}, u32[]{:S(2)}) collective-permute-start(bf16[130,192]{1,0:T(8,128)(2,1)S(1)} %pad_maximum_fusion.3), channel_id=1, source_target_pairs={{8,0},{16,8},{24,16},{9,1},{17,9},{25,17},{10,2},{18,10},{26,18},{... | collective-permute-start | bytes 149768 | tf_op jit(solution)/shard_map/ppermute | solution.py:491
where the time goes:
time: 138 us
  Pallas kernels  53.4 us (39%)
  starting transfers between devices  27.4 us (20%)
  local copies, waits for them, and re-layouts  25.3 us (18%)
  waiting for transfers between devices  14.8 us (11%)
  blocking collectives  13.3 us (10%)
  other arithmetic  1.96 us (1%)
  between operations  1.46 us (1%)
    pallas_call x2, Pallas kernels, conv_core(): pl.pallas_call(functools.partial(conv_kernel, back, block), grid=(rows //...  18 us
    unnamed x20, local copies, waits for them, and re-layouts  16.6 us
    ppermute x8, starting transfers between devices, shift(): return lax.ppermute(x, axis, pairs)  15.8 us
    all_to_all x1, blocking collectives, exchange(): return lax.all_to_all(x, AXES, split_axis=0, concat_axis=0, tiled=True)  13.3 us
    all_to_all x2, starting transfers between devices, exchange(): return lax.all_to_all(x, AXES, split_axis=0, concat_axis=0, tiled=True)  11.6 us
    pallas_call x1, Pallas kernels, spread(): pl.pallas_call(spread_kernel, out_shape=(jax.ShapeDtypeStruct(gate.shape,...  11 us
    ppermute x8, waiting for transfers between devices, shift(): return lax.ppermute(x, axis, pairs)  10.6 us
    pallas_call x1, Pallas kernels, sample(): pl.pallas_call(sample_kernel, out_shape=(jax.ShapeDtypeStruct(asked.shape...  9.52 us
  transfers between devices with their start and end apart: 10, of which 6 were waited for; matrix products, arithmetic and copies ran while one was open for 10% of the time, Pallas kernels for 15%

commit v1 on v0

v1 whole, which is shorter than its diff:
```python
import functools
import math

import jax
import jax.numpy as jnp
from jax import lax
from jax.experimental import pallas as pl
from jax.experimental.pallas import tpu as pltpu
from jax.sharding import PartitionSpec as P

HEADS = 3
EPS = 1e-06
NEG = -1e30
AXES = ("lat", "lon")
F32 = jnp.float32
BF16 = jnp.bfloat16
VMEM = pltpu.VMEM
DIAGONALS = ((-1, -1), (-1, 1), (1, -1), (1, 1))
PARAMS = pltpu.CompilerParams(vmem_limit_bytes=32 << 20)


def nn(a, b):
    return lax.dot_general(a, b, (((1,), (0,)), ((), ())), preferred_element_type=F32)


def nt(a, b):
    return lax.dot_general(a, b, (((1,), (1,)), ((), ())), preferred_element_type=F32)


def tn(a, b):
    return lax.dot_general(a, b, (((0,), (0,)), ((), ())), preferred_element_type=F32)


def iota(shape, dim):
    return lax.broadcasted_iota(jnp.int32, shape, dim)


def iota_f(shape, dim):
    return iota(shape, dim).astype(F32)


def onehot(test):
    return jnp.where(test, 1.0, 0.0).astype(BF16)


def up(n, m):
    return -(-n // m) * m


def whole(count):
    return [pl.BlockSpec(memory_space=VMEM)] * count


SCALARS = [pl.BlockSpec(memory_space=pltpu.SMEM)]
SDS = jax.ShapeDtypeStruct


def slab_rows(cap):
    return up(cap + cap // 2 + 6, 16)


def corner_rows(tile, base):
    return [
        jnp.concatenate(
            [tile[base + q : base + q + 1], tile[base + 4 + q // 2 : base + 5 + q // 2, (q % 2) * 64 : (q % 2) * 64 + 64]],
            axis=1,
        )
        for q in range(4)
    ]


def corner_tile(rows):
    halves = [jnp.concatenate([rows[2 * k][:, 128:], rows[2 * k + 1][:, 128:]], axis=1) for k in range(2)]
    return [r[:, :128] for r in rows] + halves


def near_corners(diag_ref, slab_ref, base):
    rows = []
    for q in range(4):
        at = diag_ref[q]
        tile = slab_ref[jnp.maximum(at, 0)].astype(F32)
        rows.append(corner_rows(tile, base)[q] * jnp.where(at >= 0, 1.0, 0.0))
    return rows


def route_parts(route_row, wide):
    stations = route_row.shape[1]
    member = onehot(route_row == iota((wide, stations), 0))
    same = tn(member, member)
    row, col = iota((stations, stations), 0), iota((stations, stations), 1)
    rank_col = jnp.sum(jnp.where(col < row, same, 0.0), axis=1, keepdims=True)
    rank_row = jnp.sum(jnp.where(row < col, same, 0.0), axis=0, keepdims=True)
    route_col = tn(member, iota((wide, 128), 0).astype(F32).astype(BF16))[:, 0:1]
    return rank_col, rank_row, route_col


def intro_kernel(route_ref, spot_ref, x_ref, slab_ref, xs_ref, top_ref, bot_ref, left_ref, right_ref):
    rows, ch, cols = x_ref.shape
    regions = slab_ref.shape[0]
    stations = route_ref.shape[1]
    deep = xs_ref.shape[2]
    eye = onehot(iota((cols, cols), 0) == iota((cols, cols), 1))
    pad = jnp.zeros((cols, deep - ch), BF16)
    blank = jnp.zeros((cols, deep), BF16)
    xs_ref[0] = blank
    xs_ref[rows + 1] = blank
    lefts, rights = [], []
    for r in range(rows):
        turned = nt(eye, x_ref[r])
        lefts.append(turned[0:1])
        rights.append(turned[cols - 1 : cols])
        turned = turned.astype(BF16)
        xs_ref[r + 1] = jnp.concatenate([turned, pad], axis=1)
        if r == 0:
            bot_ref[...] = turned
        if r == rows - 1:
            top_ref[...] = turned
    left_ref[...] = jnp.concatenate(rights, axis=0).astype(BF16)
    right_ref[...] = jnp.concatenate(lefts, axis=0).astype(BF16)

    rank_col, _, _ = route_parts(route_ref[...], up(regions, 128))
    spot = spot_ref[...].astype(F32)
    high = jnp.floor(spot * (1.0 / 256.0))
    low = spot - 256.0 * high
    member = route_ref[...] == iota((regions, stations), 0)
    ranked = onehot(rank_col == iota_f((stations, 128), 1))
    req = 256.0 * nn(jnp.where(member, high, 0.0).astype(BF16), ranked) + nn(
        jnp.where(member, low, 0.0).astype(BF16), ranked
    )
    slab_ref[:, 0, :] = req
    slab_ref[:, 1, :] = req
    mine = corner_tile([rights[-1], lefts[-1], rights[0], lefts[0]])
    for k in range(6):
        slab_ref[:, 2 + k, :] = jnp.broadcast_to(mine[k], (regions, 128))


def intro(route, spot, x_t, regions):
    rows, ch, cols = x_t.shape
    return pl.pallas_call(
        intro_kernel,
        out_shape=(
            SDS((regions, 8, 128), F32),
            SDS((rows + 2, cols, up(ch, 128)), BF16),
            SDS((cols, ch), BF16),
            SDS((cols, ch), BF16),
            SDS((rows, ch), BF16),
            SDS((rows, ch), BF16),
        ),
        in_specs=whole(3),
        out_specs=tuple(whole(6)),
        compiler_params=PARAMS,
        name="intro",
    )(route, spot, x_t)


def conv_weights(w_ref, wc, back):
    ch = w_ref.shape[1]
    deep = up(ch, 128)
    wc[...] = jnp.zeros_like(wc)
    for dy in range(3):
        for dx in range(3):
            if back:
                wc[dx, :, dy * deep : dy * deep + ch] = w_ref[8 - (3 * dy + dx)]
            else:
                wc[dx, dy * deep : dy * deep + ch, :] = w_ref[3 * dy + dx]


def conv_kernel(back, block, xs_ref, w_ref, *refs):
    o_ref, wc = refs[-2:]
    rows, cols, ch = o_ref.shape
    deep = xs_ref.shape[2]
    conv_weights(w_ref, wc, back)
    dot = nt if back else nn
    col = iota((block * cols, ch), 0) % cols
    first, last = col == 0, col == cols - 1

    def body(i, carry):
        r0 = i * block
        lhs = jnp.concatenate(
            [xs_ref[pl.ds(r0 + dy, block)].reshape(block * cols, deep) for dy in range(3)], axis=1
        )
        total = dot(lhs, wc[1])
        total = total + jnp.where(first, 0.0, pltpu.roll(dot(lhs, wc[0]), 1, 0))
        total = total + jnp.where(last, 0.0, pltpu.roll(dot(lhs, wc[2]), block * cols - 1, 0))
        total = total.reshape(block, cols, ch)
        if back:
            total = total + refs[0][pl.ds(r0, block)]
        o_ref[pl.ds(r0, block)] = total
        return carry

    lax.fori_loop(0, rows // block, body, 0)


def conv_core(xs, taps, add=None, block=8):
    rows, cols, deep = xs.shape
    rows, ch = rows - 2, taps.shape[1]
    back = add is not None
    wc = (3, ch, 3 * deep) if back else (3, 3 * deep, ch)
    args = (xs, taps, add) if back else (xs, taps)
    return pl.pallas_call(
        functools.partial(conv_kernel, back, block),
        out_shape=SDS((rows, cols, ch), F32),
        in_specs=whole(len(args)),
        out_specs=whole(1)[0],
        scratch_shapes=[VMEM(wc, BF16)],
        compiler_params=PARAMS,
        name="conv_back" if back else "conv_core",
    )(*args)


def border_rows(line, w_ref, dy, back):
    cols, ch = line.shape
    dot = nt if back else nn
    tap = lambda dx: w_ref[8 - (3 * dy + dx)] if back else w_ref[3 * dy + dx]
    col = iota((cols, ch), 0)
    total = dot(line, tap(1))
    total = total + jnp.where(col == 0, 0.0, pltpu.roll(dot(line, tap(0)), 1, 0))
    return total + jnp.where(col == cols - 1, 0.0, pltpu.roll(dot(line, tap(2)), cols - 1, 0))


def border_cols(side, corners, w_ref, dx, back):
    rows, ch = side.shape
    dot = nt if back else nn
    ends = jnp.concatenate(list(corners) + [jnp.zeros((6, ch), F32)], axis=0)
    both = jnp.concatenate([side.astype(F32), ends], axis=0).astype(BF16)
    row = iota((rows, ch), 0)
    total = None
    for dy in range(3):
        tap = w_ref[8 - (3 * dy + dx)] if back else w_ref[3 * dy + dx]
        term = dot(both, tap)
        if dy == 0:
            part = jnp.where(row == 0, term[rows : rows + 1], pltpu.roll(term[:rows], 1, 0))
        elif dy == 1:
            part = term[:rows]
        else:
            part = jnp.where(row == rows - 1, term[rows + 1 : rows + 2], pltpu.roll(term[:rows], rows - 1, 0))
        total = part if total is None else total + part
    return total


def add_sides(line, fix, r):
    cols, ch = line.shape
    near = iota((8, ch), 0)
    head = line[:8] + jnp.where(near == 0, fix[0, pl.ds(r, 1)], 0.0)
    tail = line[cols - 8 :] + jnp.where(near == 7, fix[1, pl.ds(r, 1)], 0.0)
    return jnp.concatenate([head, line[8 : cols - 8], tail], axis=0)


def fine_cell(spot, cols):
    fine = float(4 * (cols - 1))
    fr = jnp.floor((spot + 0.5) * (1.0 / fine))
    fc = spot - fine * fr
    r, c = jnp.floor(fr * 0.25), jnp.floor(fc * 0.25)
    return r, c, (fr - 4.0 * r + 0.5) * 0.25, (fc - 4.0 * c + 0.5) * 0.25


def hat(cell, at, frac):
    return jnp.where(cell == at, 1.0 - frac, jnp.where(cell == at + 1.0, frac, 0.0))


def split_spots(asked):
    high = jnp.floor(asked * (1.0 / 256.0))
    return high.astype(BF16), (asked - 256.0 * high).astype(BF16)


def spots_column(asked, slots):
    regions, wide = asked.shape
    capacity = slots // regions
    high, low = split_spots(asked)
    k, t = iota((slots, regions), 0), iota((slots, regions), 1)
    pick = onehot((k >= t * capacity) & (k < (t + 1) * capacity))
    both = 256.0 * nn(pick, high) + nn(pick, low)
    k, c = iota((slots, wide), 0), iota((slots, wide), 1)
    return jnp.sum(jnp.where(k % capacity == c, both, 0.0), axis=1, keepdims=True)


def spots_row(asked, slots):
    regions, wide = asked.shape
    capacity = slots // regions
    high, low = split_spots(asked)
    t, k = iota((regions, slots), 0), iota((regions, slots), 1)
    pick = onehot((k >= t * capacity) & (k < (t + 1) * capacity))
    both = 256.0 * tn(high, pick) + tn(low, pick)
    c, k = iota((wide, slots), 0), iota((wide, slots), 1)
    return jnp.sum(jnp.where(k % capacity == c, both, 0.0), axis=0, keepdims=True)


def sample_kernel(
    cap, diag_ref, y_ref, xs_ref, w_ref, asked_ref, top_ref, bot_ref, left_ref, right_ref, ans_ref, gate_ref,
    field, fix, edge, pack,
):
    rows, cols, ch = gate_ref.shape
    regions = ans_ref.shape[0]
    slots = regions * cap
    half = cap // 2
    tl, tr, bl, br = near_corners(diag_ref, asked_ref, 2)
    edge[0] = border_rows(top_ref[...], w_ref, 0, False)
    edge[1] = border_rows(bot_ref[...], w_ref, 2, False)
    fix[0] = border_cols(left_ref[...], (tl, bl), w_ref, 0, False)
    fix[1] = border_cols(right_ref[...], (tr, br), w_ref, 2, False)

    def gates(r, pre):
        pre = add_sides(pre, fix, r)
        sg = 1.0 / (1.0 + jnp.exp(-pre))
        field[pl.ds(r * cols, cols), :] = (xs_ref[r + 1, :, :ch].astype(F32) + pre * sg).astype(BF16)
        gate_ref[r] = (sg * (1.0 + pre * (1.0 - sg))).astype(BF16)

    def inner(r, carry):
        gates(r, y_ref[r])
        return carry

    gates(0, y_ref[0] + edge[0])
    lax.fori_loop(1, rows - 1, inner, 0)
    gates(rows - 1, y_ref[rows - 1] + edge[1])

    spot = spots_column(asked_ref[:, 0, :], slots)
    r, c, a, b = fine_cell(spot, cols)
    by_row = hat(iota_f((slots, rows), 1), r, a)
    by_col = hat(iota_f((slots, cols), 1), c, b)
    total = jnp.zeros((slots, ch), F32)
    for pair in range(0, rows, 2):
        weights = jnp.concatenate(
            [(by_row[:, pair + k : pair + k + 1] * by_col).astype(BF16) for k in range(2)], axis=1
        )
        total = total + nn(weights, field[pair * cols : (pair + 2) * cols, :])
    pack[...] = jnp.zeros_like(pack)
    for t in range(regions):
        at = t * cap
        pack[t, 0:cap, :] = total[at : at + cap, :128]
        pack[t, cap : cap + half, 0 : ch - 128] = total[at : at + half, 128:]
        pack[t, cap : cap + half, 64 : 64 + ch - 128] = total[at + half : at + cap, 128:]
    first, final = gate_ref[0].astype(F32), gate_ref[rows - 1].astype(F32)
    mine = corner_tile([final[cols - 1 :], final[0:1], first[cols - 1 :], first[0:1]])
    for k in range(6):
        pack[:, cap + half + k, :] = jnp.broadcast_to(mine[k], (regions, 128))
    ans_ref[...] = pack[...].astype(BF16)


def sample(diag, y, xs, taps, asked, top, bot, left, right, cap):
    rows, cols, ch = y.shape
    regions = asked.shape[0]
    deep = slab_rows(cap)
    return pl.pallas_call(
        functools.partial(sample_kernel, cap),
        out_shape=(SDS((regions, deep, 128), BF16), SDS((rows, cols, ch), BF16)),
        in_specs=SCALARS + whole(8),
        out_specs=tuple(whole(2)),
        scratch_shapes=[
            VMEM((rows * cols, ch), BF16),
            VMEM((2, rows, ch), F32),
            VMEM((2, cols, ch), F32),
            VMEM((regions, deep, 128), F32),
        ],
        compiler_params=PARAMS,
        name="sample",
    )(diag, y, xs, taps, asked, top, bot, left, right)


def spread_kernel(
    cap, block, diag_ref, asked_ref, inc_ref, ans_ref, gate_ref, df_ref, dp_ref, top_ref, bot_ref, left_ref,
    right_ref, corner_ref, by_row, inc, edges,
):
    rows, cols, ch = gate_ref.shape
    regions = inc_ref.shape[0]
    slots = regions * cap
    half = cap // 2
    deep = dp_ref.shape[2]
    spot = spots_row(asked_ref[:, 0, :], slots)
    r, c, a, b = fine_cell(spot, cols)
    by_row[...] = hat(iota_f((rows, slots), 0), r, a)
    by_col = hat(iota_f((cols, slots), 0), c, b)
    sums = jnp.zeros((inc_ref.shape[1], 128), F32)
    for t in range(regions):
        at = t * cap
        slab = inc_ref[t].astype(F32)
        sums = sums + slab
        inc[at : at + cap, 0:128] = slab[0:cap]
        inc[at : at + half, 128:ch] = slab[cap : cap + half, 0 : ch - 128]
        inc[at + half : at + cap, 128:ch] = slab[cap : cap + half, 64 : 64 + ch - 128]
    incoming = inc[...].astype(BF16)
    pad = jnp.zeros((block, cols, deep - ch), BF16)
    dp_ref[0] = jnp.zeros((cols, deep), BF16)
    dp_ref[rows + 1] = jnp.zeros((cols, deep), BF16)

    def body(i, carry):
        r0 = i * block
        weights = jnp.concatenate(
            [(by_row[pl.ds(r0 + k, 1)] * by_col).astype(BF16) for k in range(block)], axis=0
        )
        d_field = nn(weights, incoming).reshape(block, cols, ch)
        df_ref[pl.ds(r0, block)] = d_field
        d_pre = d_field * gate_ref[pl.ds(r0, block)].astype(F32)
        for k in range(block):
            edges[0, pl.ds(r0 + k, 1)] = d_pre[k, 0:1]
            edges[1, pl.ds(r0 + k, 1)] = d_pre[k, cols - 1 : cols]
        dp_ref[pl.ds(r0 + 1, block)] = jnp.concatenate([d_pre.astype(BF16), pad], axis=2)
        return carry

    lax.fori_loop(0, rows // block, body, 0)
    bot_ref[...] = dp_ref[1, :, :ch]
    top_ref[...] = dp_ref[rows, :, :ch]
    right_ref[...] = edges[0].astype(BF16)
    left_ref[...] = edges[1].astype(BF16)
    base = cap + half
    gates = near_corners(diag_ref, ans_ref, base)
    corners = [g * s for g, s in zip(gates, corner_rows(sums, base))]
    corner_ref[...] = jnp.concatenate(corners + [jnp.zeros((4, ch), F32)], axis=0)


def spread(diag, asked, incoming, answer, gate, cap, block=4):
    rows, cols, ch = gate.shape
    slots = incoming.shape[0] * cap
    return pl.pallas_call(
        functools.partial(spread_kernel, cap, block),
        out_shape=(
            SDS(gate.shape, F32),
            SDS((rows + 2, cols, up(ch, 128)), BF16),
            SDS((cols, ch), BF16),
            SDS((cols, ch), BF16),
            SDS((rows, ch), BF16),
            SDS((rows, ch), BF16),
            SDS((8, ch), F32),
        ),
        in_specs=SCALARS + whole(4),
        out_specs=tuple(whole(7)),
        scratch_shapes=[VMEM((rows, slots), F32), VMEM((slots, ch), F32), VMEM((2, rows, ch), F32)],
        compiler_params=PARAMS,
        name="spread",
    )(diag, asked, incoming, answer, gate)


def finish_kernel(g_ref, w_ref, top_ref, bot_ref, left_ref, right_ref, corner_ref, o_ref, fix, edge):
    block, cols, ch = g_ref.shape
    step = pl.program_id(0)
    steps = pl.num_programs(0)

    @pl.when(step == 0)
    def _():
        corners = corner_ref[...]
        edge[0] = border_rows(top_ref[...], w_ref, 0, True)
        edge[1] = border_rows(bot_ref[...], w_ref, 2, True)
        fix[0] = border_cols(left_ref[...], (corners[0:1], corners[2:3]), w_ref, 0, True)
        fix[1] = border_cols(right_ref[...], (corners[1:2], corners[3:4]), w_ref, 2, True)

    for k in range(block):
        out = add_sides(g_ref[k], fix, step * block + k)
        if k == 0:
            out = out + jnp.where(step == 0, edge[0], 0.0)
        if k == block - 1:
            out = out + jnp.where(step == steps - 1, edge[1], 0.0)
        o_ref[k] = out.T


def finish(grad, taps, top, bot, left, right, corners, block=8):
    rows, cols, ch = grad.shape
    return pl.pallas_call(
        finish_kernel,
        grid=(rows // block,),
        out_shape=SDS((rows, ch, cols), F32),
        in_specs=[pl.BlockSpec((block, cols, ch), lambda i: (i, 0, 0))] + whole(6),
        out_specs=pl.BlockSpec((block, ch, cols), lambda i: (i, 0, 0)),
        scratch_shapes=[VMEM((2, rows, ch), F32), VMEM((2, cols, ch), F32)],
        compiler_params=PARAMS,
        name="finish",
    )(grad, taps, top, bot, left, right, corners)


def prepare_kernel(
    cap, tile, n_lon, live_ref, route_ref, spot_ref, near_ref, count_ref, bias_ref, obs_ref, mask_ref, w_ref,
    to_ref, rest_ref, half_ref, from_ref, bias_out, part_ref,
):
    stations, packed = to_ref.shape
    features = obs_ref.shape[1]
    deep = slab_rows(cap)
    regions = packed // deep
    rows, cols = tile
    half, base = cap // 2, cap + cap // 2
    route = route_ref[...]
    rank_col, rank_row, route_col = route_parts(route, up(regions, 128))
    upper = jnp.where(rank_col >= half, 1.0, 0.0)
    at = iota_f((stations, packed), 1)
    to_ref[...] = onehot(at == route_col * deep + rank_col)
    rest_ref[...] = onehot(at == route_col * deep + cap + rank_col - half * upper)
    half_ref[...] = jnp.broadcast_to(upper, (stations, 128))

    row, col, a, b = fine_cell(spot_ref[...].astype(F32), cols)
    share = []
    for dy, dx in DIAGONALS:
        by_row = jnp.where(row == rows - 2.0, a, 0.0) if dy < 0 else jnp.where(row == 0.0, 1.0 - a, 0.0)
        by_col = jnp.where(col == cols - 2.0, b, 0.0) if dx < 0 else jnp.where(col == 0.0, 1.0 - b, 0.0)
        share.append(by_row * by_col)
    j = iota((deep, stations), 0)
    jf = j.astype(F32)
    spare = (j >= cap) & (j < base)
    picks = (
        jnp.where(rank_row == jf, 1.0, 0.0),
        jnp.where(spare & (rank_row == jf - cap), 1.0, 0.0),
        jnp.where(spare & (rank_row == jf - cap + half), 1.0, 0.0),
    )

    def fill(u, carry):
        lat, lon = u // n_lon, u % n_lon
        mine = route == u
        corner = []
        for q, (dy, dx) in enumerate(DIAGONALS):
            inside = (lat + dy >= 0) & (lat + dy < regions // n_lon)
            v = jnp.where(inside, (lat + dy) * n_lon + (lon + dx + n_lon) % n_lon, -1)
            corner.append(jnp.where(route == v, share[q], 0.0))
        blocks = [jnp.where(mine, p, 0.0) for p in picks]
        for q in range(4):
            blocks[0] = jnp.where(j == base + q, corner[q], blocks[0])
        for k in range(2):
            for side in range(2):
                blocks[1 + side] = jnp.where(j == base + 4 + k, corner[2 * k + side], blocks[1 + side])
        from_ref[pl.ds(u * deep, deep), :] = jnp.concatenate(blocks, axis=1).astype(BF16)
        return carry

    lax.fori_loop(0, regions, fill, 0)

    live = live_ref[0].astype(F32)
    width = near_ref.shape[0]
    near, bias = near_ref[...].astype(F32), bias_ref[...]
    valid = (iota((width, stations), 0) < count_ref[...]) & (near < live)
    near = jnp.where(valid, near, -1.0)
    bias = jnp.where(valid, bias, NEG)
    own = near == iota_f((width, stations), 1)
    top = jnp.where(own, jnp.maximum(bias, 0.0), bias)
    for d in range(1, width):
        same = pltpu.roll(near, d, 0) == near
        top = jnp.maximum(top, jnp.where(same, pltpu.roll(bias, d, 0), NEG))
    mass = jnp.exp(bias - top) + jnp.where(own, jnp.exp(jnp.minimum(-top, 0.0)), 0.0)
    for d in range(1, width):
        same = pltpu.roll(near, d, 0) == near
        other = jnp.exp(jnp.minimum(pltpu.roll(bias, d, 0) - top, 0.0))
        mass = mass + jnp.where(same, other, 0.0)
    merged = top + jnp.log(mass)
    own_top = jnp.max(jnp.where(own, jnp.maximum(bias, 0.0), 0.0), axis=0, keepdims=True)
    own_mass = jnp.exp(-own_top) + jnp.sum(
        jnp.where(own, jnp.exp(jnp.minimum(bias - own_top, 0.0)), 0.0), axis=0, keepdims=True
    )
    own_bias = own_top + jnp.log(own_mass)
    key = iota_f((stations, stations), 0)
    table = jnp.full((stations, stations), NEG, F32)
    for k in range(width):
        table = jnp.where(key == near[k : k + 1], merged[k : k + 1], table)
    bias_out[...] = jnp.where(key == iota_f((stations, stations), 1), own_bias, table)

    mask = mask_ref[...].astype(F32)
    part_ref[...] = nt((obs_ref[...] * (1.0 - mask)).astype(BF16), w_ref[:, :features]) + nt(
        mask.astype(BF16), w_ref[:, features : 2 * features]
    )


def prepare(route, spot, near, count, bias, live, obs, mask, w_in, regions, cap, tile, n_lon):
    stations = obs.shape[0]
    packed = regions * slab_rows(cap)
    return pl.pallas_call(
        functools.partial(prepare_kernel, cap, tile, n_lon),
        out_shape=(
            SDS((stations, packed), BF16),
            SDS((stations, packed), BF16),
            SDS((stations, 128), F32),
            SDS((packed, 3 * stations), BF16),
            SDS((stations, stations), F32),
            SDS((stations, w_in.shape[0]), F32),
        ),
        in_specs=SCALARS + whole(8),
        out_specs=tuple(whole(6)),
        compiler_params=PARAMS,
        name="prepare",
    )(live, route, spot, near, count.reshape(1, -1), bias, obs, mask, w_in)


def station_kernel(
    live_ref, ans_ref, to_ref, rest_ref, half_ref, from_ref, bias_ref, part_ref, obs_ref, mask_ref, w_in, g1_ref,
    w_qkv, w_out, g2_ref, w_head, pred_ref, out_ref, prob, d_qkv,
):
    stations, packed = to_ref.shape
    ch = part_ref.shape[1]
    dim = ch // HEADS
    scale = 1.0 / math.sqrt(dim)
    below = w_in.shape[1] - ch
    inv = 1.0 / ch
    g1, g2 = g1_ref[...], g2_ref[...]

    flat = ans_ref[...].reshape(packed, 128)
    main = nn(to_ref[...], flat).astype(BF16)
    rest = nn(rest_ref[...], flat)
    rest = jnp.where(half_ref[...] > 0.0, pltpu.roll(rest, 64, 1), rest)[:, : ch - 128].astype(BF16)
    embedded = part_ref[...] + nt(jnp.concatenate([main, rest], axis=1), w_in[:, below:])
    r1 = lax.rsqrt(jnp.sum(embedded * embedded, axis=1, keepdims=True) * inv + EPS)
    unit1 = embedded * r1
    projected = nn((unit1 * g1).astype(BF16), w_qkv[...]).astype(BF16)
    cut = lambda block, h: projected[:, block * ch + h * dim : block * ch + (h + 1) * dim]
    residual = embedded
    for h in range(HEADS):
        score = nt(cut(1, h), cut(0, h)) * scale + bias_ref[...]
        weight = jnp.exp(score - jnp.max(score, axis=0, keepdims=True))
        p = weight * (1.0 / jnp.sum(weight, axis=0, keepdims=True))
        prob[h] = p
        mixed = tn(p.astype(BF16), cut(2, h))
        residual = residual + nn(mixed.astype(BF16), w_out[h * dim : (h + 1) * dim])
    r2 = lax.rsqrt(jnp.sum(residual * residual, axis=1, keepdims=True) * inv + EPS)
    unit2 = residual * r2
    alive = jnp.where(iota((stations, 1), 0) < live_ref[0], 1.0, 0.0)
    predicted = nn((unit2 * g2).astype(BF16), w_head[...]) * alive
    pred_ref[...] = predicted

    d_pred = (2.0 * alive) * mask_ref[...].astype(F32) * (predicted - obs_ref[...])
    u2 = nt(d_pred.astype(BF16), w_head[...]).astype(BF16).astype(F32) * g2
    d_res = r2 * (u2 - unit2 * (jnp.sum(u2 * unit2, axis=1, keepdims=True) * inv))
    d_res_b = d_res.astype(BF16)
    for h in range(HEADS):
        p = prob[h]
        d_mixed = nt(d_res_b, w_out[h * dim : (h + 1) * dim]).astype(BF16)
        d_p = nt(cut(2, h), d_mixed)
        d_score = p * (d_p - jnp.sum(p * d_p, axis=0, keepdims=True))
        d_score = (d_score * scale).astype(BF16)
        d_qkv[:, h * dim : (h + 1) * dim] = tn(d_score, cut(1, h)).astype(BF16)
        d_qkv[:, ch + h * dim : ch + (h + 1) * dim] = nn(d_score, cut(0, h)).astype(BF16)
        d_qkv[:, 2 * ch + h * dim : 2 * ch + (h + 1) * dim] = nn(p.astype(BF16), d_mixed).astype(BF16)
    u1 = nt(d_qkv[...], w_qkv[...]).astype(BF16).astype(F32) * g1
    d_emb = d_res + r1 * (u1 - unit1 * (jnp.sum(u1 * unit1, axis=1, keepdims=True) * inv))
    d_interp = nn(d_emb.astype(BF16), w_in[:, below:]).astype(BF16).astype(F32)
    extra = d_interp[:, 128:]
    blank = jnp.zeros((stations, 256 - ch), F32)
    parts = [
        d_interp[:, :128],
        jnp.concatenate([extra, blank], axis=1),
        jnp.concatenate([blank, extra], axis=1),
    ]
    out = nn(from_ref[...], jnp.concatenate(parts, axis=0).astype(BF16))
    out_ref[...] = out.astype(BF16).reshape(out_ref.shape)


def stations_pass(live, answer, prepared, obs, mask, w_in, g1, w_qkv, w_out, g2, w_head):
    n, ch = prepared[-1].shape
    return pl.pallas_call(
        station_kernel,
        out_shape=(SDS(obs.shape, F32), SDS(answer.shape, BF16)),
        in_specs=SCALARS + whole(15),
        out_specs=tuple(whole(2)),
        scratch_shapes=[VMEM((HEADS, n, n), F32), VMEM((n, 3 * ch), BF16)],
        compiler_params=PARAMS,
        name="stations",
    )(live, answer, *prepared, obs, mask, w_in, g1.reshape(1, -1), w_qkv, w_out, g2.reshape(1, -1), w_head)


def shift(x, axis, step, wrap):
    n = lax.axis_size(axis)
    pairs = [(i, (i + step) % n) for i in range(n) if wrap or 0 <= i + step < n]
    return lax.ppermute(x, axis, pairs)


def halo(top, bot, left, right):
    return (
        shift(top, "lat", 1, False),
        shift(bot, "lat", -1, False),
        shift(left, "lon", 1, True),
        shift(right, "lon", -1, True),
    )


def exchange(x):
    return lax.all_to_all(x, AXES, split_axis=0, concat_axis=0, tiled=True)


def diagonal_tiles():
    n_lat, n_lon = lax.axis_size("lat"), lax.axis_size("lon")
    lat = lax.axis_index("lat") + jnp.array([d[0] for d in DIAGONALS], jnp.int32)
    lon = lax.axis_index("lon") + jnp.array([d[1] for d in DIAGONALS], jnp.int32)
    return jnp.where((lat >= 0) & (lat < n_lat), lat * n_lon + (lon + n_lon) % n_lon, -1)


def on_device(
    grid_field,
    conv_weight,
    observed,
    hidden_mask,
    tile_route,
    station_spot,
    neighbours,
    neighbour_count,
    edge_bias,
    live_count,
    in_weight,
    norm_gain,
    qkv_weight,
    out_weight,
    final_gain,
    head_weight,
):
    n_lon = lax.axis_size("lon")
    regions = lax.axis_size("lat") * n_lon
    cap = max(2, 2 * observed.shape[0] // regions)
    tile = grid_field.shape[:2]
    route, spot = tile_route.reshape(1, -1), station_spot.reshape(1, -1)
    w_in = in_weight.T
    diag = diagonal_tiles()

    asks, xs, *sides = intro(route, spot, jnp.swapaxes(grid_field, 1, 2), regions)
    asked = exchange(asks)
    borders = halo(*sides)
    y = conv_core(xs, conv_weight)
    answer, gate = sample(diag, y, xs, conv_weight, asked, *borders, cap)
    answer = exchange(answer)
    prepared = prepare(
        route, spot, neighbours.T, neighbour_count, edge_bias.T, live_count, observed, hidden_mask, w_in,
        regions, cap, tile, n_lon,
    )
    predicted, outgoing = stations_pass(
        live_count, answer, prepared, observed, hidden_mask, w_in, norm_gain, qkv_weight, out_weight,
        final_gain, head_weight,
    )
    d_field, d_pre, *sides, corners = spread(diag, asked, exchange(outgoing), answer, gate, cap)
    borders = halo(*sides)
    grad = conv_core(d_pre, conv_weight, d_field)
    return predicted, jnp.swapaxes(finish(grad, conv_weight, *borders, corners), 1, 2)


def solution(mesh):
    split = P(AXES, None)
    one = P(AXES)
    in_specs = (
        P("lat", "lon", None), P(), split, split, split, one, split, one, split, one,
        P(), P(), P(), P(), P(), P(),
    )
    out_specs = (split, P("lat", "lon", None))
    return jax.shard_map(
        on_device, mesh=mesh, in_specs=in_specs, out_specs=out_specs, check_vma=False
    )
```

time: 138 us -> 108 us (0.78); the launches traced: 138 us -> 106 us
  Pallas kernels: 53.4 us -> 33.5 us
  waiting for transfers between devices: 14.8 us -> 0.03 us
  blocking collectives: 13.3 us -> 15.6 us
  starting transfers between devices: 27.4 us -> 29 us
    pallas_call x8, Pallas kernels: 53.4 us -> 33.5 us  [the longest x2 11.4 us: conv_core(): pl.pallas_call(functools.partial(conv_kernel, back, block), out_shape=SDS...]
    ppermute x8, waiting for transfers between devices: 10.6 us -> 0.02 us  [shift(): return lax.ppermute(x, axis, pairs)]
    unnamed x20 -> x64, local copies, waits for them, and re-layouts: 16.6 us -> 25.2 us
    slice x13 -> x0, local copies, waits for them, and re-layouts: 5.07 us -> none  [the longest x1 2.53 us: halo(): left = shift(x[:, cols - 1], 'lon', 1, True)]
    all_to_all x2, waiting for transfers between devices: 4.19 us -> 0.01 us  [exchange(): return lax.all_to_all(x, AXES, split_axis=0, concat_axis=0, tiled=True)]
    pallas_call x1 -> x0, local copies, waits for them, and re-layouts: 2.76 us -> none  [spread(): pl.pallas_call(spread_kernel, out_shape=(jax.ShapeDtypeStruct(gate.shape,...]
    all_to_all x1, blocking collectives: 13.3 us -> 15.6 us  [exchange(): return lax.all_to_all(x, AXES, split_axis=0, concat_axis=0, tiled=True)]
    concatenate x7 -> x0, other arithmetic: 1.96 us -> none  [the longest x2 1.26 us: halo(): left = jnp.concatenate([top[cols:cols + 1], left, bot[cols:cols + 1]])]
  transfers between devices with their start and end apart: 10 -> 10, of which waited for: 6 -> 0; matrix products, arithmetic and copies ran while one was open for 10% -> 1% of each run, Pallas kernels for 15% -> 13%
where the time goes in v1:
time: 108 us; the launch traced here: 106 us
  Pallas kernels  33.5 us (31%)
  starting transfers between devices  29 us (27%)
  local copies, waits for them, and re-layouts  25.2 us (23%)
  blocking collectives  15.6 us (14%)
  between operations  1.49 us (1%)
  other arithmetic  1.22 us (1%)
    unnamed x64, local copies, waits for them, and re-layouts  25.2 us
    ppermute x8, starting transfers between devices, shift(): return lax.ppermute(x, axis, pairs)  16.8 us
    all_to_all x1, blocking collectives, exchange(): return lax.all_to_all(x, AXES, split_axis=0, concat_axis=0, tiled=True)  15.6 us
    all_to_all x2, starting transfers between devices, exchange(): return lax.all_to_all(x, AXES, split_axis=0, concat_axis=0, tiled=True)  12.2 us
    pallas_call x2, Pallas kernels, conv_core(): pl.pallas_call(functools.partial(conv_kernel, back, block), out_shape=SDS...  11.4 us
    pallas_call x1, Pallas kernels, sample(): pl.pallas_call(functools.partial(sample_kernel, cap), out_shape=(SDS((reg...  6.15 us
    pallas_call x1, Pallas kernels, stations_pass(): pl.pallas_call(station_kernel, out_shape=(SDS(obs.shape, F32), SDS(answer...  5.03 us
    pallas_call x1, Pallas kernels, spread(): pl.pallas_call(functools.partial(spread_kernel, cap, block), out_shape=(S...  3.46 us
  transfers between devices with their start and end apart: 10, of which 0 were waited for; matrix products, arithmetic and copies ran while one was open for 1% of the time, Pallas kernels for 13%

profile of v1, /device:TPU:0, one launch (start us, length us, event | category | flops | bytes accessed | tf_op | source)
XLA Modules:
  0.0 106.1 jit_solution(15716015301934227361)
XLA Ops:
  0.6 0.0 copy-start.2
  0.6 0.0 copy-start.5
  0.6 1.5 %copy-done.5 = bf16[32,128,192]{1,2,0:T(8,128)(2,1)S(1)} copy-done((bf16[32,128,192]{1,2,0:T(8,128)(2,1)S(1)}, bf16[32,128,192]{1,2,0:T(8,128)(2,1)}, u32[]{:S(2)}) %copy-start.5) | copy-done | bytes 1572888
  2.1 0.7 copy-done.25
  2.8 0.7 copy-done.27
  3.5 2.2 %intro.1 = (f32[32,8,128]{2,1,0:T(8,128)}, bf16[34,128,256]{2,1,0:T(8,128)(2,1)S(1)}, bf16[128,192]{1,0:T(8,128)(2,1)}, bf16[128,192]{1,0:T(8,128)(2,1)}, bf16[3...) custom-call(s32[1,256]{1,0:T(1,128)S(1)} %bitcast.15, s32[1,256]{1,0:T(1,128)S(1)} %bitcast.17, bf16[32,192,128]{2,1,0:T(8,128)(2,1)S(1)} %bitcast.10), custom_call_target="tpu_custom_call" | custom-call | tf_op jit(solution)/shard_map/intro/pallas_call | solution.py:139
  5.7 7.3 %all-to-all-start = ((f32[32,8,128]{2,1,0:T(8,128)}), f32[32,8,128]{2,1,0:T(8,128)S(1)}, u32[]{:S(2)}, u32[]{:S(2)}) async-start(f32[32,8,128]{2,1,0:T(8,128)} %get-tuple-element.26), calls=%async_computation | async-start | bytes 262144 | tf_op jit(solution)/shard_map/all_to_all | solution.py:665
  13.0 4.3 %collective-permute-start = (bf16[128,192]{1,0:T(8,128)(2,1)}, bf16[128,192]{1,0:T(8,128)(2,1)}, u32[]{:S(2)}, u32[]{:S(2)}) collective-permute-start(bf16[128,192]{1,0:T(8,128)(2,1)} %get-tuple-element.27), channel_id=1, source_target_pairs={{0,8},{8,16},{16,24},{1,9},{9,17},{17,25},{2,10},{10,18},{18,26},{... | collective-permute-start | bytes 147464 | tf_op jit(solution)/shard_map/ppermute | solution.py:652
  17.3 1.3 %collective-permute-start.1 = (bf16[128,192]{1,0:T(8,128)(2,1)}, bf16[128,192]{1,0:T(8,128)(2,1)}, u32[]{:S(2)}, u32[]{:S(2)}) collective-permute-start(bf16[128,192]{1,0:T(8,128)(2,1)} %get-tuple-element.28), channel_id=1, source_target_pairs={{8,0},{16,8},{24,16},{9,1},{17,9},{25,17},{10,2},{18,10},{26,18},{... | collective-permute-start | bytes 147464 | tf_op jit(solution)/shard_map/ppermute | solution.py:652
  18.6 0.1 collective-permute-start.2
  18.7 3.5 %collective-permute-start.3 = (bf16[32,192]{1,0:T(8,128)(2,1)}, bf16[32,192]{1,0:T(8,128)(2,1)}, u32[]{:S(2)}, u32[]{:S(2)}) collective-permute-start(bf16[32,192]{1,0:T(8,128)(2,1)} %get-tuple-element.30), channel_id=1, source_target_pairs={{0,7},{1,0},{2,1},{3,2},{4,3},{5,4},{6,5},{7,6},{8,15},{9,8},{10,9... | collective-permute-start | bytes 36872 | tf_op jit(solution)/shard_map/ppermute | solution.py:652
  22.2 1.2 %and_select_fusion.1.diag_ref = s32[4]{0:T(128)} fusion(s32[4]{0:T(128)} %constant.33.clone, s32[4]{0:T(128)} %constant.34.clone, s32[]{:T(128)S(6)} %axis_index.25, s32[]{:T(128)S(6)} %axis_index.23), kind=kLoop, calls=%fused_computation.3 | loop fusion | flops 80 | bytes 56 | tf_op jit(solution)/shard_map/jit(_where)/select_n | solution.py:672
  23.4 0.0 copy-done.2
  23.4 5.7 %conv_core.1.y_ref = f32[32,128,192]{2,1,0:T(8,128)S(1)} custom-call(bf16[34,128,256]{2,1,0:T(8,128)(2,1)S(1)} %get-tuple-element.25.xs_ref, bf16[9,192,192]{2,1,0:T(8,128)(2,1)S(1)} %copy-done.2), custom_call_target="tpu_custom_call" | custom-call | tf_op jit(solution)/shard_map/conv_core/pallas_call | solution.py:200
  29.1 0.0 copy-start
  29.2 2.0 %copy-done = f32[32,128,192]{2,1,0:T(8,128)} copy-done((f32[32,128,192]{2,1,0:T(8,128)}, f32[32,128,192]{2,1,0:T(8,128)S(1)}, u32[]{:S(2)}) %copy-start) | copy-done | bytes 3145752
  31.1 0.0 collective-permute-done.2.left_ref
  31.1 0.0 collective-permute-done.3.right_ref
  31.1 0.0 collective-permute-done.top_ref
  31.1 0.0 collective-permute-done.1.bot_ref
  31.1 0.0 all-to-all-done.asked_ref
  31.1 0.0 copy-start.1
  31.2 2.2 %copy-done.1 = f32[32,128,192]{2,1,0:T(8,128)S(1)} copy-done((f32[32,128,192]{2,1,0:T(8,128)S(1)}, f32[32,128,192]{2,1,0:T(8,128)}, u32[]{:S(2)}) %copy-start.1) | copy-done | bytes 3145752
  33.3 0.6 copy-done.23
  34.0 6.2 %sample.1 = (bf16[32,32,128]{2,1,0:T(8,128)(2,1)S(1)}, bf16[32,128,192]{2,1,0:T(8,128)(2,1)S(1)}) custom-call(s32[4]{0:T(128)S(1)} %copy-done.23, f32[32,128,192]{2,1,0:T(8,128)S(1)} %copy-done.1, bf16[34,128,256]{2,1,0:T(8,128)(2,1)S(1)} %get-tuple-element.25.xs_ref, bf16[9,192,192]{2,1,0:T(8,128)(2,1)S(1)} %copy-done.2, ...), custom_call_target="tpu_custom_call" | custom-call | tf_op jit(solution)/shard_map/sample/pallas_call | solution.py:343
  40.1 1.3 %copy-done.3 = bf16[32,128,192]{2,1,0:T(8,128)(2,1)} copy-done((bf16[32,128,192]{2,1,0:T(8,128)(2,1)}, bf16[32,128,192]{2,1,0:T(8,128)(2,1)S(1)}, u32[]{:S(2)}) %copy-start.3) | copy-done | bytes 1572888
  41.4 0.7 copy-done.17
  42.1 4.9 %all-to-all-start.1 = ((bf16[32,32,128]{2,1,0:T(8,128)(2,1)}), bf16[32,32,128]{2,1,0:T(8,128)(2,1)S(1)}, u32[]{:S(2)}, u32[]{:S(2)}) async-start(bf16[32,32,128]{2,1,0:T(8,128)(2,1)} %copy-done.17), calls=%async_computation.1 | async-start | bytes 524288 | tf_op jit(solution)/shard_map/all_to_all | solution.py:665
  47.7 0.0 copy-done.6
  47.7 0.0 copy-start.7
  47.7 0.9 copy-done.7
  48.6 0.9 copy-done.9
  49.5 0.7 copy-done.21
  50.2 0.7 copy-done.22
  50.9 0.7 copy-done.26
  51.6 0.7 copy-done.28
  52.3 0.7 copy-done.29
  53.0 1.9 %prepare.1 = (bf16[256,1024]{1,0:T(8,128)(2,1)S(1)}, bf16[256,1024]{1,0:T(8,128)(2,1)S(1)}, f32[256,128]{1,0:T(8,128)S(1)}, bf16[1024,768]{1,0:T(8,128)(2,1)S(1)...) custom-call(s32[1]{0:T(128)S(6)} %copy.20.live_ref, s32[1,256]{1,0:T(1,128)S(1)} %bitcast.16, s32[1,256]{1,0:T(1,128)S(1)} %bitcast.18, ...), custom_call_target="tpu_custom_call" | custom-call | tf_op jit(solution)/shard_map/prepare/pallas_call | solution.py:557
  54.8 0.8 copy-done.11
  55.6 0.8 copy-done.13
  56.4 0.7 copy-done.15
  57.2 0.0 all-to-all-done.1.ans_ref
  57.2 0.9 copy-done.8
  58.1 0.9 copy-done.10
  59.0 1.0 copy-done.12
  60.0 1.0 copy-done.14
  61.1 0.9 copy-done.16
  62.0 0.9 copy-done.18
  63.0 0.8 copy-done.20
  63.8 0.7 copy-done.30
  64.5 0.7 copy-done.31
  65.1 5.0 %stations.1 = (f32[256,128]{1,0:T(8,128)}, bf16[32,32,128]{2,1,0:T(8,128)(2,1)S(1)}) custom-call(s32[1]{0:T(128)S(6)} %copy.20.live_ref, bf16[32,32,128]{2,1,0:T(8,128)(2,1)S(1)} %all-to-all-done.1.ans_ref, bf16[256,1024]{1,0:T(8,128)(2,1)S(1)} %copy-done.12, bf16[256,1024]{1,0:T(8,128)(2,1)S(1)} %copy-done.14, f32[256,128]{1,0:T(8,128)S(1)} %get-tuple-element.34.half_ref, ...), custom_call_target="tpu_custom_call" | custom-call | tf_op jit(solution)/shard_map/stations/pallas_call | solution.py:638
  70.2 15.6 %all_to_all.15.inc_ref = bf16[32,32,128]{2,1,0:T(8,128)(2,1)S(1)} all-to-all(bf16[32,32,128]{2,1,0:T(8,128)(2,1)S(1)} %get-tuple-element.39), channel_id=1, replica_groups=mesh['lat'=4,'lon'=8] {'lat','lon'}, dimensions={0} | all-to-all | bytes 524288 | tf_op jit(solution)/shard_map/all_to_all | solution.py:665
  85.8 3.5 %spread.1 = (f32[32,128,192]{2,1,0:T(8,128)S(1)}, bf16[34,128,256]{2,1,0:T(8,128)(2,1)S(1)}, bf16[128,192]{1,0:T(8,128)(2,1)S(1)}, bf16[128,192]{1,0:T(8,128)(2,...) custom-call(s32[4]{0:T(128)S(1)} %copy-done.24, ...), custom_call_target="tpu_custom_call" | custom-call | tf_op jit(solution)/shard_map/spread/pallas_call | solution.py:413
  89.3 2.8 %collective-permute-start.4 = (bf16[128,192]{1,0:T(8,128)(2,1)S(1)}, bf16[128,192]{1,0:T(8,128)(2,1)S(1)}, u32[]{:S(2)}, u32[]{:S(2)}) collective-permute-start(bf16[128,192]{1,0:T(8,128)(2,1)S(1)} %get-tuple-element.43), channel_id=1, source_target_pairs={{0,8},{8,16},{16,24},{1,9},{9,17},{17,25},{2,10},{10,18},{18,26},{... | collective-permute-start | bytes 147464 | tf_op jit(solution)/shard_map/ppermute | solution.py:652
  92.1 1.3 %collective-permute-start.5 = (bf16[128,192]{1,0:T(8,128)(2,1)S(1)}, bf16[128,192]{1,0:T(8,128)(2,1)S(1)}, u32[]{:S(2)}, u32[]{:S(2)}) collective-permute-start(bf16[128,192]{1,0:T(8,128)(2,1)S(1)} %get-tuple-element.44), channel_id=1, source_target_pairs={{8,0},{16,8},{24,16},{9,1},{17,9},{25,17},{10,2},{18,10},{26,18},{... | collective-permute-start | bytes 147464 | tf_op jit(solution)/shard_map/ppermute | solution.py:652
  93.4 0.5 collective-permute-start.6
  93.8 3.1 %collective-permute-start.7 = (bf16[32,192]{1,0:T(8,128)(2,1)S(1)}, bf16[32,192]{1,0:T(8,128)(2,1)S(1)}, u32[]{:S(2)}, u32[]{:S(2)}) collective-permute-start(bf16[32,192]{1,0:T(8,128)(2,1)S(1)} %get-tuple-element.46), channel_id=1, source_target_pairs={{0,7},{1,0},{2,1},{3,2},{4,3},{5,4},{6,5},{7,6},{8,15},{9,8},{10,9... | collective-permute-start | bytes 36872 | tf_op jit(solution)/shard_map/ppermute | solution.py:652
  97.0 5.7 %conv_back.1.g_ref = f32[32,128,192]{2,1,0:T(8,128)S(1)} custom-call(bf16[34,128,256]{2,1,0:T(8,128)(2,1)S(1)} %get-tuple-element.41.xs_ref, bf16[9,192,192]{2,1,0:T(8,128)(2,1)S(1)} %copy-done.2, f32[32,128,192]{2,1,0:T(8,128)S(1)} %get-tuple-element.42.refs_0_), custom_call_target="tpu_custom_call" | custom-call | tf_op jit(solution)/shard_map/conv_back/pallas_call | solution.py:200
  102.7 0.0 collective-permute-done.6.left_ref
  102.7 0.0 collective-permute-done.7.right_ref
  102.7 0.0 collective-permute-done.4.top_ref
  102.7 0.0 collective-permute-done.5.bot_ref
  102.8 3.3 %finish.1 = f32[32,192,128]{2,1,0:T(8,128)} custom-call(f32[32,128,192]{2,1,0:T(8,128)S(1)} %conv_back.1.g_ref, bf16[9,192,192]{2,1,0:T(8,128)(2,1)S(1)} %copy-done.2, bf16[128,192]{1,0:T(8,128)(2,1)S(1)} %collective-permute-done.4.top_ref, bf16[128,192]{1,0:T(8,128)(2,1)S(1)} %collective-permute-done.5.bot_ref, ...), custom_call_target="tpu_custom_call" | custom-call | tf_op jit(solution)/shard_map/finish/pallas_call | solution.py:456
  (30 shorter events, 0.0 us)
Async XLA Ops:
  0.6 22.8 %copy-start.2 = (bf16[9,192,192]{2,1,0:T(8,128)(2,1)S(1)}, bf16[9,192,192]{2,1,0:T(8,128)(2,1)}, u32[]{:S(2)}) copy-start(bf16[9,192,192]{2,1,0:T(8,128)(2,1)} %w_ref.7) | copy-start | bytes 1990660
  0.6 1.5 %copy-start.5 = (bf16[32,128,192]{1,2,0:T(8,128)(2,1)S(1)}, bf16[32,128,192]{1,2,0:T(8,128)(2,1)}, u32[]{:S(2)}) copy-start(bf16[32,128,192]{1,2,0:T(8,128)(2,1)} %param.18) | copy-start | bytes 4718596
  2.1 0.7 copy-start.25
  2.8 0.7 copy-start.27
  5.7 25.5 %all-to-all-start = ((f32[32,8,128]{2,1,0:T(8,128)}), f32[32,8,128]{2,1,0:T(8,128)S(1)}, u32[]{:S(2)}, u32[]{:S(2)}) async-start(f32[32,8,128]{2,1,0:T(8,128)} %get-tuple-element.26), calls=%async_computation | async-start | bytes 262144 | tf_op jit(solution)/shard_map/all_to_all | solution.py:665
  13.0 18.1 %collective-permute-start = (bf16[128,192]{1,0:T(8,128)(2,1)}, bf16[128,192]{1,0:T(8,128)(2,1)}, u32[]{:S(2)}, u32[]{:S(2)}) collective-permute-start(bf16[128,192]{1,0:T(8,128)(2,1)} %get-tuple-element.27), channel_id=1, source_target_pairs={{0,8},{8,16},{16,24},{1,9},{9,17},{17,25},{2,10},{10,18},{18,26},{... | collective-permute-start | bytes 147464 | tf_op jit(solution)/shard_map/ppermute | solution.py:652
  17.3 13.8 %collective-permute-start.1 = (bf16[128,192]{1,0:T(8,128)(2,1)}, bf16[128,192]{1,0:T(8,128)(2,1)}, u32[]{:S(2)}, u32[]{:S(2)}) collective-permute-start(bf16[128,192]{1,0:T(8,128)(2,1)} %get-tuple-element.28), channel_id=1, source_target_pairs={{8,0},{16,8},{24,16},{9,1},{17,9},{25,17},{10,2},{18,10},{26,18},{... | collective-permute-start | bytes 147464 | tf_op jit(solution)/shard_map/ppermute | solution.py:652
  18.6 12.5 %collective-permute-start.2 = (bf16[32,192]{1,0:T(8,128)(2,1)}, bf16[32,192]{1,0:T(8,128)(2,1)S(1)}, u32[]{:S(2)}, u32[]{:S(2)}) collective-permute-start(bf16[32,192]{1,0:T(8,128)(2,1)} %get-tuple-element.29), channel_id=1, source_target_pairs={{0,1},{1,2},{2,3},{3,4},{4,5},{5,6},{6,7},{7,0},{8,9},{9,10},{10,1... | collective-permute-start | bytes 36872 | tf_op jit(solution)/shard_map/ppermute | solution.py:652
  18.7 12.4 %collective-permute-start.3 = (bf16[32,192]{1,0:T(8,128)(2,1)}, bf16[32,192]{1,0:T(8,128)(2,1)}, u32[]{:S(2)}, u32[]{:S(2)}) collective-permute-start(bf16[32,192]{1,0:T(8,128)(2,1)} %get-tuple-element.30), channel_id=1, source_target_pairs={{0,7},{1,0},{2,1},{3,2},{4,3},{5,4},{6,5},{7,6},{8,15},{9,8},{10,9... | collective-permute-start | bytes 36872 | tf_op jit(solution)/shard_map/ppermute | solution.py:652
  23.4 24.2 %copy-start.6 = (bf16[448,192]{0,1:T(8,128)(2,1)S(1)}, bf16[448,192]{0,1:T(8,128)(2,1)}, u32[]{:S(2)}) copy-start(bf16[448,192]{0,1:T(8,128)(2,1)} %param.28) | copy-start | bytes 516100
  23.4 33.8 %copy-start.19 = (bf16[192,192]{1,0:T(8,128)(2,1)S(1)}, bf16[192,192]{1,0:T(8,128)(2,1)}, u32[]{:S(2)}) copy-start(bf16[192,192]{1,0:T(8,128)(2,1)} %w_out.1) | copy-start | bytes 221188
  29.1 2.0 %copy-start = (f32[32,128,192]{2,1,0:T(8,128)}, f32[32,128,192]{2,1,0:T(8,128)S(1)}, u32[]{:S(2)}) copy-start(f32[32,128,192]{2,1,0:T(8,128)S(1)} %conv_core.1.y_ref) | copy-start | bytes 9437188
  31.1 2.2 %copy-start.1 = (f32[32,128,192]{2,1,0:T(8,128)S(1)}, f32[32,128,192]{2,1,0:T(8,128)}, u32[]{:S(2)}) copy-start(f32[32,128,192]{2,1,0:T(8,128)} %copy-done) | copy-start | bytes 9437188
  33.3 0.6 copy-start.23
  40.1 1.3 %copy-start.3 = (bf16[32,128,192]{2,1,0:T(8,128)(2,1)}, bf16[32,128,192]{2,1,0:T(8,128)(2,1)S(1)}, u32[]{:S(2)}) copy-start(bf16[32,128,192]{2,1,0:T(8,128)(2,1)S(1)} %get-tuple-element.40.gate_ref) | copy-start | bytes 4718596
  41.4 0.7 copy-start.17
  42.1 15.0 %all-to-all-start.1 = ((bf16[32,32,128]{2,1,0:T(8,128)(2,1)}), bf16[32,32,128]{2,1,0:T(8,128)(2,1)S(1)}, u32[]{:S(2)}, u32[]{:S(2)}) async-start(bf16[32,32,128]{2,1,0:T(8,128)(2,1)} %copy-done.17), calls=%async_computation.1 | async-start | bytes 524288 | tf_op jit(solution)/shard_map/all_to_all | solution.py:665
  47.7 0.9 copy-start.7
  48.6 0.9 copy-start.9
  49.5 0.7 copy-start.21
  50.2 0.7 copy-start.22
  50.9 0.7 copy-start.26
  51.6 0.7 copy-start.28
  52.3 0.7 copy-start.29
  54.8 0.8 copy-start.11
  55.6 0.8 copy-start.13
  56.4 0.7 copy-start.15
  57.2 0.9 copy-start.8
  58.1 0.9 copy-start.10
  59.0 1.0 copy-start.12
  60.0 1.0 copy-start.14
  61.1 0.9 copy-start.16
  62.0 0.9 copy-start.18
  63.0 0.8 copy-start.20
  63.8 0.7 copy-start.30
  64.5 0.7 copy-start.31
  65.1 20.7 %copy-start.4 = (bf16[32,128,192]{2,1,0:T(8,128)(2,1)S(1)}, bf16[32,128,192]{2,1,0:T(8,128)(2,1)}, u32[]{:S(2)}) copy-start(bf16[32,128,192]{2,1,0:T(8,128)(2,1)} %copy-done.3) | copy-start | bytes 4718596
  65.1 20.7 %copy-start.24 = (s32[4]{0:T(128)S(1)}, s32[4]{0:T(128)}, u32[]{:S(2)}) copy-start(s32[4]{0:T(128)} %and_select_fusion.1.diag_ref) | copy-start | bytes 52
  89.3 13.4 %collective-permute-start.4 = (bf16[128,192]{1,0:T(8,128)(2,1)S(1)}, bf16[128,192]{1,0:T(8,128)(2,1)S(1)}, u32[]{:S(2)}, u32[]{:S(2)}) collective-permute-start(bf16[128,192]{1,0:T(8,128)(2,1)S(1)} %get-tuple-element.43), channel_id=1, source_target_pairs={{0,8},{8,16},{16,24},{1,9},{9,17},{17,25},{2,10},{10,18},{18,26},{... | collective-permute-start | bytes 147464 | tf_op jit(solution)/shard_map/ppermute | solution.py:652
  92.1 10.7 %collective-permute-start.5 = (bf16[128,192]{1,0:T(8,128)(2,1)S(1)}, bf16[128,192]{1,0:T(8,128)(2,1)S(1)}, u32[]{:S(2)}, u32[]{:S(2)}) collective-permute-start(bf16[128,192]{1,0:T(8,128)(2,1)S(1)} %get-tuple-element.44), channel_id=1, source_target_pairs={{8,0},{16,8},{24,16},{9,1},{17,9},{25,17},{10,2},{18,10},{26,18},{... | collective-permute-start | bytes 147464 | tf_op jit(solution)/shard_map/ppermute | solution.py:652
  93.4 9.3 %collective-permute-start.6 = (bf16[32,192]{1,0:T(8,128)(2,1)S(1)}, bf16[32,192]{1,0:T(8,128)(2,1)S(1)}, u32[]{:S(2)}, u32[]{:S(2)}) collective-permute-start(bf16[32,192]{1,0:T(8,128)(2,1)S(1)} %get-tuple-element.45), channel_id=1, source_target_pairs={{0,1},{1,2},{2,3},{3,4},{4,5},{5,6},{6,7},{7,0},{8,9},{9,10},{10,1... | collective-permute-start | bytes 36872 | tf_op jit(solution)/shard_map/ppermute | solution.py:652
  93.8 8.9 %collective-permute-start.7 = (bf16[32,192]{1,0:T(8,128)(2,1)S(1)}, bf16[32,192]{1,0:T(8,128)(2,1)S(1)}, u32[]{:S(2)}, u32[]{:S(2)}) collective-permute-start(bf16[32,192]{1,0:T(8,128)(2,1)S(1)} %get-tuple-element.46), channel_id=1, source_target_pairs={{0,7},{1,0},{2,1},{3,2},{4,3},{5,4},{6,5},{7,6},{8,15},{9,8},{10,9... | collective-permute-start | bytes 36872 | tf_op jit(solution)/shard_map/ppermute | solution.py:652

commit v2 on v1

--- a/solution.py
+++ b/solution.py
@@ -74,12 +74,14 @@
     return [r[:, :128] for r in rows] + halves
 
 
-def near_corners(diag_ref, slab_ref, base):
+def near_corners(slab_ref, base):
+    n_lat, n_lon = lax.axis_size("lat"), lax.axis_size("lon")
+    lat, lon = lax.axis_index("lat"), lax.axis_index("lon")
     rows = []
-    for q in range(4):
-        at = diag_ref[q]
-        tile = slab_ref[jnp.maximum(at, 0)].astype(F32)
-        rows.append(corner_rows(tile, base)[q] * jnp.where(at >= 0, 1.0, 0.0))
+    for q, (dy, dx) in enumerate(DIAGONALS):
+        inside = (lat + dy >= 0) & (lat + dy < n_lat)
+        at = jnp.where(inside, (lat + dy) * n_lon + (lon + dx + n_lon) % n_lon, 0)
+        rows.append(corner_rows(slab_ref[at].astype(F32), base)[q] * jnp.where(inside, 1.0, 0.0))
     return rows
 
 
@@ -94,29 +96,20 @@
     return rank_col, rank_row, route_col
 
 
-def intro_kernel(route_ref, spot_ref, x_ref, slab_ref, xs_ref, top_ref, bot_ref, left_ref, right_ref):
+def intro_kernel(route_ref, spot_ref, x_ref, slab_ref, top_ref, bot_ref, left_ref, right_ref):
     rows, ch, cols = x_ref.shape
     regions = slab_ref.shape[0]
     stations = route_ref.shape[1]
-    deep = xs_ref.shape[2]
     eye = onehot(iota((cols, cols), 0) == iota((cols, cols), 1))
-    pad = jnp.zeros((cols, deep - ch), BF16)
-    blank = jnp.zeros((cols, deep), BF16)
-    xs_ref[0] = blank
-    xs_ref[rows + 1] = blank
-    lefts, rights = [], []
-    for r in range(rows):
-        turned = nt(eye, x_ref[r])
-        lefts.append(turned[0:1])
-        rights.append(turned[cols - 1 : cols])
-        turned = turned.astype(BF16)
-        xs_ref[r + 1] = jnp.concatenate([turned, pad], axis=1)
-        if r == 0:
-            bot_ref[...] = turned
-        if r == rows - 1:
-            top_ref[...] = turned
-    left_ref[...] = jnp.concatenate(rights, axis=0).astype(BF16)
-    right_ref[...] = jnp.concatenate(lefts, axis=0).astype(BF16)
+    row, lane = iota((16, cols), 0), iota((16, cols), 1)
+    ends = onehot(((row == 0) & (lane == 0)) | ((row == 1) & (lane == cols - 1)))
+    pairs = [nt(ends, x_ref[r]) for r in range(rows)]
+    firsts = [p[0:1] for p in pairs]
+    lasts = [p[1:2] for p in pairs]
+    left_ref[...] = jnp.concatenate(lasts, axis=0).astype(BF16)
+    right_ref[...] = jnp.concatenate(firsts, axis=0).astype(BF16)
+    bot_ref[...] = nt(eye, x_ref[0]).astype(BF16)
+    top_ref[...] = nt(eye, x_ref[rows - 1]).astype(BF16)
 
     rank_col, _, _ = route_parts(route_ref[...], up(regions, 128))
     spot = spot_ref[...].astype(F32)
@@ -129,7 +122,7 @@
     )
     slab_ref[:, 0, :] = req
     slab_ref[:, 1, :] = req
-    mine = corner_tile([rights[-1], lefts[-1], rights[0], lefts[0]])
+    mine = corner_tile([lasts[-1], firsts[-1], lasts[0], firsts[0]])
     for k in range(6):
         slab_ref[:, 2 + k, :] = jnp.broadcast_to(mine[k], (regions, 128))
 
@@ -140,15 +133,13 @@
         intro_kernel,
         out_shape=(
             SDS((regions, 8, 128), F32),
-            SDS((rows + 2, cols, up(ch, 128)), BF16),
             SDS((cols, ch), BF16),
             SDS((cols, ch), BF16),
             SDS((rows, ch), BF16),
             SDS((rows, ch), BF16),
         ),
         in_specs=whole(3),
-        out_specs=tuple(whole(6)),
-        compiler_params=PARAMS,
+        out_specs=tuple(whole(5)),
         name="intro",
     )(route, spot, x_t)
 
@@ -165,11 +156,9 @@
                 wc[dx, dy * deep : dy * deep + ch, :] = w_ref[3 * dy + dx]
 
 
-def conv_kernel(back, block, xs_ref, w_ref, *refs):
-    o_ref, wc = refs[-2:]
+def conv_blocks(back, block, xs_ref, wc, add_ref, o_ref):
     rows, cols, ch = o_ref.shape
     deep = xs_ref.shape[2]
-    conv_weights(w_ref, wc, back)
     dot = nt if back else nn
     col = iota((block * cols, ch), 0) % cols
     first, last = col == 0, col == cols - 1
@@ -184,28 +173,56 @@
         total = total + jnp.where(last, 0.0, pltpu.roll(dot(lhs, wc[2]), block * cols - 1, 0))
         total = total.reshape(block, cols, ch)
         if back:
-            total = total + refs[0][pl.ds(r0, block)]
+            total = total + add_ref[pl.ds(r0, block)]
         o_ref[pl.ds(r0, block)] = total
         return carry
 
     lax.fori_loop(0, rows // block, body, 0)
 
 
-def conv_core(xs, taps, add=None, block=8):
-    rows, cols, deep = xs.shape
-    rows, ch = rows - 2, taps.shape[1]
-    back = add is not None
-    wc = (3, ch, 3 * deep) if back else (3, 3 * deep, ch)
-    args = (xs, taps, add) if back else (xs, taps)
+def conv_core_kernel(block, x_ref, w_ref, o_ref, xs_ref, wc):
+    rows, ch, cols = x_ref.shape
+    deep = xs_ref.shape[2]
+    eye = onehot(iota((cols, cols), 0) == iota((cols, cols), 1))
+    pad = jnp.zeros((cols, deep - ch), BF16)
+    xs_ref[0] = jnp.zeros((cols, deep), BF16)
+    xs_ref[rows + 1] = jnp.zeros((cols, deep), BF16)
+    for r in range(rows):
+        xs_ref[r + 1] = jnp.concatenate([nt(eye, x_ref[r]).astype(BF16), pad], axis=1)
+    conv_weights(w_ref, wc, False)
+    conv_blocks(False, block, xs_ref, wc, None, o_ref)
+
+
+def conv_back_kernel(block, xs_ref, w_ref, add_ref, o_ref, wc):
+    conv_weights(w_ref, wc, True)
+    conv_blocks(True, block, xs_ref, wc, add_ref, o_ref)
+
+
+def conv_core(x_t, taps, block=8):
+    rows, ch, cols = x_t.shape
+    deep = up(ch, 128)
     return pl.pallas_call(
-        functools.partial(conv_kernel, back, block),
-        out_shape=SDS((rows, cols, ch), F32),
-        in_specs=whole(len(args)),
+        functools.partial(conv_core_kernel, block),
+        out_shape=(SDS((rows, cols, ch), F32), SDS((rows + 2, cols, deep), BF16)),
+        in_specs=whole(2),
+        out_specs=tuple(whole(2)),
+        scratch_shapes=[VMEM((3, 3 * deep, ch), BF16)],
+        compiler_params=PARAMS,
+        name="conv_core",
+    )(x_t, taps)
+
+
+def conv_back(xs, taps, add, block=8):
+    rows, cols, ch = add.shape
+    return pl.pallas_call(
+        functools.partial(conv_back_kernel, block),
+        out_shape=SDS(add.shape, F32),
+        in_specs=whole(3),
         out_specs=whole(1)[0],
-        scratch_shapes=[VMEM(wc, BF16)],
+        scratch_shapes=[VMEM((3, ch, 3 * xs.shape[2]), BF16)],
         compiler_params=PARAMS,
-        name="conv_back" if back else "conv_core",
-    )(*args)
+        name="conv_back",
+    )(xs, taps, add)
 
 
 def border_rows(line, w_ref, dy, back):
@@ -286,14 +303,14 @@
 
 
 def sample_kernel(
-    cap, diag_ref, y_ref, xs_ref, w_ref, asked_ref, top_ref, bot_ref, left_ref, right_ref, ans_ref, gate_ref,
-    field, fix, edge, pack,
+    cap, y_ref, xs_ref, w_ref, asked_ref, top_ref, bot_ref, left_ref, right_ref, ans_hbm, gate_hbm,
+    field, fix, edge, pack, gate_ref, ans_ref, sem,
 ):
     rows, cols, ch = gate_ref.shape
     regions = ans_ref.shape[0]
     slots = regions * cap
     half = cap // 2
-    tl, tr, bl, br = near_corners(diag_ref, asked_ref, 2)
+    tl, tr, bl, br = near_corners(asked_ref, 2)
     edge[0] = border_rows(top_ref[...], w_ref, 0, False)
     edge[1] = border_rows(bot_ref[...], w_ref, 2, False)
     fix[0] = border_cols(left_ref[...], (tl, bl), w_ref, 0, False)
@@ -313,6 +330,8 @@
     lax.fori_loop(1, rows - 1, inner, 0)
     gates(rows - 1, y_ref[rows - 1] + edge[1])
 
+    gate_out = pltpu.make_async_copy(gate_ref, gate_hbm, sem.at[0])
+    gate_out.start()
     spot = spots_column(asked_ref[:, 0, :], slots)
     r, c, a, b = fine_cell(spot, cols)
     by_row = hat(iota_f((slots, rows), 1), r, a)
@@ -334,30 +353,37 @@
     for k in range(6):
         pack[:, cap + half + k, :] = jnp.broadcast_to(mine[k], (regions, 128))
     ans_ref[...] = pack[...].astype(BF16)
-
-
-def sample(diag, y, xs, taps, asked, top, bot, left, right, cap):
+    ans_out = pltpu.make_async_copy(ans_ref, ans_hbm, sem.at[1])
+    ans_out.start()
+    gate_out.wait()
+    ans_out.wait()
+
+
+def sample(y, xs, taps, asked, top, bot, left, right, cap):
     rows, cols, ch = y.shape
     regions = asked.shape[0]
     deep = slab_rows(cap)
     return pl.pallas_call(
         functools.partial(sample_kernel, cap),
         out_shape=(SDS((regions, deep, 128), BF16), SDS((rows, cols, ch), BF16)),
-        in_specs=SCALARS + whole(8),
-        out_specs=tuple(whole(2)),
+        in_specs=whole(8),
+        out_specs=(pl.BlockSpec(memory_space=pltpu.HBM),) * 2,
         scratch_shapes=[
             VMEM((rows * cols, ch), BF16),
             VMEM((2, rows, ch), F32),
             VMEM((2, cols, ch), F32),
             VMEM((regions, deep, 128), F32),
+            VMEM((rows, cols, ch), BF16),
+            VMEM((regions, deep, 128), BF16),
+            pltpu.SemaphoreType.DMA((2,)),
         ],
         compiler_params=PARAMS,
         name="sample",
-    )(diag, y, xs, taps, asked, top, bot, left, right)
+    )(y, xs, taps, asked, top, bot, left, right)
 
 
 def spread_kernel(
-    cap, block, diag_ref, asked_ref, inc_ref, ans_ref, gate_ref, df_ref, dp_ref, top_ref, bot_ref, left_ref,
+    cap, block, asked_ref, inc_ref, ans_ref, gate_ref, df_ref, dp_ref, top_ref, bot_ref, left_ref,
     right_ref, corner_ref, by_row, inc, edges,
 ):
     rows, cols, ch = gate_ref.shape
@@ -402,12 +428,12 @@
     right_ref[...] = edges[0].astype(BF16)
     left_ref[...] = edges[1].astype(BF16)
     base = cap + half
-    gates = near_corners(diag_ref, ans_ref, base)
+    gates = near_corners(ans_ref, base)
     corners = [g * s for g, s in zip(gates, corner_rows(sums, base))]
     corner_ref[...] = jnp.concatenate(corners + [jnp.zeros((4, ch), F32)], axis=0)
 
 
-def spread(diag, asked, incoming, answer, gate, cap, block=4):
+def spread(asked, incoming, answer, gate, cap, block=4):
     rows, cols, ch = gate.shape
     slots = incoming.shape[0] * cap
     return pl.pallas_call(
@@ -421,12 +447,12 @@
             SDS((rows, ch), BF16),
             SDS((8, ch), F32),
         ),
-        in_specs=SCALARS + whole(4),
+        in_specs=whole(4),
         out_specs=tuple(whole(7)),
         scratch_shapes=[VMEM((rows, slots), F32), VMEM((slots, ch), F32), VMEM((2, rows, ch), F32)],
         compiler_params=PARAMS,
         name="spread",
-    )(diag, asked, incoming, answer, gate)
+    )(asked, incoming, answer, gate)
 
 
 def finish_kernel(g_ref, w_ref, top_ref, bot_ref, left_ref, right_ref, corner_ref, o_ref, fix, edge):
@@ -566,14 +592,13 @@
         ),
         in_specs=SCALARS + whole(8),
         out_specs=tuple(whole(6)),
-        compiler_params=PARAMS,
         name="prepare",
     )(live, route, spot, near, count.reshape(1, -1), bias, obs, mask, w_in)
 
 
 def station_kernel(
-    live_ref, ans_ref, to_ref, rest_ref, half_ref, from_ref, bias_ref, part_ref, obs_ref, mask_ref, w_in, g1_ref,
-    w_qkv, w_out, g2_ref, w_head, pred_ref, out_ref, prob, d_qkv,
+    live_ref, ans_ref, to_ref, rest_ref, half_ref, from_hbm, bias_ref, part_ref, obs_ref, mask_ref, w_in, g1_ref,
+    w_qkv, w_out, g2_ref, w_head, pred_ref, out_ref, prob, d_qkv, from_ref, sem,
 ):
     stations, packed = to_ref.shape
     ch = part_ref.shape[1]
@@ -582,6 +607,8 @@
     below = w_in.shape[1] - ch
     inv = 1.0 / ch
     g1, g2 = g1_ref[...], g2_ref[...]
+    fetch = pltpu.make_async_copy(from_hbm, from_ref, sem)
+    fetch.start()
 
     flat = ans_ref[...].reshape(packed, 128)
     main = nn(to_ref[...], flat).astype(BF16)
@@ -629,19 +656,26 @@
         jnp.concatenate([extra, blank], axis=1),
         jnp.concatenate([blank, extra], axis=1),
     ]
+    fetch.wait()
     out = nn(from_ref[...], jnp.concatenate(parts, axis=0).astype(BF16))
     out_ref[...] = out.astype(BF16).reshape(out_ref.shape)
 
 
 def stations_pass(live, answer, prepared, obs, mask, w_in, g1, w_qkv, w_out, g2, w_head):
     n, ch = prepared[-1].shape
+    specs = SCALARS + whole(15)
+    specs[5] = pl.BlockSpec(memory_space=pltpu.HBM)
     return pl.pallas_call(
         station_kernel,
         out_shape=(SDS(obs.shape, F32), SDS(answer.shape, BF16)),
-        in_specs=SCALARS + whole(15),
+        in_specs=specs,
         out_specs=tuple(whole(2)),
-        scratch_shapes=[VMEM((HEADS, n, n), F32), VMEM((n, 3 * ch), BF16)],
-        compiler_params=PARAMS,
+        scratch_shapes=[
+            VMEM((HEADS, n, n), F32),
+            VMEM((n, 3 * ch), BF16),
+            VMEM(prepared[3].shape, BF16),
+            pltpu.SemaphoreType.DMA,
+        ],
         name="stations",
     )(live, answer, *prepared, obs, mask, w_in, g1.reshape(1, -1), w_qkv, w_out, g2.reshape(1, -1), w_head)
 
@@ -663,13 +697,6 @@
 
 def exchange(x):
     return lax.all_to_all(x, AXES, split_axis=0, concat_axis=0, tiled=True)
-
-
-def diagonal_tiles():
-    n_lat, n_lon = lax.axis_size("lat"), lax.axis_size("lon")
-    lat = lax.axis_index("lat") + jnp.array([d[0] for d in DIAGONALS], jnp.int32)
-    lon = lax.axis_index("lon") + jnp.array([d[1] for d in DIAGONALS], jnp.int32)
-    return jnp.where((lat >= 0) & (lat < n_lat), lat * n_lon + (lon + n_lon) % n_lon, -1)
 
 
 def on_device(
@@ -696,13 +723,14 @@
     tile = grid_field.shape[:2]
     route, spot = tile_route.reshape(1, -1), station_spot.reshape(1, -1)
     w_in = in_weight.T
-    diag = diagonal_tiles()
-
-    asks, xs, *sides = intro(route, spot, jnp.swapaxes(grid_field, 1, 2), regions)
+
+    x_t = jnp.swapaxes(grid_field, 1, 2)
+    asks, *sides = intro(route, spot, x_t, regions)
     asked = exchange(asks)
     borders = halo(*sides)
-    y = conv_core(xs, conv_weight)
-    answer, gate = sample(diag, y, xs, conv_weight, asked, *borders, cap)
+    asked, x_in = lax.optimization_barrier((asked, x_t))
+    y, xs = conv_core(x_in, conv_weight)
+    answer, gate = sample(y, xs, conv_weight, asked, *borders, cap)
     answer = exchange(answer)
     prepared = prepare(
         route, spot, neighbours.T, neighbour_count, edge_bias.T, live_count, observed, hidden_mask, w_in,
@@ -712,9 +740,9 @@
         live_count, answer, prepared, observed, hidden_mask, w_in, norm_gain, qkv_weight, out_weight,
         final_gain, head_weight,
     )
-    d_field, d_pre, *sides, corners = spread(diag, asked, exchange(outgoing), answer, gate, cap)
+    d_field, d_pre, *sides, corners = spread(asked, exchange(outgoing), answer, gate, cap)
     borders = halo(*sides)
-    grad = conv_core(d_pre, conv_weight, d_field)
+    grad = conv_back(d_pre, conv_weight, d_field)
     return predicted, jnp.swapaxes(finish(grad, conv_weight, *borders, corners), 1, 2)
 
 

time: 108 us -> 92.6 us (0.86)
  local copies, waits for them, and re-layouts: 25.2 us -> 3.75 us
  Pallas kernels: 33.5 us -> 39.6 us
  waiting for transfers between devices: 0.03 us -> 5.36 us
  blocking collectives: 15.6 us -> 12.9 us
  other arithmetic: 1.22 us -> 0 us
    unnamed x64 -> x10, local copies, waits for them, and re-layouts: 25.2 us -> 3.75 us
    all_to_all x2, waiting for transfers between devices: 0.01 us -> 5.34 us  [exchange(): return lax.all_to_all(x, AXES, split_axis=0, concat_axis=0, tiled=True)]
    all_to_all x1, blocking collectives: 15.6 us -> 12.9 us  [exchange(): return lax.all_to_all(x, AXES, split_axis=0, concat_axis=0, tiled=True)]
    pallas_call x1, Pallas kernels: 5.03 us -> 7.59 us  [stations_pass(): pl.pallas_call(station_kernel, out_shape=(SDS(obs.shape, F32), SDS(answer...]
    pallas_call x1, Pallas kernels: 1.86 us -> 4.02 us  [prepare(): pl.pallas_call(functools.partial(prepare_kernel, cap, tile, n_lon), out_s...]
    pallas_call x1, Pallas kernels: 2.2 us -> 3.5 us  [intro(): pl.pallas_call(intro_kernel, out_shape=(SDS((regions, 8, 128), F32), SDS(...]
    pallas_call x2, Pallas kernels: 11.4 us -> 12.7 us  [the longest x1 6.85 us: conv_core(): pl.pallas_call(functools.partial(conv_core_kernel, block), out_shape=(SDS...]
    select_n x1 -> x0, other arithmetic: 1.22 us -> none  [diagonal_tiles(): jnp.where((lat >= 0) & (lat < n_lat), lat * n_lon + (lon + n_lon) % n_lon...]
  transfers between devices with their start and end apart: 10 -> 10, of which waited for: 0 -> 1; matrix products, arithmetic and copies ran while one was open for 1% -> 0% of each run, Pallas kernels for 13% -> 18%
where the time goes in v2:
time: 92.6 us; the launch traced here: 91.5 us
  Pallas kernels  39.6 us (43%)
  starting transfers between devices  28.5 us (31%)
  blocking collectives  12.9 us (14%)
  waiting for transfers between devices  5.36 us (6%)
  local copies, waits for them, and re-layouts  3.75 us (4%)
  between operations  1.45 us (2%)
    ppermute x8, starting transfers between devices, shift(): return lax.ppermute(x, axis, pairs)  16.2 us
    all_to_all x1, blocking collectives, exchange(): return lax.all_to_all(x, AXES, split_axis=0, concat_axis=0, tiled=True)  12.9 us
    all_to_all x2, starting transfers between devices, exchange(): return lax.all_to_all(x, AXES, split_axis=0, concat_axis=0, tiled=True)  12.2 us
    pallas_call x1, Pallas kernels, stations_pass(): pl.pallas_call(station_kernel, out_shape=(SDS(obs.shape, F32), SDS(answer...  7.59 us
    pallas_call x1, Pallas kernels, conv_core(): pl.pallas_call(functools.partial(conv_core_kernel, block), out_shape=(SDS...  6.85 us
    pallas_call x1, Pallas kernels, conv_back(): pl.pallas_call(functools.partial(conv_back_kernel, block), out_shape=SDS(...  5.87 us
    pallas_call x1, Pallas kernels, sample(): pl.pallas_call(functools.partial(sample_kernel, cap), out_shape=(SDS((reg...  5.52 us
    all_to_all x2, waiting for transfers between devices, exchange(): return lax.all_to_all(x, AXES, split_axis=0, concat_axis=0, tiled=True)  5.34 us
  transfers between devices with their start and end apart: 10, of which 1 were waited for; matrix products, arithmetic and copies ran while one was open for 0% of the time, Pallas kernels for 18%

profile of v2, /device:TPU:0, one launch (start us, length us, event | category | flops | bytes accessed | tf_op | source)
XLA Modules:
  0.0 91.5 jit_solution(773249494247482586)
XLA Ops:
  0.6 0.0 copy-start
  0.6 3.5 %intro.1 = (f32[32,8,128]{2,1,0:T(8,128)}, bf16[128,192]{1,0:T(8,128)(2,1)}, bf16[128,192]{1,0:T(8,128)(2,1)}, bf16[32,192]{1,0:T(8,128)(2,1)}, bf16[32,192]{1,0:T(8,128)(2,1)}) custom-call(s32[1,256]{1,0:T(1,128)} %bitcast.17, s32[1,256]{1,0:T(1,128)} %bitcast.19, bf16[32,192,128]{2,1,0:T(8,128)(2,1)} %bitcast.10), custom_call_target="tpu_custom_call" | custom-call | tf_op jit(solution)/shard_map/intro/pallas_call | solution.py:132
  4.1 7.3 %all-to-all-start = ((f32[32,8,128]{2,1,0:T(8,128)}), f32[32,8,128]{2,1,0:T(8,128)S(1)}, u32[]{:S(2)}, u32[]{:S(2)}) async-start(f32[32,8,128]{2,1,0:T(8,128)} %get-tuple-element.28), calls=%async_computation | async-start | bytes 262144 | tf_op jit(solution)/shard_map/all_to_all | solution.py:699
  11.5 3.7 %collective-permute-start = (bf16[128,192]{1,0:T(8,128)(2,1)}, bf16[128,192]{1,0:T(8,128)(2,1)S(1)}, u32[]{:S(2)}, u32[]{:S(2)}) collective-permute-start(bf16[128,192]{1,0:T(8,128)(2,1)} %get-tuple-element.33), channel_id=1, source_target_pairs={{0,8},{8,16},{16,24},{1,9},{9,17},{17,25},{2,10},{10,18},{18,26},{... | collective-permute-start | bytes 147464 | tf_op jit(solution)/shard_map/ppermute | solution.py:686
  15.2 1.3 %collective-permute-start.1 = (bf16[128,192]{1,0:T(8,128)(2,1)}, bf16[128,192]{1,0:T(8,128)(2,1)S(1)}, u32[]{:S(2)}, u32[]{:S(2)}) collective-permute-start(bf16[128,192]{1,0:T(8,128)(2,1)} %get-tuple-element.34), channel_id=1, source_target_pairs={{8,0},{16,8},{24,16},{9,1},{17,9},{25,17},{10,2},{18,10},{26,18},{... | collective-permute-start | bytes 147464 | tf_op jit(solution)/shard_map/ppermute | solution.py:686
  16.5 0.1 collective-permute-start.2
  16.5 3.5 %collective-permute-start.3 = (bf16[32,192]{1,0:T(8,128)(2,1)}, bf16[32,192]{1,0:T(8,128)(2,1)S(1)}, u32[]{:S(2)}, u32[]{:S(2)}) collective-permute-start(bf16[32,192]{1,0:T(8,128)(2,1)} %get-tuple-element.36), channel_id=1, source_target_pairs={{0,7},{1,0},{2,1},{3,2},{4,3},{5,4},{6,5},{7,6},{8,15},{9,8},{10,9... | collective-permute-start | bytes 36872 | tf_op jit(solution)/shard_map/ppermute | solution.py:686
  20.0 0.0 all-to-all-done.asked_ref
  20.1 0.0 copy-done
  20.1 0.0 copy-start.1
  20.1 1.4 %copy-done.1 = bf16[32,128,192]{1,2,0:T(8,128)(2,1)S(1)} copy-done((bf16[32,128,192]{1,2,0:T(8,128)(2,1)S(1)}, bf16[32,128,192]{1,2,0:T(8,128)(2,1)}, u32[]{:S(2)}) %copy-start.1) | copy-done | bytes 1572888
  21.5 6.9 %conv_core.1 = (f32[32,128,192]{2,1,0:T(8,128)S(1)}, bf16[34,128,256]{2,1,0:T(8,128)(2,1)S(1)}) custom-call(bf16[32,192,128]{2,1,0:T(8,128)(2,1)S(1)} %bitcast.11, bf16[9,192,192]{2,1,0:T(8,128)(2,1)S(1)} %copy-done), custom_call_target="tpu_custom_call" | custom-call | tf_op jit(solution)/shard_map/conv_core/pallas_call | solution.py:204
  28.3 0.0 collective-permute-done.2.left_ref
  28.3 0.0 collective-permute-done.3.right_ref
  28.3 0.0 collective-permute-done.top_ref
  28.4 0.0 collective-permute-done.1.bot_ref
  28.4 5.5 %sample.1 = (bf16[32,32,128]{2,1,0:T(8,128)(2,1)S(1)}, bf16[32,128,192]{2,1,0:T(8,128)(2,1)S(1)}) custom-call(f32[32,128,192]{2,1,0:T(8,128)S(1)} %get-tuple-element.30.y_ref, bf16[34,128,256]{2,1,0:T(8,128)(2,1)S(1)} %get-tuple-element.31.xs_ref, bf16[9,192,192]{2,1,0:T(8,128)(2,1)S(1)} %copy-done, f32[32,8,128]{2,1,0:T(8,128)S(1)} %all-to-all-done.asked_ref, ...), custom_call_target="tpu_custom_call" | custom-call | tf_op jit(solution)/shard_map/sample/pallas_call | solution.py:366
  33.9 0.0 copy-start.4
  33.9 0.7 copy-done.4
  34.6 4.9 %all-to-all-start.1 = ((bf16[32,32,128]{2,1,0:T(8,128)(2,1)}), bf16[32,32,128]{2,1,0:T(8,128)(2,1)S(1)}, u32[]{:S(2)}, u32[]{:S(2)}) async-start(bf16[32,32,128]{2,1,0:T(8,128)(2,1)} %copy-done.4), calls=%async_computation.1 | async-start | bytes 524288 | tf_op jit(solution)/shard_map/all_to_all | solution.py:699
  40.2 4.0 %prepare.1 = (bf16[256,1024]{1,0:T(8,128)(2,1)}, bf16[256,1024]{1,0:T(8,128)(2,1)}, f32[256,128]{1,0:T(8,128)}, bf16[1024,768]{1,0:T(8,128)(2,1)}, f32[256,256]{1,0:T(8,128)}, /*index=5*/f32[256,192]{1,0:T(8,128)}) custom-call(s32[1]{0:T(128)S(6)} %copy.18.live_ref, s32[1,256]{1,0:T(1,128)} %bitcast.18, s32[1,256]{1,0:T(1,128)} %bitcast.20, ...), custom_call_target="tpu_custom_call" | custom-call | tf_op jit(solution)/shard_map/prepare/pallas_call | solution.py:583
  44.2 5.3 %all-to-all-done.1.ans_ref = bf16[32,32,128]{2,1,0:T(8,128)(2,1)S(1)} async-done(((bf16[32,32,128]{2,1,0:T(8,128)(2,1)}), bf16[32,32,128]{2,1,0:T(8,128)(2,1)S(1)}, u32[]{:S(2)}, u32[]{:S(2)}) %all-to-all-start.1) | async-done | bytes 262176 | tf_op jit(solution)/shard_map/all_to_all | solution.py:699
  49.5 0.0 copy-start.2
  49.5 0.7 copy-done.2
  50.2 7.6 %stations.1 = (f32[256,128]{1,0:T(8,128)}, bf16[32,32,128]{2,1,0:T(8,128)(2,1)}) custom-call(s32[1]{0:T(128)S(6)} %copy.18.live_ref, bf16[32,32,128]{2,1,0:T(8,128)(2,1)} %copy-done.2, bf16[256,1024]{1,0:T(8,128)(2,1)} %get-tuple-element.38.to_ref, bf16[256,1024]{1,0:T(8,128)(2,1)} %get-tuple-element.39.rest_ref, f32[256,128]{1,0:T(8,128)} %get-tuple-element.40.half_ref, ...), custom_call_target="tpu_custom_call" | custom-call | tf_op jit(solution)/shard_map/stations/pallas_call | solution.py:668
  57.8 12.9 %all_to_all.15.inc_ref = bf16[32,32,128]{2,1,0:T(8,128)(2,1)S(1)} all-to-all(bf16[32,32,128]{2,1,0:T(8,128)(2,1)} %get-tuple-element.45), channel_id=1, replica_groups=mesh['lat'=4,'lon'=8] {'lat','lon'}, dimensions={0} | all-to-all | bytes 524288 | tf_op jit(solution)/shard_map/all_to_all | solution.py:699
  70.7 0.0 copy-start.3
  70.7 0.9 %copy-done.3 = bf16[32,32,128]{2,1,0:T(8,128)(2,1)S(1)} copy-done((bf16[32,32,128]{2,1,0:T(8,128)(2,1)S(1)}, bf16[32,32,128]{2,1,0:T(8,128)(2,1)}, u32[]{:S(2)}) %copy-start.3) | copy-done | bytes 262168
  71.6 2.9 %spread.1 = (f32[32,128,192]{2,1,0:T(8,128)S(1)}, bf16[34,128,256]{2,1,0:T(8,128)(2,1)S(1)}, bf16[128,192]{1,0:T(8,128)(2,1)S(1)}, bf16[128,192]{1,0:T(8,128)(2,...) custom-call(f32[32,8,128]{2,1,0:T(8,128)S(1)} %all-to-all-done.asked_ref, ...), custom_call_target="tpu_custom_call" | custom-call | tf_op jit(solution)/shard_map/spread/pallas_call | solution.py:439
  74.5 2.8 %collective-permute-start.4 = (bf16[128,192]{1,0:T(8,128)(2,1)S(1)}, bf16[128,192]{1,0:T(8,128)(2,1)S(1)}, u32[]{:S(2)}, u32[]{:S(2)}) collective-permute-start(bf16[128,192]{1,0:T(8,128)(2,1)S(1)} %get-tuple-element.49), channel_id=1, source_target_pairs={{0,8},{8,16},{16,24},{1,9},{9,17},{17,25},{2,10},{10,18},{18,26},{... | collective-permute-start | bytes 147464 | tf_op jit(solution)/shard_map/ppermute | solution.py:686
  77.3 1.3 %collective-permute-start.5 = (bf16[128,192]{1,0:T(8,128)(2,1)S(1)}, bf16[128,192]{1,0:T(8,128)(2,1)S(1)}, u32[]{:S(2)}, u32[]{:S(2)}) collective-permute-start(bf16[128,192]{1,0:T(8,128)(2,1)S(1)} %get-tuple-element.50), channel_id=1, source_target_pairs={{8,0},{16,8},{24,16},{9,1},{17,9},{25,17},{10,2},{18,10},{26,18},{... | collective-permute-start | bytes 147464 | tf_op jit(solution)/shard_map/ppermute | solution.py:686
  78.6 0.5 collective-permute-start.6
  79.1 3.1 %collective-permute-start.7 = (bf16[32,192]{1,0:T(8,128)(2,1)S(1)}, bf16[32,192]{1,0:T(8,128)(2,1)S(1)}, u32[]{:S(2)}, u32[]{:S(2)}) collective-permute-start(bf16[32,192]{1,0:T(8,128)(2,1)S(1)} %get-tuple-element.52), channel_id=1, source_target_pairs={{0,7},{1,0},{2,1},{3,2},{4,3},{5,4},{6,5},{7,6},{8,15},{9,8},{10,9... | collective-permute-start | bytes 36872 | tf_op jit(solution)/shard_map/ppermute | solution.py:686
  82.2 5.9 %conv_back.1.g_ref = f32[32,128,192]{2,1,0:T(8,128)S(1)} custom-call(bf16[34,128,256]{2,1,0:T(8,128)(2,1)S(1)} %get-tuple-element.47.xs_ref, bf16[9,192,192]{2,1,0:T(8,128)(2,1)S(1)} %copy-done, f32[32,128,192]{2,1,0:T(8,128)S(1)} %get-tuple-element.48.add_ref), custom_call_target="tpu_custom_call" | custom-call | tf_op jit(solution)/shard_map/conv_back/pallas_call | solution.py:217
  88.1 0.0 collective-permute-done.6.left_ref
  88.1 0.0 collective-permute-done.7.right_ref
  88.1 0.0 collective-permute-done.4.top_ref
  88.1 0.0 collective-permute-done.5.bot_ref
  88.2 3.3 %finish.1 = f32[32,192,128]{2,1,0:T(8,128)} custom-call(f32[32,128,192]{2,1,0:T(8,128)S(1)} %conv_back.1.g_ref, bf16[9,192,192]{2,1,0:T(8,128)(2,1)S(1)} %copy-done, bf16[128,192]{1,0:T(8,128)(2,1)S(1)} %collective-permute-done.4.top_ref, bf16[128,192]{1,0:T(8,128)(2,1)S(1)} %collective-permute-done.5.bot_ref, ...), custom_call_target="tpu_custom_call" | custom-call | tf_op jit(solution)/shard_map/finish/pallas_call | solution.py:482
Async XLA Ops:
  0.6 19.4 %copy-start = (bf16[9,192,192]{2,1,0:T(8,128)(2,1)S(1)}, bf16[9,192,192]{2,1,0:T(8,128)(2,1)}, u32[]{:S(2)}) copy-start(bf16[9,192,192]{2,1,0:T(8,128)(2,1)} %w_ref.7) | copy-start | bytes 1990660
  4.1 15.9 %all-to-all-start = ((f32[32,8,128]{2,1,0:T(8,128)}), f32[32,8,128]{2,1,0:T(8,128)S(1)}, u32[]{:S(2)}, u32[]{:S(2)}) async-start(f32[32,8,128]{2,1,0:T(8,128)} %get-tuple-element.28), calls=%async_computation | async-start | bytes 262144 | tf_op jit(solution)/shard_map/all_to_all | solution.py:699
  11.5 16.9 %collective-permute-start = (bf16[128,192]{1,0:T(8,128)(2,1)}, bf16[128,192]{1,0:T(8,128)(2,1)S(1)}, u32[]{:S(2)}, u32[]{:S(2)}) collective-permute-start(bf16[128,192]{1,0:T(8,128)(2,1)} %get-tuple-element.33), channel_id=1, source_target_pairs={{0,8},{8,16},{16,24},{1,9},{9,17},{17,25},{2,10},{10,18},{18,26},{... | collective-permute-start | bytes 147464 | tf_op jit(solution)/shard_map/ppermute | solution.py:686
  15.2 13.2 %collective-permute-start.1 = (bf16[128,192]{1,0:T(8,128)(2,1)}, bf16[128,192]{1,0:T(8,128)(2,1)S(1)}, u32[]{:S(2)}, u32[]{:S(2)}) collective-permute-start(bf16[128,192]{1,0:T(8,128)(2,1)} %get-tuple-element.34), channel_id=1, source_target_pairs={{8,0},{16,8},{24,16},{9,1},{17,9},{25,17},{10,2},{18,10},{26,18},{... | collective-permute-start | bytes 147464 | tf_op jit(solution)/shard_map/ppermute | solution.py:686
  16.5 11.9 %collective-permute-start.2 = (bf16[32,192]{1,0:T(8,128)(2,1)}, bf16[32,192]{1,0:T(8,128)(2,1)S(1)}, u32[]{:S(2)}, u32[]{:S(2)}) collective-permute-start(bf16[32,192]{1,0:T(8,128)(2,1)} %get-tuple-element.35), channel_id=1, source_target_pairs={{0,1},{1,2},{2,3},{3,4},{4,5},{5,6},{6,7},{7,0},{8,9},{9,10},{10,1... | collective-permute-start | bytes 36872 | tf_op jit(solution)/shard_map/ppermute | solution.py:686
  16.5 11.8 %collective-permute-start.3 = (bf16[32,192]{1,0:T(8,128)(2,1)}, bf16[32,192]{1,0:T(8,128)(2,1)S(1)}, u32[]{:S(2)}, u32[]{:S(2)}) collective-permute-start(bf16[32,192]{1,0:T(8,128)(2,1)} %get-tuple-element.36), channel_id=1, source_target_pairs={{0,7},{1,0},{2,1},{3,2},{4,3},{5,4},{6,5},{7,6},{8,15},{9,8},{10,9... | collective-permute-start | bytes 36872 | tf_op jit(solution)/shard_map/ppermute | solution.py:686
  20.1 1.4 %copy-start.1 = (bf16[32,128,192]{1,2,0:T(8,128)(2,1)S(1)}, bf16[32,128,192]{1,2,0:T(8,128)(2,1)}, u32[]{:S(2)}) copy-start(bf16[32,128,192]{1,2,0:T(8,128)(2,1)} %param.16) | copy-start | bytes 4718596
  33.9 0.7 copy-start.4
  34.6 14.9 %all-to-all-start.1 = ((bf16[32,32,128]{2,1,0:T(8,128)(2,1)}), bf16[32,32,128]{2,1,0:T(8,128)(2,1)S(1)}, u32[]{:S(2)}, u32[]{:S(2)}) async-start(bf16[32,32,128]{2,1,0:T(8,128)(2,1)} %copy-done.4), calls=%async_computation.1 | async-start | bytes 524288 | tf_op jit(solution)/shard_map/all_to_all | solution.py:699
  49.5 0.7 copy-start.2
  70.7 1.0 %copy-start.3 = (bf16[32,32,128]{2,1,0:T(8,128)(2,1)S(1)}, bf16[32,32,128]{2,1,0:T(8,128)(2,1)}, u32[]{:S(2)}) copy-start(bf16[32,32,128]{2,1,0:T(8,128)(2,1)} %copy-done.2) | copy-start | bytes 786436
  74.5 13.6 %collective-permute-start.4 = (bf16[128,192]{1,0:T(8,128)(2,1)S(1)}, bf16[128,192]{1,0:T(8,128)(2,1)S(1)}, u32[]{:S(2)}, u32[]{:S(2)}) collective-permute-start(bf16[128,192]{1,0:T(8,128)(2,1)S(1)} %get-tuple-element.49), channel_id=1, source_target_pairs={{0,8},{8,16},{16,24},{1,9},{9,17},{17,25},{2,10},{10,18},{18,26},{... | collective-permute-start | bytes 147464 | tf_op jit(solution)/shard_map/ppermute | solution.py:686
  77.3 10.8 %collective-permute-start.5 = (bf16[128,192]{1,0:T(8,128)(2,1)S(1)}, bf16[128,192]{1,0:T(8,128)(2,1)S(1)}, u32[]{:S(2)}, u32[]{:S(2)}) collective-permute-start(bf16[128,192]{1,0:T(8,128)(2,1)S(1)} %get-tuple-element.50), channel_id=1, source_target_pairs={{8,0},{16,8},{24,16},{9,1},{17,9},{25,17},{10,2},{18,10},{26,18},{... | collective-permute-start | bytes 147464 | tf_op jit(solution)/shard_map/ppermute | solution.py:686
  78.6 9.5 %collective-permute-start.6 = (bf16[32,192]{1,0:T(8,128)(2,1)S(1)}, bf16[32,192]{1,0:T(8,128)(2,1)S(1)}, u32[]{:S(2)}, u32[]{:S(2)}) collective-permute-start(bf16[32,192]{1,0:T(8,128)(2,1)S(1)} %get-tuple-element.51), channel_id=1, source_target_pairs={{0,1},{1,2},{2,3},{3,4},{4,5},{5,6},{6,7},{7,0},{8,9},{9,10},{10,1... | collective-permute-start | bytes 36872 | tf_op jit(solution)/shard_map/ppermute | solution.py:686
  79.1 9.0 %collective-permute-start.7 = (bf16[32,192]{1,0:T(8,128)(2,1)S(1)}, bf16[32,192]{1,0:T(8,128)(2,1)S(1)}, u32[]{:S(2)}, u32[]{:S(2)}) collective-permute-start(bf16[32,192]{1,0:T(8,128)(2,1)S(1)} %get-tuple-element.52), channel_id=1, source_target_pairs={{0,7},{1,0},{2,1},{3,2},{4,3},{5,4},{6,5},{7,6},{8,15},{9,8},{10,9... | collective-permute-start | bytes 36872 | tf_op jit(solution)/shard_map/ppermute | solution.py:686

commit v3 on v2

--- a/solution.py
+++ b/solution.py
@@ -51,6 +51,19 @@
     return [pl.BlockSpec(memory_space=VMEM)] * count
 
 
+def hbm(x):
+    return pltpu.with_memory_space_constraint(x, pltpu.HBM)
+
+
+def in_hbm(count):
+    return [pl.BlockSpec(memory_space=pltpu.HBM)] * count
+
+
+def inside(dy):
+    lat = lax.axis_index("lat") + dy
+    return jnp.where((lat >= 0) & (lat < lax.axis_size("lat")), 1.0, 0.0)
+
+
 SCALARS = [pl.BlockSpec(memory_space=pltpu.SMEM)]
 SDS = jax.ShapeDtypeStruct
 
@@ -96,10 +109,21 @@
     return rank_col, rank_row, route_col
 
 
-def intro_kernel(route_ref, spot_ref, x_ref, slab_ref, top_ref, bot_ref, left_ref, right_ref):
+def intro_kernel(route_ref, spot_ref, x_hbm, slab_ref, top_ref, bot_ref, left_ref, right_ref, x_ref, slab, sem):
     rows, ch, cols = x_ref.shape
+    fetch = pltpu.make_async_copy(x_hbm, x_ref, sem)
+    fetch.start()
     regions = slab_ref.shape[0]
     stations = route_ref.shape[1]
+    rank_col, _, _ = route_parts(route_ref[...], up(regions, 128))
+    spot = spot_ref[...].astype(F32)
+    high = jnp.floor(spot * (1.0 / 256.0))
+    low = spot - 256.0 * high
+    member = route_ref[...] == iota((regions, stations), 0)
+    ranked = onehot(rank_col == iota_f((stations, 128), 1))
+    slab[:, 0, :] = nn(jnp.where(member, high, 0.0).astype(BF16), ranked)
+    slab[:, 1, :] = nn(jnp.where(member, low, 0.0).astype(BF16), ranked)
+    fetch.wait()
     eye = onehot(iota((cols, cols), 0) == iota((cols, cols), 1))
     row, lane = iota((16, cols), 0), iota((16, cols), 1)
     ends = onehot(((row == 0) & (lane == 0)) | ((row == 1) & (lane == cols - 1)))
@@ -110,21 +134,10 @@
     right_ref[...] = jnp.concatenate(firsts, axis=0).astype(BF16)
     bot_ref[...] = nt(eye, x_ref[0]).astype(BF16)
     top_ref[...] = nt(eye, x_ref[rows - 1]).astype(BF16)
-
-    rank_col, _, _ = route_parts(route_ref[...], up(regions, 128))
-    spot = spot_ref[...].astype(F32)
-    high = jnp.floor(spot * (1.0 / 256.0))
-    low = spot - 256.0 * high
-    member = route_ref[...] == iota((regions, stations), 0)
-    ranked = onehot(rank_col == iota_f((stations, 128), 1))
-    req = 256.0 * nn(jnp.where(member, high, 0.0).astype(BF16), ranked) + nn(
-        jnp.where(member, low, 0.0).astype(BF16), ranked
-    )
-    slab_ref[:, 0, :] = req
-    slab_ref[:, 1, :] = req
     mine = corner_tile([lasts[-1], firsts[-1], lasts[0], firsts[0]])
     for k in range(6):
-        slab_ref[:, 2 + k, :] = jnp.broadcast_to(mine[k], (regions, 128))
+        slab[:, 2 + k, :] = jnp.broadcast_to(mine[k], (regions, 128))
+    slab_ref[...] = slab[...].astype(BF16)
 
 
 def intro(route, spot, x_t, regions):
@@ -132,16 +145,17 @@
     return pl.pallas_call(
         intro_kernel,
         out_shape=(
-            SDS((regions, 8, 128), F32),
+            SDS((regions, 8, 128), BF16),
             SDS((cols, ch), BF16),
             SDS((cols, ch), BF16),
             SDS((rows, ch), BF16),
             SDS((rows, ch), BF16),
         ),
-        in_specs=whole(3),
+        in_specs=whole(2) + in_hbm(1),
         out_specs=tuple(whole(5)),
+        scratch_shapes=[VMEM(x_t.shape, BF16), VMEM((regions, 8, 128), F32), pltpu.SemaphoreType.DMA],
         name="intro",
-    )(route, spot, x_t)
+    )(route, spot, hbm(x_t))
 
 
 def conv_weights(w_ref, wc, back):
@@ -180,42 +194,53 @@
     lax.fori_loop(0, rows // block, body, 0)
 
 
-def conv_core_kernel(block, x_ref, w_ref, o_ref, xs_ref, wc):
+def conv_core_kernel(parts, x_hbm, w_ref, o_ref, xs_ref, wc, x_ref, sem):
     rows, ch, cols = x_ref.shape
     deep = xs_ref.shape[2]
+    size = rows // parts
+    at = [pl.ds(k * size, size) for k in range(parts)]
+    fetches = [pltpu.make_async_copy(x_hbm.at[a], x_ref.at[a], sem.at[k]) for k, a in enumerate(at)]
+    for fetch in fetches:
+        fetch.start()
+    conv_weights(w_ref, wc, False)
     eye = onehot(iota((cols, cols), 0) == iota((cols, cols), 1))
     pad = jnp.zeros((cols, deep - ch), BF16)
     xs_ref[0] = jnp.zeros((cols, deep), BF16)
     xs_ref[rows + 1] = jnp.zeros((cols, deep), BF16)
     for r in range(rows):
+        if r % size == 0:
+            fetches[r // size].wait()
         xs_ref[r + 1] = jnp.concatenate([nt(eye, x_ref[r]).astype(BF16), pad], axis=1)
-    conv_weights(w_ref, wc, False)
-    conv_blocks(False, block, xs_ref, wc, None, o_ref)
-
-
-def conv_back_kernel(block, xs_ref, w_ref, add_ref, o_ref, wc):
+    conv_blocks(False, rows, xs_ref, wc, None, o_ref)
+
+
+def conv_back_kernel(xs_ref, w_ref, add_ref, o_ref, wc):
     conv_weights(w_ref, wc, True)
-    conv_blocks(True, block, xs_ref, wc, add_ref, o_ref)
-
-
-def conv_core(x_t, taps, block=8):
+    conv_blocks(True, o_ref.shape[0], xs_ref, wc, add_ref, o_ref)
+
+
+def conv_core(x_t, taps, parts=4):
     rows, ch, cols = x_t.shape
     deep = up(ch, 128)
     return pl.pallas_call(
-        functools.partial(conv_core_kernel, block),
+        functools.partial(conv_core_kernel, parts),
         out_shape=(SDS((rows, cols, ch), F32), SDS((rows + 2, cols, deep), BF16)),
-        in_specs=whole(2),
+        in_specs=in_hbm(1) + whole(1),
         out_specs=tuple(whole(2)),
-        scratch_shapes=[VMEM((3, 3 * deep, ch), BF16)],
+        scratch_shapes=[
+            VMEM((3, 3 * deep, ch), BF16),
+            VMEM(x_t.shape, BF16),
+            pltpu.SemaphoreType.DMA((parts,)),
+        ],
         compiler_params=PARAMS,
         name="conv_core",
-    )(x_t, taps)
-
-
-def conv_back(xs, taps, add, block=8):
+    )(hbm(x_t), taps)
+
+
+def conv_back(xs, taps, add):
     rows, cols, ch = add.shape
     return pl.pallas_call(
-        functools.partial(conv_back_kernel, block),
+        conv_back_kernel,
         out_shape=SDS(add.shape, F32),
         in_specs=whole(3),
         out_specs=whole(1)[0],
@@ -303,16 +328,16 @@
 
 
 def sample_kernel(
-    cap, y_ref, xs_ref, w_ref, asked_ref, top_ref, bot_ref, left_ref, right_ref, ans_hbm, gate_hbm,
-    field, fix, edge, pack, gate_ref, ans_ref, sem,
+    cap, y_ref, xs_ref, w_ref, asked_ref, top_ref, bot_ref, left_ref, right_ref, ans_hbm, gate_hbm, spots_hbm,
+    field, fix, edge, pack, gate_ref, ans_ref, spots_ref, sem,
 ):
     rows, cols, ch = gate_ref.shape
     regions = ans_ref.shape[0]
     slots = regions * cap
     half = cap // 2
     tl, tr, bl, br = near_corners(asked_ref, 2)
-    edge[0] = border_rows(top_ref[...], w_ref, 0, False)
-    edge[1] = border_rows(bot_ref[...], w_ref, 2, False)
+    edge[0] = inside(-1) * border_rows(top_ref[...], w_ref, 0, False)
+    edge[1] = inside(1) * border_rows(bot_ref[...], w_ref, 2, False)
     fix[0] = border_cols(left_ref[...], (tl, bl), w_ref, 0, False)
     fix[1] = border_cols(right_ref[...], (tr, br), w_ref, 2, False)
 
@@ -330,9 +355,13 @@
     lax.fori_loop(1, rows - 1, inner, 0)
     gates(rows - 1, y_ref[rows - 1] + edge[1])
 
+    asked = asked_ref[...].astype(F32)
+    spots_ref[...] = 256.0 * asked[:, 0, :] + asked[:, 1, :]
     gate_out = pltpu.make_async_copy(gate_ref, gate_hbm, sem.at[0])
     gate_out.start()
-    spot = spots_column(asked_ref[:, 0, :], slots)
+    spots_out = pltpu.make_async_copy(spots_ref, spots_hbm, sem.at[2])
+    spots_out.start()
+    spot = spots_column(spots_ref[...], slots)
     r, c, a, b = fine_cell(spot, cols)
     by_row = hat(iota_f((slots, rows), 1), r, a)
     by_col = hat(iota_f((slots, cols), 1), c, b)
@@ -355,6 +384,7 @@
     ans_ref[...] = pack[...].astype(BF16)
     ans_out = pltpu.make_async_copy(ans_ref, ans_hbm, sem.at[1])
     ans_out.start()
+    spots_out.wait()
     gate_out.wait()
     ans_out.wait()
 
@@ -365,9 +395,13 @@
     deep = slab_rows(cap)
     return pl.pallas_call(
         functools.partial(sample_kernel, cap),
-        out_shape=(SDS((regions, deep, 128), BF16), SDS((rows, cols, ch), BF16)),
+        out_shape=(
+            pltpu.HBM((regions, deep, 128), BF16),
+            pltpu.HBM((rows, cols, ch), BF16),
+            pltpu.HBM((regions, 128), F32),
+        ),
         in_specs=whole(8),
-        out_specs=(pl.BlockSpec(memory_space=pltpu.HBM),) * 2,
+        out_specs=tuple(in_hbm(3)),
         scratch_shapes=[
             VMEM((rows * cols, ch), BF16),
             VMEM((2, rows, ch), F32),
@@ -375,7 +409,8 @@
             VMEM((regions, deep, 128), F32),
             VMEM((rows, cols, ch), BF16),
             VMEM((regions, deep, 128), BF16),
-            pltpu.SemaphoreType.DMA((2,)),
+            VMEM((regions, 128), F32),
+            pltpu.SemaphoreType.DMA((3,)),
         ],
         compiler_params=PARAMS,
         name="sample",
@@ -383,18 +418,26 @@
 
 
 def spread_kernel(
-    cap, block, asked_ref, inc_ref, ans_ref, gate_ref, df_ref, dp_ref, top_ref, bot_ref, left_ref,
-    right_ref, corner_ref, by_row, inc, edges,
+    cap, block, spots_hbm, inc_hbm, gates_hbm, gate_ref, df_ref, dp_ref, top_ref, bot_ref, left_ref,
+    right_ref, corner_ref, by_row, inc, edges, spots_ref, inc_ref, gates_ref, sem,
 ):
+    fetches = [
+        pltpu.make_async_copy(there, here, sem.at[k])
+        for k, (there, here) in enumerate(((spots_hbm, spots_ref), (inc_hbm, inc_ref), (gates_hbm, gates_ref)))
+    ]
+    for fetch in fetches:
+        fetch.start()
+    fetches[0].wait()
     rows, cols, ch = gate_ref.shape
     regions = inc_ref.shape[0]
     slots = regions * cap
     half = cap // 2
     deep = dp_ref.shape[2]
-    spot = spots_row(asked_ref[:, 0, :], slots)
+    spot = spots_row(spots_ref[...], slots)
     r, c, a, b = fine_cell(spot, cols)
     by_row[...] = hat(iota_f((rows, slots), 0), r, a)
     by_col = hat(iota_f((cols, slots), 0), c, b)
+    fetches[1].wait()
     sums = jnp.zeros((inc_ref.shape[1], 128), F32)
     for t in range(regions):
         at = t * cap
@@ -428,12 +471,12 @@
     right_ref[...] = edges[0].astype(BF16)
     left_ref[...] = edges[1].astype(BF16)
     base = cap + half
-    gates = near_corners(ans_ref, base)
-    corners = [g * s for g, s in zip(gates, corner_rows(sums, base))]
+    fetches[2].wait()
+    corners = [gates_ref[q : q + 1] * s for q, s in enumerate(corner_rows(sums, base))]
     corner_ref[...] = jnp.concatenate(corners + [jnp.zeros((4, ch), F32)], axis=0)
 
 
-def spread(asked, incoming, answer, gate, cap, block=4):
+def spread(spots, incoming, gates, gate, cap, block=4):
     rows, cols, ch = gate.shape
     slots = incoming.shape[0] * cap
     return pl.pallas_call(
@@ -447,12 +490,20 @@
             SDS((rows, ch), BF16),
             SDS((8, ch), F32),
         ),
-        in_specs=whole(4),
+        in_specs=in_hbm(3) + whole(1),
         out_specs=tuple(whole(7)),
-        scratch_shapes=[VMEM((rows, slots), F32), VMEM((slots, ch), F32), VMEM((2, rows, ch), F32)],
+        scratch_shapes=[
+            VMEM((rows, slots), F32),
+            VMEM((slots, ch), F32),
+            VMEM((2, rows, ch), F32),
+            VMEM(spots.shape, F32),
+            VMEM(incoming.shape, BF16),
+            VMEM(gates.shape, F32),
+            pltpu.SemaphoreType.DMA((3,)),
+        ],
         compiler_params=PARAMS,
         name="spread",
-    )(asked, incoming, answer, gate)
+    )(hbm(spots), hbm(incoming), hbm(gates), gate)
 
 
 def finish_kernel(g_ref, w_ref, top_ref, bot_ref, left_ref, right_ref, corner_ref, o_ref, fix, edge):
@@ -463,8 +514,8 @@
     @pl.when(step == 0)
     def _():
         corners = corner_ref[...]
-        edge[0] = border_rows(top_ref[...], w_ref, 0, True)
-        edge[1] = border_rows(bot_ref[...], w_ref, 2, True)
+        edge[0] = inside(-1) * border_rows(top_ref[...], w_ref, 0, True)
+        edge[1] = inside(1) * border_rows(bot_ref[...], w_ref, 2, True)
         fix[0] = border_cols(left_ref[...], (corners[0:1], corners[2:3]), w_ref, 0, True)
         fix[1] = border_cols(right_ref[...], (corners[1:2], corners[3:4]), w_ref, 2, True)
 
@@ -493,9 +544,9 @@
 
 def prepare_kernel(
     cap, tile, n_lon, live_ref, route_ref, spot_ref, near_ref, count_ref, bias_ref, obs_ref, mask_ref, w_ref,
-    to_ref, rest_ref, half_ref, from_ref, bias_out, part_ref,
+    from_ref, bias_out, part_ref, index_ref,
 ):
-    stations, packed = to_ref.shape
+    packed, stations = from_ref.shape[0], index_ref.shape[0]
     features = obs_ref.shape[1]
     deep = slab_rows(cap)
     regions = packed // deep
@@ -504,10 +555,10 @@
     route = route_ref[...]
     rank_col, rank_row, route_col = route_parts(route, up(regions, 128))
     upper = jnp.where(rank_col >= half, 1.0, 0.0)
-    at = iota_f((stations, packed), 1)
-    to_ref[...] = onehot(at == route_col * deep + rank_col)
-    rest_ref[...] = onehot(at == route_col * deep + cap + rank_col - half * upper)
-    half_ref[...] = jnp.broadcast_to(upper, (stations, 128))
+    lane = iota((stations, 128), 1)
+    main_at = route_col * deep + rank_col
+    rest_at = route_col * deep + cap + rank_col - half * upper
+    index_ref[...] = jnp.where(lane == 0, main_at, jnp.where(lane == 1, rest_at, upper))
 
     row, col, a, b = fine_cell(spot_ref[...].astype(F32), cols)
     share = []
@@ -583,42 +634,57 @@
     return pl.pallas_call(
         functools.partial(prepare_kernel, cap, tile, n_lon),
         out_shape=(
-            SDS((stations, packed), BF16),
-            SDS((stations, packed), BF16),
-            SDS((stations, 128), F32),
             SDS((packed, 3 * stations), BF16),
             SDS((stations, stations), F32),
             SDS((stations, w_in.shape[0]), F32),
+            SDS((stations, 128), F32),
         ),
         in_specs=SCALARS + whole(8),
-        out_specs=tuple(whole(6)),
+        out_specs=tuple(whole(4)),
         name="prepare",
     )(live, route, spot, near, count.reshape(1, -1), bias, obs, mask, w_in)
 
 
-def station_kernel(
-    live_ref, ans_ref, to_ref, rest_ref, half_ref, from_hbm, bias_ref, part_ref, obs_ref, mask_ref, w_in, g1_ref,
-    w_qkv, w_out, g2_ref, w_head, pred_ref, out_ref, prob, d_qkv, from_ref, sem,
-):
-    stations, packed = to_ref.shape
-    ch = part_ref.shape[1]
+def station_kernel(cap, live_ref, ans_ref, *refs):
+    there, (pred_hbm, out_hbm, gates_hbm) = refs[:12], refs[12:15]
+    here = refs[15:27]
+    prob, d_qkv, pred_ref, out_ref, gates_ref, sem = refs[27:]
+    fetches = [pltpu.make_async_copy(a, b, sem.at[k]) for k, (a, b) in enumerate(zip(there, here))]
+    for copy in fetches:
+        copy.start()
+    index_ref, part_ref, w_in, g1_ref, w_qkv, bias_ref, w_out, g2_ref, w_head, mask_ref, obs_ref, from_ref = here
+    need = lambda first, last: [copy.wait() for copy in fetches[first:last]]
+    stores = [
+        pltpu.make_async_copy(a, b, sem.at[12 + k])
+        for k, (a, b) in enumerate(((pred_ref, pred_hbm), (out_ref, out_hbm), (gates_ref, gates_hbm)))
+    ]
+    stations, ch = part_ref.shape
+    packed = from_ref.shape[0]
     dim = ch // HEADS
     scale = 1.0 / math.sqrt(dim)
     below = w_in.shape[1] - ch
     inv = 1.0 / ch
-    g1, g2 = g1_ref[...], g2_ref[...]
-    fetch = pltpu.make_async_copy(from_hbm, from_ref, sem)
-    fetch.start()
-
+
+    base = cap + cap // 2
+    gates_ref[...] = jnp.concatenate(near_corners(ans_ref, base) + [jnp.zeros((4, ch), F32)], axis=0)
+    stores[2].start()
+    need(0, 3)
+    at = iota_f((stations, packed), 1)
+    to = onehot(at == index_ref[:, 0:1])
+    to_rest = onehot(at == index_ref[:, 1:2])
     flat = ans_ref[...].reshape(packed, 128)
-    main = nn(to_ref[...], flat).astype(BF16)
-    rest = nn(rest_ref[...], flat)
-    rest = jnp.where(half_ref[...] > 0.0, pltpu.roll(rest, 64, 1), rest)[:, : ch - 128].astype(BF16)
+    main = nn(to, flat).astype(BF16)
+    rest = nn(to_rest, flat)
+    rest = jnp.where(index_ref[:, 2:3] > 0.0, pltpu.roll(rest, 64, 1), rest)[:, : ch - 128].astype(BF16)
     embedded = part_ref[...] + nt(jnp.concatenate([main, rest], axis=1), w_in[:, below:])
     r1 = lax.rsqrt(jnp.sum(embedded * embedded, axis=1, keepdims=True) * inv + EPS)
     unit1 = embedded * r1
+    need(3, 6)
+    g1 = g1_ref[...]
     projected = nn((unit1 * g1).astype(BF16), w_qkv[...]).astype(BF16)
     cut = lambda block, h: projected[:, block * ch + h * dim : block * ch + (h + 1) * dim]
+    need(6, 11)
+    g2 = g2_ref[...]
     residual = embedded
     for h in range(HEADS):
         score = nt(cut(1, h), cut(0, h)) * scale + bias_ref[...]
@@ -632,6 +698,7 @@
     alive = jnp.where(iota((stations, 1), 0) < live_ref[0], 1.0, 0.0)
     predicted = nn((unit2 * g2).astype(BF16), w_head[...]) * alive
     pred_ref[...] = predicted
+    stores[0].start()
 
     d_pred = (2.0 * alive) * mask_ref[...].astype(F32) * (predicted - obs_ref[...])
     u2 = nt(d_pred.astype(BF16), w_head[...]).astype(BF16).astype(F32) * g2
@@ -656,43 +723,46 @@
         jnp.concatenate([extra, blank], axis=1),
         jnp.concatenate([blank, extra], axis=1),
     ]
-    fetch.wait()
+    need(11, 12)
     out = nn(from_ref[...], jnp.concatenate(parts, axis=0).astype(BF16))
     out_ref[...] = out.astype(BF16).reshape(out_ref.shape)
-
-
-def stations_pass(live, answer, prepared, obs, mask, w_in, g1, w_qkv, w_out, g2, w_head):
-    n, ch = prepared[-1].shape
-    specs = SCALARS + whole(15)
-    specs[5] = pl.BlockSpec(memory_space=pltpu.HBM)
+    stores[1].start()
+    for store in stores:
+        store.wait()
+
+
+def stations_pass(live, answer, prepared, obs, mask, w_in, g1, w_qkv, w_out, g2, w_head, cap):
+    outgoing, table, part, index = prepared
+    n, ch = part.shape
+    late = (
+        index, part, w_in, g1.reshape(1, -1), w_qkv, table, w_out, g2.reshape(1, -1), w_head, mask, obs, outgoing
+    )
+    outs = (pltpu.HBM(obs.shape, F32), pltpu.HBM(answer.shape, BF16), pltpu.HBM((8, ch), F32))
     return pl.pallas_call(
-        station_kernel,
-        out_shape=(SDS(obs.shape, F32), SDS(answer.shape, BF16)),
-        in_specs=specs,
-        out_specs=tuple(whole(2)),
+        functools.partial(station_kernel, cap),
+        out_shape=outs,
+        in_specs=SCALARS + whole(1) + in_hbm(len(late)),
+        out_specs=tuple(in_hbm(3)),
         scratch_shapes=[
+            *[VMEM(v.shape, v.dtype) for v in late],
             VMEM((HEADS, n, n), F32),
             VMEM((n, 3 * ch), BF16),
-            VMEM(prepared[3].shape, BF16),
-            pltpu.SemaphoreType.DMA,
+            *[VMEM(o.shape, o.dtype) for o in outs],
+            pltpu.SemaphoreType.DMA((len(late) + len(outs),)),
         ],
+        compiler_params=PARAMS,
         name="stations",
-    )(live, answer, *prepared, obs, mask, w_in, g1.reshape(1, -1), w_qkv, w_out, g2.reshape(1, -1), w_head)
-
-
-def shift(x, axis, step, wrap):
+    )(live, answer, *[hbm(v) for v in late])
+
+
+def shift(x, axis, step):
     n = lax.axis_size(axis)
-    pairs = [(i, (i + step) % n) for i in range(n) if wrap or 0 <= i + step < n]
-    return lax.ppermute(x, axis, pairs)
+    return lax.ppermute(x, axis, [(i, (i + step) % n) for i in range(n)])
 
 
 def halo(top, bot, left, right):
-    return (
-        shift(top, "lat", 1, False),
-        shift(bot, "lat", -1, False),
-        shift(left, "lon", 1, True),
-        shift(right, "lon", -1, True),
-    )
+    left, right = shift(left, "lon", 1), shift(right, "lon", -1)
+    return shift(top, "lat", 1), shift(bot, "lat", -1), left, right
 
 
 def exchange(x):
@@ -730,17 +800,17 @@
     borders = halo(*sides)
     asked, x_in = lax.optimization_barrier((asked, x_t))
     y, xs = conv_core(x_in, conv_weight)
-    answer, gate = sample(y, xs, conv_weight, asked, *borders, cap)
+    answer, gate, spots = sample(y, xs, conv_weight, asked, *borders, cap)
     answer = exchange(answer)
     prepared = prepare(
         route, spot, neighbours.T, neighbour_count, edge_bias.T, live_count, observed, hidden_mask, w_in,
         regions, cap, tile, n_lon,
     )
-    predicted, outgoing = stations_pass(
+    predicted, outgoing, gates = stations_pass(
         live_count, answer, prepared, observed, hidden_mask, w_in, norm_gain, qkv_weight, out_weight,
-        final_gain, head_weight,
+        final_gain, head_weight, cap,
     )
-    d_field, d_pre, *sides, corners = spread(asked, exchange(outgoing), answer, gate, cap)
+    d_field, d_pre, *sides, corners = spread(spots, exchange(outgoing), gates, gate, cap)
     borders = halo(*sides)
     grad = conv_back(d_pre, conv_weight, d_field)
     return predicted, jnp.swapaxes(finish(grad, conv_weight, *borders, corners), 1, 2)

time: 92.6 us -> 86.3 us (0.932)
  starting transfers between devices: 28.5 us -> 23.2 us
  local copies, waits for them, and re-layouts: 3.75 us -> 0.01 us
  Pallas kernels: 39.6 us -> 41.6 us
    unnamed x10 -> x4, local copies, waits for them, and re-layouts: 3.75 us -> 0.01 us
    ppermute x8, starting transfers between devices: 16.2 us -> 13 us  [shift(): return lax.ppermute(x, axis, [(i, (i + step) % n) for i in range(n)])]
    all_to_all x2, starting transfers between devices: 12.2 us -> 10.1 us  [exchange(): return lax.all_to_all(x, AXES, split_axis=0, concat_axis=0, tiled=True)]
    pallas_call x5, Pallas kernels: 29.3 us -> 30.8 us  [the longest x1 7.6 us: conv_core(): pl.pallas_call(functools.partial(conv_core_kernel, parts), out_shape=(SDS...]
  transfers between devices with their start and end apart: 10 -> 10, of which waited for: 1 -> 2; matrix products, arithmetic and copies ran while one was open for 0% -> 0% of each run, Pallas kernels for 18% -> 20%
where the time goes in v3:
time: 86.3 us; the launch traced here: 85.8 us
  Pallas kernels  41.6 us (48%)
  starting transfers between devices  23.2 us (27%)
  blocking collectives  13.3 us (15%)
  waiting for transfers between devices  6.22 us (7%)
  between operations  1.58 us (2%)
    all_to_all x1, blocking collectives, exchange(): return lax.all_to_all(x, AXES, split_axis=0, concat_axis=0, tiled=True)  13.3 us
    ppermute x8, starting transfers between devices, shift(): return lax.ppermute(x, axis, [(i, (i + step) % n) for i in range(n)])  13 us
    all_to_all x2, starting transfers between devices, exchange(): return lax.all_to_all(x, AXES, split_axis=0, concat_axis=0, tiled=True)  10.1 us
    pallas_call x1, Pallas kernels, conv_core(): pl.pallas_call(functools.partial(conv_core_kernel, parts), out_shape=(SDS...  7.6 us
    pallas_call x1, Pallas kernels, stations_pass(): pl.pallas_call(functools.partial(station_kernel, cap), out_shape=outs, in...  7.34 us
    pallas_call x1, Pallas kernels, sample(): pl.pallas_call(functools.partial(sample_kernel, cap), out_shape=(pltpu.HB...  6.42 us
    all_to_all x2, waiting for transfers between devices, exchange(): return lax.all_to_all(x, AXES, split_axis=0, concat_axis=0, tiled=True)  6.19 us
    pallas_call x1, Pallas kernels, conv_back(): pl.pallas_call(conv_back_kernel, out_shape=SDS(add.shape, F32), in_specs=...  5.52 us
  transfers between devices with their start and end apart: 10, of which 2 were waited for; matrix products, arithmetic and copies ran while one was open for 0% of the time, Pallas kernels for 20%

profile of v3, /device:TPU:0, one launch (start us, length us, event | category | flops | bytes accessed | tf_op | source)
XLA Modules:
  0.0 85.8 jit_solution(70214124328425460)
XLA Ops:
  0.6 0.0 copy-start
  0.6 3.9 %intro.1 = (bf16[32,8,128]{2,1,0:T(8,128)(2,1)}, bf16[128,192]{1,0:T(8,128)(2,1)}, bf16[128,192]{1,0:T(8,128)(2,1)}, bf16[32,192]{1,0:T(8,128)(2,1)}, bf16[32,192]{1,0:T(8,128)(2,1)}) custom-call(s32[1,256]{1,0:T(1,128)} %bitcast.17, s32[1,256]{1,0:T(1,128)} %bitcast.19, bf16[32,192,128]{2,1,0:T(8,128)(2,1)} %bitcast.10), custom_call_target="tpu_custom_call" | custom-call | tf_op jit(solution)/shard_map/intro/pallas_call | solution.py:145
  4.6 7.3 %all-to-all-start = ((bf16[32,8,128]{2,1,0:T(8,128)(2,1)}), bf16[32,8,128]{2,1,0:T(8,128)(2,1)S(1)}, u32[]{:S(2)}, u32[]{:S(2)}) async-start(bf16[32,8,128]{2,1,0:T(8,128)(2,1)} %get-tuple-element.28), calls=%async_computation | async-start | bytes 131072 | tf_op jit(solution)/shard_map/all_to_all | solution.py:769
  11.9 1.8 %collective-permute-start = (bf16[128,192]{1,0:T(8,128)(2,1)}, bf16[128,192]{1,0:T(8,128)(2,1)S(1)}, u32[]{:S(2)}, u32[]{:S(2)}) collective-permute-start(bf16[128,192]{1,0:T(8,128)(2,1)} %get-tuple-element.33), channel_id=1, source_target_pairs={{0,8},{8,16},{16,24},{24,0},{1,9},{9,17},{17,25},{25,1},{2,10},{10... | collective-permute-start | bytes 147464 | tf_op jit(solution)/shard_map/ppermute | solution.py:760
  13.7 1.2 %collective-permute-start.1 = (bf16[128,192]{1,0:T(8,128)(2,1)}, bf16[128,192]{1,0:T(8,128)(2,1)S(1)}, u32[]{:S(2)}, u32[]{:S(2)}) collective-permute-start(bf16[128,192]{1,0:T(8,128)(2,1)} %get-tuple-element.34), channel_id=1, source_target_pairs={{0,24},{8,0},{16,8},{24,16},{1,25},{9,1},{17,9},{25,17},{2,26},{10... | collective-permute-start | bytes 147464 | tf_op jit(solution)/shard_map/ppermute | solution.py:760
  14.9 0.0 collective-permute-start.2
  14.9 3.5 %collective-permute-start.3 = (bf16[32,192]{1,0:T(8,128)(2,1)}, bf16[32,192]{1,0:T(8,128)(2,1)S(1)}, u32[]{:S(2)}, u32[]{:S(2)}) collective-permute-start(bf16[32,192]{1,0:T(8,128)(2,1)} %get-tuple-element.36), channel_id=1, source_target_pairs={{0,7},{1,0},{2,1},{3,2},{4,3},{5,4},{6,5},{7,6},{8,15},{9,8},{10,9... | collective-permute-start | bytes 36872 | tf_op jit(solution)/shard_map/ppermute | solution.py:760
  18.4 0.9 %all-to-all-done.asked_ref = bf16[32,8,128]{2,1,0:T(8,128)(2,1)S(1)} async-done(((bf16[32,8,128]{2,1,0:T(8,128)(2,1)}), bf16[32,8,128]{2,1,0:T(8,128)(2,1)S(1)}, u32[]{:S(2)}, u32[]{:S(2)}) %all-to-all-start) | async-done | bytes 65568 | tf_op jit(solution)/shard_map/all_to_all | solution.py:769
  19.3 0.0 copy-done
  19.3 7.6 %conv_core.1 = (f32[32,128,192]{2,1,0:T(8,128)S(1)}, bf16[34,128,256]{2,1,0:T(8,128)(2,1)S(1)}) custom-call(bf16[32,192,128]{2,1,0:T(8,128)(2,1)} %bitcast.11, bf16[9,192,192]{2,1,0:T(8,128)(2,1)S(1)} %copy-done), custom_call_target="tpu_custom_call" | custom-call | tf_op jit(solution)/shard_map/conv_core/pallas_call | solution.py:225
  26.9 0.0 collective-permute-done.2.left_ref
  26.9 0.0 collective-permute-done.3.right_ref
  26.9 0.0 collective-permute-done.top_ref
  26.9 0.0 collective-permute-done.1.bot_ref
  26.9 6.4 %sample.1 = (bf16[32,32,128]{2,1,0:T(8,128)(2,1)}, bf16[32,128,192]{2,1,0:T(8,128)(2,1)}, f32[32,128]{1,0:T(8,128)}) custom-call(f32[32,128,192]{2,1,0:T(8,128)S(1)} %get-tuple-element.30.y_ref, bf16[34,128,256]{2,1,0:T(8,128)(2,1)S(1)} %get-tuple-element.31.xs_ref, bf16[9,192,192]{2,1,0:T(8,128)(2,1)S(1)} %copy-done, ...), custom_call_target="tpu_custom_call" | custom-call | tf_op jit(solution)/shard_map/sample/pallas_call | solution.py:396
  33.4 2.8 %all-to-all-start.1 = ((bf16[32,32,128]{2,1,0:T(8,128)(2,1)}), bf16[32,32,128]{2,1,0:T(8,128)(2,1)S(1)}, u32[]{:S(2)}, u32[]{:S(2)}) async-start(bf16[32,32,128]{2,1,0:T(8,128)(2,1)} %get-tuple-element.37), calls=%async_computation.1 | async-start | bytes 524288 | tf_op jit(solution)/shard_map/all_to_all | solution.py:769
  36.2 0.0 copy-start.1
  37.0 3.7 %prepare.1 = (bf16[1024,768]{1,0:T(8,128)(2,1)}, f32[256,256]{1,0:T(8,128)}, f32[256,192]{1,0:T(8,128)}, f32[256,128]{1,0:T(8,128)}) custom-call(s32[1]{0:T(128)S(6)} %copy.18.live_ref, s32[1,256]{1,0:T(1,128)} %bitcast.18, s32[1,256]{1,0:T(1,128)} %bitcast.20, s32[16,256]{1,0:T(8,128)} %bitcast.15, s32[1,256]{1,0:T(1,128)} %bitcast.23, f32[16,256]{1,0:T(8,128)} %bitcast.16, ...), custom_call_target="tpu_custom_call" | custom-call | tf_op jit(solution)/shard_map/prepare/pallas_call | solution.py:634
  40.7 5.3 %all-to-all-done.1.ans_ref = bf16[32,32,128]{2,1,0:T(8,128)(2,1)S(1)} async-done(((bf16[32,32,128]{2,1,0:T(8,128)(2,1)}), bf16[32,32,128]{2,1,0:T(8,128)(2,1)S(1)}, u32[]{:S(2)}, u32[]{:S(2)}) %all-to-all-start.1) | async-done | bytes 262176 | tf_op jit(solution)/shard_map/all_to_all | solution.py:769
  46.0 7.3 %stations.1 = (f32[256,128]{1,0:T(8,128)}, bf16[32,32,128]{2,1,0:T(8,128)(2,1)}, f32[8,192]{1,0:T(8,128)}) custom-call(s32[1]{0:T(128)S(6)} %copy.18.live_ref, bf16[32,32,128]{2,1,0:T(8,128)(2,1)S(1)} %all-to-all-done.1.ans_ref, f32[256,128]{1,0:T(8,128)} %get-tuple-element.38.refs_0_, f32[256,192]{1,0:T(8,128)} %get-tuple-element.39.refs_1_, ...), custom_call_target="tpu_custom_call" | custom-call | tf_op jit(solution)/shard_map/stations/pallas_call | solution.py:741
  53.3 13.3 %all_to_all.15.inc_hbm = bf16[32,32,128]{2,1,0:T(8,128)(2,1)} all-to-all(bf16[32,32,128]{2,1,0:T(8,128)(2,1)} %get-tuple-element.44), channel_id=1, replica_groups=mesh['lat'=4,'lon'=8] {'lat','lon'}, dimensions={0} | all-to-all | bytes 524288 | tf_op jit(solution)/shard_map/all_to_all | solution.py:769
  66.6 0.0 copy-done.1
  66.6 3.8 %spread.1 = (f32[32,128,192]{2,1,0:T(8,128)S(1)}, bf16[34,128,256]{2,1,0:T(8,128)(2,1)S(1)}, bf16[128,192]{1,0:T(8,128)(2,1)S(1)}, bf16[128,192]{1,0:T(8,128)(2,...) custom-call(f32[32,128]{1,0:T(8,128)} %get-tuple-element.43.spots_hbm, ...), custom_call_target="tpu_custom_call" | custom-call | tf_op jit(solution)/shard_map/spread/pallas_call | solution.py:482
  70.4 0.9 %collective-permute-start.4 = (bf16[128,192]{1,0:T(8,128)(2,1)S(1)}, bf16[128,192]{1,0:T(8,128)(2,1)S(1)}, u32[]{:S(2)}, u32[]{:S(2)}) collective-permute-start(bf16[128,192]{1,0:T(8,128)(2,1)S(1)} %get-tuple-element.49), channel_id=1, source_target_pairs={{0,8},{8,16},{16,24},{24,0},{1,9},{9,17},{17,25},{25,1},{2,10},{10... | collective-permute-start | bytes 147464 | tf_op jit(solution)/shard_map/ppermute | solution.py:760
  71.3 2.1 %collective-permute-start.5 = (bf16[128,192]{1,0:T(8,128)(2,1)S(1)}, bf16[128,192]{1,0:T(8,128)(2,1)S(1)}, u32[]{:S(2)}, u32[]{:S(2)}) collective-permute-start(bf16[128,192]{1,0:T(8,128)(2,1)S(1)} %get-tuple-element.50), channel_id=1, source_target_pairs={{0,24},{8,0},{16,8},{24,16},{1,25},{9,1},{17,9},{25,17},{2,26},{10... | collective-permute-start | bytes 147464 | tf_op jit(solution)/shard_map/ppermute | solution.py:760
  73.4 0.2 collective-permute-start.6
  73.5 3.4 %collective-permute-start.7 = (bf16[32,192]{1,0:T(8,128)(2,1)S(1)}, bf16[32,192]{1,0:T(8,128)(2,1)S(1)}, u32[]{:S(2)}, u32[]{:S(2)}) collective-permute-start(bf16[32,192]{1,0:T(8,128)(2,1)S(1)} %get-tuple-element.52), channel_id=1, source_target_pairs={{0,7},{1,0},{2,1},{3,2},{4,3},{5,4},{6,5},{7,6},{8,15},{9,8},{10,9... | collective-permute-start | bytes 36872 | tf_op jit(solution)/shard_map/ppermute | solution.py:760
  76.9 5.5 %conv_back.1.g_ref = f32[32,128,192]{2,1,0:T(8,128)S(1)} custom-call(bf16[34,128,256]{2,1,0:T(8,128)(2,1)S(1)} %get-tuple-element.47.xs_ref, bf16[9,192,192]{2,1,0:T(8,128)(2,1)S(1)} %copy-done, f32[32,128,192]{2,1,0:T(8,128)S(1)} %get-tuple-element.48.add_ref), custom_call_target="tpu_custom_call" | custom-call | tf_op jit(solution)/shard_map/conv_back/pallas_call | solution.py:242
  82.5 0.0 collective-permute-done.6.left_ref
  82.5 0.0 collective-permute-done.7.right_ref
  82.5 0.0 collective-permute-done.4.top_ref
  82.5 0.0 collective-permute-done.5.bot_ref
  82.5 3.3 %finish.1 = f32[32,192,128]{2,1,0:T(8,128)} custom-call(f32[32,128,192]{2,1,0:T(8,128)S(1)} %conv_back.1.g_ref, bf16[9,192,192]{2,1,0:T(8,128)(2,1)S(1)} %copy-done, bf16[128,192]{1,0:T(8,128)(2,1)S(1)} %collective-permute-done.4.top_ref, bf16[128,192]{1,0:T(8,128)(2,1)S(1)} %collective-permute-done.5.bot_ref, ...), custom_call_target="tpu_custom_call" | custom-call | tf_op jit(solution)/shard_map/finish/pallas_call | solution.py:533
Async XLA Ops:
  0.6 18.7 %copy-start = (bf16[9,192,192]{2,1,0:T(8,128)(2,1)S(1)}, bf16[9,192,192]{2,1,0:T(8,128)(2,1)}, u32[]{:S(2)}) copy-start(bf16[9,192,192]{2,1,0:T(8,128)(2,1)} %w_ref.7) | copy-start | bytes 1990660
  4.6 14.7 %all-to-all-start = ((bf16[32,8,128]{2,1,0:T(8,128)(2,1)}), bf16[32,8,128]{2,1,0:T(8,128)(2,1)S(1)}, u32[]{:S(2)}, u32[]{:S(2)}) async-start(bf16[32,8,128]{2,1,0:T(8,128)(2,1)} %get-tuple-element.28), calls=%async_computation | async-start | bytes 131072 | tf_op jit(solution)/shard_map/all_to_all | solution.py:769
  11.9 15.0 %collective-permute-start = (bf16[128,192]{1,0:T(8,128)(2,1)}, bf16[128,192]{1,0:T(8,128)(2,1)S(1)}, u32[]{:S(2)}, u32[]{:S(2)}) collective-permute-start(bf16[128,192]{1,0:T(8,128)(2,1)} %get-tuple-element.33), channel_id=1, source_target_pairs={{0,8},{8,16},{16,24},{24,0},{1,9},{9,17},{17,25},{25,1},{2,10},{10... | collective-permute-start | bytes 147464 | tf_op jit(solution)/shard_map/ppermute | solution.py:760
  13.7 13.2 %collective-permute-start.1 = (bf16[128,192]{1,0:T(8,128)(2,1)}, bf16[128,192]{1,0:T(8,128)(2,1)S(1)}, u32[]{:S(2)}, u32[]{:S(2)}) collective-permute-start(bf16[128,192]{1,0:T(8,128)(2,1)} %get-tuple-element.34), channel_id=1, source_target_pairs={{0,24},{8,0},{16,8},{24,16},{1,25},{9,1},{17,9},{25,17},{2,26},{10... | collective-permute-start | bytes 147464 | tf_op jit(solution)/shard_map/ppermute | solution.py:760
  14.9 12.0 %collective-permute-start.2 = (bf16[32,192]{1,0:T(8,128)(2,1)}, bf16[32,192]{1,0:T(8,128)(2,1)S(1)}, u32[]{:S(2)}, u32[]{:S(2)}) collective-permute-start(bf16[32,192]{1,0:T(8,128)(2,1)} %get-tuple-element.35), channel_id=1, source_target_pairs={{0,1},{1,2},{2,3},{3,4},{4,5},{5,6},{6,7},{7,0},{8,9},{9,10},{10,1... | collective-permute-start | bytes 36872 | tf_op jit(solution)/shard_map/ppermute | solution.py:760
  14.9 12.0 %collective-permute-start.3 = (bf16[32,192]{1,0:T(8,128)(2,1)}, bf16[32,192]{1,0:T(8,128)(2,1)S(1)}, u32[]{:S(2)}, u32[]{:S(2)}) collective-permute-start(bf16[32,192]{1,0:T(8,128)(2,1)} %get-tuple-element.36), channel_id=1, source_target_pairs={{0,7},{1,0},{2,1},{3,2},{4,3},{5,4},{6,5},{7,6},{8,15},{9,8},{10,9... | collective-permute-start | bytes 36872 | tf_op jit(solution)/shard_map/ppermute | solution.py:760
  33.4 12.6 %all-to-all-start.1 = ((bf16[32,32,128]{2,1,0:T(8,128)(2,1)}), bf16[32,32,128]{2,1,0:T(8,128)(2,1)S(1)}, u32[]{:S(2)}, u32[]{:S(2)}) async-start(bf16[32,32,128]{2,1,0:T(8,128)(2,1)} %get-tuple-element.37), calls=%async_computation.1 | async-start | bytes 524288 | tf_op jit(solution)/shard_map/all_to_all | solution.py:769
  36.2 30.5 %copy-start.1 = (bf16[32,128,192]{2,1,0:T(8,128)(2,1)S(1)}, bf16[32,128,192]{2,1,0:T(8,128)(2,1)}, u32[]{:S(2)}) copy-start(bf16[32,128,192]{2,1,0:T(8,128)(2,1)} %get-tuple-element.46.gate_ref) | copy-start | bytes 4718596
  70.4 12.1 %collective-permute-start.4 = (bf16[128,192]{1,0:T(8,128)(2,1)S(1)}, bf16[128,192]{1,0:T(8,128)(2,1)S(1)}, u32[]{:S(2)}, u32[]{:S(2)}) collective-permute-start(bf16[128,192]{1,0:T(8,128)(2,1)S(1)} %get-tuple-element.49), channel_id=1, source_target_pairs={{0,8},{8,16},{16,24},{24,0},{1,9},{9,17},{17,25},{25,1},{2,10},{10... | collective-permute-start | bytes 147464 | tf_op jit(solution)/shard_map/ppermute | solution.py:760
  71.3 11.2 %collective-permute-start.5 = (bf16[128,192]{1,0:T(8,128)(2,1)S(1)}, bf16[128,192]{1,0:T(8,128)(2,1)S(1)}, u32[]{:S(2)}, u32[]{:S(2)}) collective-permute-start(bf16[128,192]{1,0:T(8,128)(2,1)S(1)} %get-tuple-element.50), channel_id=1, source_target_pairs={{0,24},{8,0},{16,8},{24,16},{1,25},{9,1},{17,9},{25,17},{2,26},{10... | collective-permute-start | bytes 147464 | tf_op jit(solution)/shard_map/ppermute | solution.py:760
  73.4 9.1 %collective-permute-start.6 = (bf16[32,192]{1,0:T(8,128)(2,1)S(1)}, bf16[32,192]{1,0:T(8,128)(2,1)S(1)}, u32[]{:S(2)}, u32[]{:S(2)}) collective-permute-start(bf16[32,192]{1,0:T(8,128)(2,1)S(1)} %get-tuple-element.51), channel_id=1, source_target_pairs={{0,1},{1,2},{2,3},{3,4},{4,5},{5,6},{6,7},{7,0},{8,9},{9,10},{10,1... | collective-permute-start | bytes 36872 | tf_op jit(solution)/shard_map/ppermute | solution.py:760
  73.5 8.9 %collective-permute-start.7 = (bf16[32,192]{1,0:T(8,128)(2,1)S(1)}, bf16[32,192]{1,0:T(8,128)(2,1)S(1)}, u32[]{:S(2)}, u32[]{:S(2)}) collective-permute-start(bf16[32,192]{1,0:T(8,128)(2,1)S(1)} %get-tuple-element.52), channel_id=1, source_target_pairs={{0,7},{1,0},{2,1},{3,2},{4,3},{5,4},{6,5},{7,6},{8,15},{9,8},{10,9... | collective-permute-start | bytes 36872 | tf_op jit(solution)/shard_map/ppermute | solution.py:760

commit v4 on v3

--- a/solution.py
+++ b/solution.py
@@ -109,12 +109,19 @@
     return rank_col, rank_row, route_col
 
 
-def intro_kernel(route_ref, spot_ref, x_hbm, slab_ref, top_ref, bot_ref, left_ref, right_ref, x_ref, slab, sem):
+def intro_kernel(
+    route_hbm, spot_hbm, x_hbm, slab_ref, top_ref, bot_ref, left_ref, right_ref, route_ref, spot_ref, x_ref, slab,
+    sem,
+):
     rows, ch, cols = x_ref.shape
-    fetch = pltpu.make_async_copy(x_hbm, x_ref, sem)
-    fetch.start()
+    pairs = ((route_hbm, route_ref), (spot_hbm, spot_ref), (x_hbm, x_ref))
+    fetches = [pltpu.make_async_copy(a, b, sem.at[k]) for k, (a, b) in enumerate(pairs)]
+    for fetch in fetches:
+        fetch.start()
     regions = slab_ref.shape[0]
     stations = route_ref.shape[1]
+    fetches[0].wait()
+    fetches[1].wait()
     rank_col, _, _ = route_parts(route_ref[...], up(regions, 128))
     spot = spot_ref[...].astype(F32)
     high = jnp.floor(spot * (1.0 / 256.0))
@@ -123,7 +130,7 @@
     ranked = onehot(rank_col == iota_f((stations, 128), 1))
     slab[:, 0, :] = nn(jnp.where(member, high, 0.0).astype(BF16), ranked)
     slab[:, 1, :] = nn(jnp.where(member, low, 0.0).astype(BF16), ranked)
-    fetch.wait()
+    fetches[2].wait()
     eye = onehot(iota((cols, cols), 0) == iota((cols, cols), 1))
     row, lane = iota((16, cols), 0), iota((16, cols), 1)
     ends = onehot(((row == 0) & (lane == 0)) | ((row == 1) & (lane == cols - 1)))
@@ -151,47 +158,57 @@
             SDS((rows, ch), BF16),
             SDS((rows, ch), BF16),
         ),
-        in_specs=whole(2) + in_hbm(1),
+        in_specs=in_hbm(3),
         out_specs=tuple(whole(5)),
-        scratch_shapes=[VMEM(x_t.shape, BF16), VMEM((regions, 8, 128), F32), pltpu.SemaphoreType.DMA],
+        scratch_shapes=[
+            VMEM(route.shape, jnp.int32),
+            VMEM(spot.shape, jnp.int32),
+            VMEM(x_t.shape, BF16),
+            VMEM((regions, 8, 128), F32),
+            pltpu.SemaphoreType.DMA((3,)),
+        ],
         name="intro",
-    )(route, spot, hbm(x_t))
+    )(hbm(route), hbm(spot), hbm(x_t))
 
 
 def conv_weights(w_ref, wc, back):
     ch = w_ref.shape[1]
-    deep = up(ch, 128)
     wc[...] = jnp.zeros_like(wc)
-    for dy in range(3):
-        for dx in range(3):
+    for dx in range(3):
+        g = [(w_ref[8 - (3 * dy + dx)] if back else w_ref[3 * dy + dx]).astype(F32) for dy in range(3)]
+        ends = g[0] + g[2]
+        for i, u in enumerate((g[0], 0.5 * (ends + g[1]), 0.5 * (ends - g[1]), g[2])):
             if back:
-                wc[dx, :, dy * deep : dy * deep + ch] = w_ref[8 - (3 * dy + dx)]
+                wc[4 * dx + i, :, :ch] = u.astype(BF16)
             else:
-                wc[dx, dy * deep : dy * deep + ch, :] = w_ref[3 * dy + dx]
-
-
-def conv_blocks(back, block, xs_ref, wc, add_ref, o_ref):
+                wc[4 * dx + i, :ch, :] = u.astype(BF16)
+
+
+def conv_blocks(back, pairs, xs_ref, wc, add_ref, o_ref):
     rows, cols, ch = o_ref.shape
-    deep = xs_ref.shape[2]
     dot = nt if back else nn
-    col = iota((block * cols, ch), 0) % cols
+    count = pairs * cols
+    col = iota((count, ch), 0) % cols
     first, last = col == 0, col == cols - 1
-
-    def body(i, carry):
-        r0 = i * block
-        lhs = jnp.concatenate(
-            [xs_ref[pl.ds(r0 + dy, block)].reshape(block * cols, deep) for dy in range(3)], axis=1
-        )
-        total = dot(lhs, wc[1])
-        total = total + jnp.where(first, 0.0, pltpu.roll(dot(lhs, wc[0]), 1, 0))
-        total = total + jnp.where(last, 0.0, pltpu.roll(dot(lhs, wc[2]), block * cols - 1, 0))
-        total = total.reshape(block, cols, ch)
-        if back:
-            total = total + add_ref[pl.ds(r0, block)]
-        o_ref[pl.ds(r0, block)] = total
-        return carry
-
-    lax.fori_loop(0, rows // block, body, 0)
+    for base in range(0, rows, 2 * pairs):
+        d0, d1, d2, d3 = [
+            jnp.concatenate([xs_ref[base + 2 * p + k] for p in range(pairs)], axis=0) for k in range(4)
+        ]
+        seen = (d0 - d2, d1 + d2, d2 - d1, d1 - d3)
+        upper = lower = None
+        for dx in (1, 0, 2):
+            m1, m2, m3, m4 = [dot(v, wc[4 * dx + i]) for i, v in enumerate(seen)]
+            a, c = m1 + m2 + m3, m2 - m3 - m4
+            if dx == 0:
+                a, c = [jnp.where(first, 0.0, pltpu.roll(t, 1, 0)) for t in (a, c)]
+            if dx == 2:
+                a, c = [jnp.where(last, 0.0, pltpu.roll(t, count - 1, 0)) for t in (a, c)]
+            upper, lower = (a, c) if upper is None else (upper + a, lower + c)
+        for p in range(pairs):
+            for k, t in enumerate((upper, lower)):
+                r = base + 2 * p + k
+                line = t[p * cols : (p + 1) * cols]
+                o_ref[r] = line + add_ref[r] if back else line
 
 
 def conv_core_kernel(parts, x_hbm, w_ref, o_ref, xs_ref, wc, x_ref, sem):
@@ -211,12 +228,12 @@
         if r % size == 0:
             fetches[r // size].wait()
         xs_ref[r + 1] = jnp.concatenate([nt(eye, x_ref[r]).astype(BF16), pad], axis=1)
-    conv_blocks(False, rows, xs_ref, wc, None, o_ref)
+    conv_blocks(False, rows // 4, xs_ref, wc, None, o_ref)
 
 
 def conv_back_kernel(xs_ref, w_ref, add_ref, o_ref, wc):
     conv_weights(w_ref, wc, True)
-    conv_blocks(True, o_ref.shape[0], xs_ref, wc, add_ref, o_ref)
+    conv_blocks(True, o_ref.shape[0] // 4, xs_ref, wc, add_ref, o_ref)
 
 
 def conv_core(x_t, taps, parts=4):
@@ -228,7 +245,7 @@
         in_specs=in_hbm(1) + whole(1),
         out_specs=tuple(whole(2)),
         scratch_shapes=[
-            VMEM((3, 3 * deep, ch), BF16),
+            VMEM((12, deep, ch), BF16),
             VMEM(x_t.shape, BF16),
             pltpu.SemaphoreType.DMA((parts,)),
         ],
@@ -244,7 +261,7 @@
         out_shape=SDS(add.shape, F32),
         in_specs=whole(3),
         out_specs=whole(1)[0],
-        scratch_shapes=[VMEM((3, ch, 3 * xs.shape[2]), BF16)],
+        scratch_shapes=[VMEM((12, ch, xs.shape[2]), BF16)],
         compiler_params=PARAMS,
         name="conv_back",
     )(xs, taps, add)
@@ -343,7 +360,7 @@
 
     def gates(r, pre):
         pre = add_sides(pre, fix, r)
-        sg = 1.0 / (1.0 + jnp.exp(-pre))
+        sg = 0.5 * jnp.tanh(0.5 * pre) + 0.5
         field[pl.ds(r * cols, cols), :] = (xs_ref[r + 1, :, :ch].astype(F32) + pre * sg).astype(BF16)
         gate_ref[r] = (sg * (1.0 + pre * (1.0 - sg))).astype(BF16)
 
@@ -363,12 +380,12 @@
     spots_out.start()
     spot = spots_column(spots_ref[...], slots)
     r, c, a, b = fine_cell(spot, cols)
-    by_row = hat(iota_f((slots, rows), 1), r, a)
-    by_col = hat(iota_f((slots, cols), 1), c, b)
+    by_row = hat(iota_f((slots, rows), 1), r, a).astype(BF16)
+    by_col = hat(iota_f((slots, cols), 1), c, b).astype(BF16)
     total = jnp.zeros((slots, ch), F32)
     for pair in range(0, rows, 2):
         weights = jnp.concatenate(
-            [(by_row[:, pair + k : pair + k + 1] * by_col).astype(BF16) for k in range(2)], axis=1
+            [by_row[:, pair + k : pair + k + 1] * by_col for k in range(2)], axis=1
         )
         total = total + nn(weights, field[pair * cols : (pair + 2) * cols, :])
     pack[...] = jnp.zeros_like(pack)
@@ -436,7 +453,7 @@
     spot = spots_row(spots_ref[...], slots)
     r, c, a, b = fine_cell(spot, cols)
     by_row[...] = hat(iota_f((rows, slots), 0), r, a)
-    by_col = hat(iota_f((cols, slots), 0), c, b)
+    by_col = hat(iota_f((cols, slots), 0), c, b).astype(BF16)
     fetches[1].wait()
     sums = jnp.zeros((inc_ref.shape[1], 128), F32)
     for t in range(regions):
@@ -454,7 +471,7 @@
     def body(i, carry):
         r0 = i * block
         weights = jnp.concatenate(
-            [(by_row[pl.ds(r0 + k, 1)] * by_col).astype(BF16) for k in range(block)], axis=0
+            [by_row[pl.ds(r0 + k, 1)].astype(BF16) * by_col for k in range(block)], axis=0
         )
         d_field = nn(weights, incoming).reshape(block, cols, ch)
         df_ref[pl.ds(r0, block)] = d_field
@@ -506,37 +523,43 @@
     )(hbm(spots), hbm(incoming), hbm(gates), gate)
 
 
-def finish_kernel(g_ref, w_ref, top_ref, bot_ref, left_ref, right_ref, corner_ref, o_ref, fix, edge):
-    block, cols, ch = g_ref.shape
-    step = pl.program_id(0)
-    steps = pl.num_programs(0)
-
-    @pl.when(step == 0)
-    def _():
-        corners = corner_ref[...]
-        edge[0] = inside(-1) * border_rows(top_ref[...], w_ref, 0, True)
-        edge[1] = inside(1) * border_rows(bot_ref[...], w_ref, 2, True)
-        fix[0] = border_cols(left_ref[...], (corners[0:1], corners[2:3]), w_ref, 0, True)
-        fix[1] = border_cols(right_ref[...], (corners[1:2], corners[3:4]), w_ref, 2, True)
-
-    for k in range(block):
-        out = add_sides(g_ref[k], fix, step * block + k)
-        if k == 0:
-            out = out + jnp.where(step == 0, edge[0], 0.0)
-        if k == block - 1:
-            out = out + jnp.where(step == steps - 1, edge[1], 0.0)
-        o_ref[k] = out.T
-
-
-def finish(grad, taps, top, bot, left, right, corners, block=8):
+def finish_kernel(parts, g_ref, w_ref, top_ref, bot_ref, left_ref, right_ref, corner_ref, o_hbm, fix, o_ref, sem):
+    rows, cols, ch = g_ref.shape
+    corners = corner_ref[...]
+    above = inside(-1) * border_rows(top_ref[...], w_ref, 0, True)
+    below = inside(1) * border_rows(bot_ref[...], w_ref, 2, True)
+    fix[0] = border_cols(left_ref[...], (corners[0:1], corners[2:3]), w_ref, 0, True)
+    fix[1] = border_cols(right_ref[...], (corners[1:2], corners[3:4]), w_ref, 2, True)
+    size = rows // parts
+    stores = []
+    for r in range(rows):
+        out = g_ref[r]
+        if r == 0:
+            out = out + above
+        if r == rows - 1:
+            out = out + below
+        o_ref[r] = add_sides(out, fix, r).T
+        if (r + 1) % size == 0:
+            k = r // size
+            at = pl.ds(k * size, size)
+            stores.append(pltpu.make_async_copy(o_ref.at[at], o_hbm.at[at], sem.at[k]))
+            stores[-1].start()
+    for store in stores:
+        store.wait()
+
+
+def finish(grad, taps, top, bot, left, right, corners, parts=8):
     rows, cols, ch = grad.shape
     return pl.pallas_call(
-        finish_kernel,
-        grid=(rows // block,),
-        out_shape=SDS((rows, ch, cols), F32),
-        in_specs=[pl.BlockSpec((block, cols, ch), lambda i: (i, 0, 0))] + whole(6),
-        out_specs=pl.BlockSpec((block, ch, cols), lambda i: (i, 0, 0)),
-        scratch_shapes=[VMEM((2, rows, ch), F32), VMEM((2, cols, ch), F32)],
+        functools.partial(finish_kernel, parts),
+        out_shape=pltpu.HBM((rows, ch, cols), F32),
+        in_specs=whole(7),
+        out_specs=in_hbm(1)[0],
+        scratch_shapes=[
+            VMEM((2, rows, ch), F32),
+            VMEM((rows, ch, cols), F32),
+            pltpu.SemaphoreType.DMA((parts,)),
+        ],
         compiler_params=PARAMS,
         name="finish",
     )(grad, taps, top, bot, left, right, corners)

time: 86.3 us -> 82.1 us (0.951)
  Pallas kernels: 41.6 us -> 37.2 us
    pallas_call x1, Pallas kernels: 7.6 us -> 6.52 us  [conv_core(): pl.pallas_call(functools.partial(conv_core_kernel, parts), out_shape=(SDS...]
    pallas_call x1, Pallas kernels: 3.34 us -> 2.44 us  [finish(): pl.pallas_call(functools.partial(finish_kernel, parts), out_shape=pltpu.H...]
    pallas_call x1, Pallas kernels: 5.52 us -> 4.64 us  [conv_back(): pl.pallas_call(conv_back_kernel, out_shape=SDS(add.shape, F32), in_specs=...]
  transfers between devices with their start and end apart: 10 -> 10, of which waited for: 2 -> 2; matrix products, arithmetic and copies ran while one was open for 0% -> 0% of each run, Pallas kernels for 20% -> 18%
where the time goes in v4:
time: 82.1 us; the launch traced here: 81.7 us
  Pallas kernels  37.2 us (45%)
  starting transfers between devices  23.2 us (28%)
  blocking collectives  13.3 us (16%)
  waiting for transfers between devices  6.22 us (8%)
  between operations  1.74 us (2%)
    all_to_all x1, blocking collectives, exchange(): return lax.all_to_all(x, AXES, split_axis=0, concat_axis=0, tiled=True)  13.3 us
    ppermute x8, starting transfers between devices, shift(): return lax.ppermute(x, axis, [(i, (i + step) % n) for i in range(n)])  13 us
    all_to_all x2, starting transfers between devices, exchange(): return lax.all_to_all(x, AXES, split_axis=0, concat_axis=0, tiled=True)  10.1 us
    pallas_call x1, Pallas kernels, stations_pass(): pl.pallas_call(functools.partial(station_kernel, cap), out_shape=outs, in...  7.34 us
    pallas_call x1, Pallas kernels, conv_core(): pl.pallas_call(functools.partial(conv_core_kernel, parts), out_shape=(SDS...  6.52 us
    all_to_all x2, waiting for transfers between devices, exchange(): return lax.all_to_all(x, AXES, split_axis=0, concat_axis=0, tiled=True)  6.19 us
    pallas_call x1, Pallas kernels, sample(): pl.pallas_call(functools.partial(sample_kernel, cap), out_shape=(pltpu.HB...  5.66 us
    pallas_call x1, Pallas kernels, conv_back(): pl.pallas_call(conv_back_kernel, out_shape=SDS(add.shape, F32), in_specs=...  4.64 us
  transfers between devices with their start and end apart: 10, of which 2 were waited for; matrix products, arithmetic and copies ran while one was open for 0% of the time, Pallas kernels for 18%

profile of v4, /device:TPU:0, one launch (start us, length us, event | category | flops | bytes accessed | tf_op | source)
XLA Modules:
  0.0 81.7 jit_solution(9251456967969578635)
XLA Ops:
  0.6 0.0 copy-start
  0.6 3.3 %intro.1 = (bf16[32,8,128]{2,1,0:T(8,128)(2,1)}, bf16[128,192]{1,0:T(8,128)(2,1)}, bf16[128,192]{1,0:T(8,128)(2,1)}, bf16[32,192]{1,0:T(8,128)(2,1)}, bf16[32,192]{1,0:T(8,128)(2,1)}) custom-call(s32[1,256]{1,0:T(1,128)} %bitcast.17, s32[1,256]{1,0:T(1,128)} %bitcast.19, bf16[32,192,128]{2,1,0:T(8,128)(2,1)} %bitcast.10), custom_call_target="tpu_custom_call" | custom-call | tf_op jit(solution)/shard_map/intro/pallas_call | solution.py:152
  3.9 7.3 %all-to-all-start = ((bf16[32,8,128]{2,1,0:T(8,128)(2,1)}), bf16[32,8,128]{2,1,0:T(8,128)(2,1)S(1)}, u32[]{:S(2)}, u32[]{:S(2)}) async-start(bf16[32,8,128]{2,1,0:T(8,128)(2,1)} %get-tuple-element.28), calls=%async_computation | async-start | bytes 131072 | tf_op jit(solution)/shard_map/all_to_all | solution.py:792
  11.3 1.8 %collective-permute-start = (bf16[128,192]{1,0:T(8,128)(2,1)}, bf16[128,192]{1,0:T(8,128)(2,1)S(1)}, u32[]{:S(2)}, u32[]{:S(2)}) collective-permute-start(bf16[128,192]{1,0:T(8,128)(2,1)} %get-tuple-element.33), channel_id=1, source_target_pairs={{0,8},{8,16},{16,24},{24,0},{1,9},{9,17},{17,25},{25,1},{2,10},{10... | collective-permute-start | bytes 147464 | tf_op jit(solution)/shard_map/ppermute | solution.py:783
  13.1 1.2 %collective-permute-start.1 = (bf16[128,192]{1,0:T(8,128)(2,1)}, bf16[128,192]{1,0:T(8,128)(2,1)S(1)}, u32[]{:S(2)}, u32[]{:S(2)}) collective-permute-start(bf16[128,192]{1,0:T(8,128)(2,1)} %get-tuple-element.34), channel_id=1, source_target_pairs={{0,24},{8,0},{16,8},{24,16},{1,25},{9,1},{17,9},{25,17},{2,26},{10... | collective-permute-start | bytes 147464 | tf_op jit(solution)/shard_map/ppermute | solution.py:783
  14.2 0.0 collective-permute-start.2
  14.2 3.5 %collective-permute-start.3 = (bf16[32,192]{1,0:T(8,128)(2,1)}, bf16[32,192]{1,0:T(8,128)(2,1)S(1)}, u32[]{:S(2)}, u32[]{:S(2)}) collective-permute-start(bf16[32,192]{1,0:T(8,128)(2,1)} %get-tuple-element.36), channel_id=1, source_target_pairs={{0,7},{1,0},{2,1},{3,2},{4,3},{5,4},{6,5},{7,6},{8,15},{9,8},{10,9... | collective-permute-start | bytes 36872 | tf_op jit(solution)/shard_map/ppermute | solution.py:783
  17.8 0.9 %all-to-all-done.asked_ref = bf16[32,8,128]{2,1,0:T(8,128)(2,1)S(1)} async-done(((bf16[32,8,128]{2,1,0:T(8,128)(2,1)}), bf16[32,8,128]{2,1,0:T(8,128)(2,1)S(1)}, u32[]{:S(2)}, u32[]{:S(2)}) %all-to-all-start) | async-done | bytes 65568 | tf_op jit(solution)/shard_map/all_to_all | solution.py:792
  18.6 0.0 copy-done
  18.6 6.5 %conv_core.1 = (f32[32,128,192]{2,1,0:T(8,128)S(1)}, bf16[34,128,256]{2,1,0:T(8,128)(2,1)S(1)}) custom-call(bf16[32,192,128]{2,1,0:T(8,128)(2,1)} %bitcast.11, bf16[9,192,192]{2,1,0:T(8,128)(2,1)S(1)} %copy-done), custom_call_target="tpu_custom_call" | custom-call | tf_op jit(solution)/shard_map/conv_core/pallas_call | solution.py:242
  25.2 0.0 collective-permute-done.2.left_ref
  25.2 0.0 collective-permute-done.3.right_ref
  25.2 0.0 collective-permute-done.top_ref
  25.2 0.0 collective-permute-done.1.bot_ref
  25.2 5.7 %sample.1 = (bf16[32,32,128]{2,1,0:T(8,128)(2,1)}, bf16[32,128,192]{2,1,0:T(8,128)(2,1)}, f32[32,128]{1,0:T(8,128)}) custom-call(f32[32,128,192]{2,1,0:T(8,128)S(1)} %get-tuple-element.30.y_ref, bf16[34,128,256]{2,1,0:T(8,128)(2,1)S(1)} %get-tuple-element.31.xs_ref, bf16[9,192,192]{2,1,0:T(8,128)(2,1)S(1)} %copy-done, ...), custom_call_target="tpu_custom_call" | custom-call | tf_op jit(solution)/shard_map/sample/pallas_call | solution.py:413
  30.9 2.8 %all-to-all-start.1 = ((bf16[32,32,128]{2,1,0:T(8,128)(2,1)}), bf16[32,32,128]{2,1,0:T(8,128)(2,1)S(1)}, u32[]{:S(2)}, u32[]{:S(2)}) async-start(bf16[32,32,128]{2,1,0:T(8,128)(2,1)} %get-tuple-element.37), calls=%async_computation.1 | async-start | bytes 524288 | tf_op jit(solution)/shard_map/all_to_all | solution.py:792
  33.7 0.0 copy-start.1
  34.5 3.7 %prepare.1 = (bf16[1024,768]{1,0:T(8,128)(2,1)}, f32[256,256]{1,0:T(8,128)}, f32[256,192]{1,0:T(8,128)}, f32[256,128]{1,0:T(8,128)}) custom-call(s32[1]{0:T(128)S(6)} %copy.18.live_ref, s32[1,256]{1,0:T(1,128)} %bitcast.18, s32[1,256]{1,0:T(1,128)} %bitcast.20, s32[16,256]{1,0:T(8,128)} %bitcast.15, s32[1,256]{1,0:T(1,128)} %bitcast.23, f32[16,256]{1,0:T(8,128)} %bitcast.16, ...), custom_call_target="tpu_custom_call" | custom-call | tf_op jit(solution)/shard_map/prepare/pallas_call | solution.py:657
  38.2 5.3 %all-to-all-done.1.ans_ref = bf16[32,32,128]{2,1,0:T(8,128)(2,1)S(1)} async-done(((bf16[32,32,128]{2,1,0:T(8,128)(2,1)}), bf16[32,32,128]{2,1,0:T(8,128)(2,1)S(1)}, u32[]{:S(2)}, u32[]{:S(2)}) %all-to-all-start.1) | async-done | bytes 262176 | tf_op jit(solution)/shard_map/all_to_all | solution.py:792
  43.5 7.3 %stations.1 = (f32[256,128]{1,0:T(8,128)}, bf16[32,32,128]{2,1,0:T(8,128)(2,1)}, f32[8,192]{1,0:T(8,128)}) custom-call(s32[1]{0:T(128)S(6)} %copy.18.live_ref, bf16[32,32,128]{2,1,0:T(8,128)(2,1)S(1)} %all-to-all-done.1.ans_ref, f32[256,128]{1,0:T(8,128)} %get-tuple-element.38.refs_0_, f32[256,192]{1,0:T(8,128)} %get-tuple-element.39.refs_1_, ...), custom_call_target="tpu_custom_call" | custom-call | tf_op jit(solution)/shard_map/stations/pallas_call | solution.py:764
  50.8 13.3 %all_to_all.15.inc_hbm = bf16[32,32,128]{2,1,0:T(8,128)(2,1)} all-to-all(bf16[32,32,128]{2,1,0:T(8,128)(2,1)} %get-tuple-element.44), channel_id=1, replica_groups=mesh['lat'=4,'lon'=8] {'lat','lon'}, dimensions={0} | all-to-all | bytes 524288 | tf_op jit(solution)/shard_map/all_to_all | solution.py:792
  64.1 0.0 copy-done.1
  64.1 3.7 %spread.1 = (f32[32,128,192]{2,1,0:T(8,128)S(1)}, bf16[34,128,256]{2,1,0:T(8,128)(2,1)S(1)}, bf16[128,192]{1,0:T(8,128)(2,1)S(1)}, bf16[128,192]{1,0:T(8,128)(2,...) custom-call(f32[32,128]{1,0:T(8,128)} %get-tuple-element.43.spots_hbm, ...), custom_call_target="tpu_custom_call" | custom-call | tf_op jit(solution)/shard_map/spread/pallas_call | solution.py:499
  67.8 0.9 %collective-permute-start.4 = (bf16[128,192]{1,0:T(8,128)(2,1)S(1)}, bf16[128,192]{1,0:T(8,128)(2,1)S(1)}, u32[]{:S(2)}, u32[]{:S(2)}) collective-permute-start(bf16[128,192]{1,0:T(8,128)(2,1)S(1)} %get-tuple-element.49), channel_id=1, source_target_pairs={{0,8},{8,16},{16,24},{24,0},{1,9},{9,17},{17,25},{25,1},{2,10},{10... | collective-permute-start | bytes 147464 | tf_op jit(solution)/shard_map/ppermute | solution.py:783
  68.7 2.1 %collective-permute-start.5 = (bf16[128,192]{1,0:T(8,128)(2,1)S(1)}, bf16[128,192]{1,0:T(8,128)(2,1)S(1)}, u32[]{:S(2)}, u32[]{:S(2)}) collective-permute-start(bf16[128,192]{1,0:T(8,128)(2,1)S(1)} %get-tuple-element.50), channel_id=1, source_target_pairs={{0,24},{8,0},{16,8},{24,16},{1,25},{9,1},{17,9},{25,17},{2,26},{10... | collective-permute-start | bytes 147464 | tf_op jit(solution)/shard_map/ppermute | solution.py:783
  70.8 0.2 collective-permute-start.6
  71.0 3.4 %collective-permute-start.7 = (bf16[32,192]{1,0:T(8,128)(2,1)S(1)}, bf16[32,192]{1,0:T(8,128)(2,1)S(1)}, u32[]{:S(2)}, u32[]{:S(2)}) collective-permute-start(bf16[32,192]{1,0:T(8,128)(2,1)S(1)} %get-tuple-element.52), channel_id=1, source_target_pairs={{0,7},{1,0},{2,1},{3,2},{4,3},{5,4},{6,5},{7,6},{8,15},{9,8},{10,9... | collective-permute-start | bytes 36872 | tf_op jit(solution)/shard_map/ppermute | solution.py:783
  74.4 4.6 %conv_back.1.g_ref = f32[32,128,192]{2,1,0:T(8,128)S(1)} custom-call(bf16[34,128,256]{2,1,0:T(8,128)(2,1)S(1)} %get-tuple-element.47.xs_ref, bf16[9,192,192]{2,1,0:T(8,128)(2,1)S(1)} %copy-done, f32[32,128,192]{2,1,0:T(8,128)S(1)} %get-tuple-element.48.add_ref), custom_call_target="tpu_custom_call" | custom-call | tf_op jit(solution)/shard_map/conv_back/pallas_call | solution.py:259
  79.0 0.0 collective-permute-done.6.left_ref
  79.0 0.0 collective-permute-done.7.right_ref
  79.0 0.0 collective-permute-done.4.top_ref
  79.0 0.0 collective-permute-done.5.bot_ref
  79.0 2.4 %finish.1 = f32[32,192,128]{2,1,0:T(8,128)} custom-call(f32[32,128,192]{2,1,0:T(8,128)S(1)} %conv_back.1.g_ref, bf16[9,192,192]{2,1,0:T(8,128)(2,1)S(1)} %copy-done, bf16[128,192]{1,0:T(8,128)(2,1)S(1)} %collective-permute-done.4.top_ref, bf16[128,192]{1,0:T(8,128)(2,1)S(1)} %collective-permute-done.5.bot_ref, ...), custom_call_target="tpu_custom_call" | custom-call | tf_op jit(solution)/shard_map/finish/pallas_call | solution.py:553
Async XLA Ops:
  0.6 18.0 %copy-start = (bf16[9,192,192]{2,1,0:T(8,128)(2,1)S(1)}, bf16[9,192,192]{2,1,0:T(8,128)(2,1)}, u32[]{:S(2)}) copy-start(bf16[9,192,192]{2,1,0:T(8,128)(2,1)} %w_ref.7) | copy-start | bytes 1990660
  3.9 14.7 %all-to-all-start = ((bf16[32,8,128]{2,1,0:T(8,128)(2,1)}), bf16[32,8,128]{2,1,0:T(8,128)(2,1)S(1)}, u32[]{:S(2)}, u32[]{:S(2)}) async-start(bf16[32,8,128]{2,1,0:T(8,128)(2,1)} %get-tuple-element.28), calls=%async_computation | async-start | bytes 131072 | tf_op jit(solution)/shard_map/all_to_all | solution.py:792
  11.3 13.9 %collective-permute-start = (bf16[128,192]{1,0:T(8,128)(2,1)}, bf16[128,192]{1,0:T(8,128)(2,1)S(1)}, u32[]{:S(2)}, u32[]{:S(2)}) collective-permute-start(bf16[128,192]{1,0:T(8,128)(2,1)} %get-tuple-element.33), channel_id=1, source_target_pairs={{0,8},{8,16},{16,24},{24,0},{1,9},{9,17},{17,25},{25,1},{2,10},{10... | collective-permute-start | bytes 147464 | tf_op jit(solution)/shard_map/ppermute | solution.py:783
  13.1 12.1 %collective-permute-start.1 = (bf16[128,192]{1,0:T(8,128)(2,1)}, bf16[128,192]{1,0:T(8,128)(2,1)S(1)}, u32[]{:S(2)}, u32[]{:S(2)}) collective-permute-start(bf16[128,192]{1,0:T(8,128)(2,1)} %get-tuple-element.34), channel_id=1, source_target_pairs={{0,24},{8,0},{16,8},{24,16},{1,25},{9,1},{17,9},{25,17},{2,26},{10... | collective-permute-start | bytes 147464 | tf_op jit(solution)/shard_map/ppermute | solution.py:783
  14.2 10.9 %collective-permute-start.2 = (bf16[32,192]{1,0:T(8,128)(2,1)}, bf16[32,192]{1,0:T(8,128)(2,1)S(1)}, u32[]{:S(2)}, u32[]{:S(2)}) collective-permute-start(bf16[32,192]{1,0:T(8,128)(2,1)} %get-tuple-element.35), channel_id=1, source_target_pairs={{0,1},{1,2},{2,3},{3,4},{4,5},{5,6},{6,7},{7,0},{8,9},{9,10},{10,1... | collective-permute-start | bytes 36872 | tf_op jit(solution)/shard_map/ppermute | solution.py:783
  14.2 11.0 %collective-permute-start.3 = (bf16[32,192]{1,0:T(8,128)(2,1)}, bf16[32,192]{1,0:T(8,128)(2,1)S(1)}, u32[]{:S(2)}, u32[]{:S(2)}) collective-permute-start(bf16[32,192]{1,0:T(8,128)(2,1)} %get-tuple-element.36), channel_id=1, source_target_pairs={{0,7},{1,0},{2,1},{3,2},{4,3},{5,4},{6,5},{7,6},{8,15},{9,8},{10,9... | collective-permute-start | bytes 36872 | tf_op jit(solution)/shard_map/ppermute | solution.py:783
  30.9 12.6 %all-to-all-start.1 = ((bf16[32,32,128]{2,1,0:T(8,128)(2,1)}), bf16[32,32,128]{2,1,0:T(8,128)(2,1)S(1)}, u32[]{:S(2)}, u32[]{:S(2)}) async-start(bf16[32,32,128]{2,1,0:T(8,128)(2,1)} %get-tuple-element.37), calls=%async_computation.1 | async-start | bytes 524288 | tf_op jit(solution)/shard_map/all_to_all | solution.py:792
  33.7 30.5 %copy-start.1 = (bf16[32,128,192]{2,1,0:T(8,128)(2,1)S(1)}, bf16[32,128,192]{2,1,0:T(8,128)(2,1)}, u32[]{:S(2)}) copy-start(bf16[32,128,192]{2,1,0:T(8,128)(2,1)} %get-tuple-element.46.gate_ref) | copy-start | bytes 4718596
  67.8 11.2 %collective-permute-start.4 = (bf16[128,192]{1,0:T(8,128)(2,1)S(1)}, bf16[128,192]{1,0:T(8,128)(2,1)S(1)}, u32[]{:S(2)}, u32[]{:S(2)}) collective-permute-start(bf16[128,192]{1,0:T(8,128)(2,1)S(1)} %get-tuple-element.49), channel_id=1, source_target_pairs={{0,8},{8,16},{16,24},{24,0},{1,9},{9,17},{17,25},{25,1},{2,10},{10... | collective-permute-start | bytes 147464 | tf_op jit(solution)/shard_map/ppermute | solution.py:783
  68.7 10.3 %collective-permute-start.5 = (bf16[128,192]{1,0:T(8,128)(2,1)S(1)}, bf16[128,192]{1,0:T(8,128)(2,1)S(1)}, u32[]{:S(2)}, u32[]{:S(2)}) collective-permute-start(bf16[128,192]{1,0:T(8,128)(2,1)S(1)} %get-tuple-element.50), channel_id=1, source_target_pairs={{0,24},{8,0},{16,8},{24,16},{1,25},{9,1},{17,9},{25,17},{2,26},{10... | collective-permute-start | bytes 147464 | tf_op jit(solution)/shard_map/ppermute | solution.py:783
  70.8 8.2 %collective-permute-start.6 = (bf16[32,192]{1,0:T(8,128)(2,1)S(1)}, bf16[32,192]{1,0:T(8,128)(2,1)S(1)}, u32[]{:S(2)}, u32[]{:S(2)}) collective-permute-start(bf16[32,192]{1,0:T(8,128)(2,1)S(1)} %get-tuple-element.51), channel_id=1, source_target_pairs={{0,1},{1,2},{2,3},{3,4},{4,5},{5,6},{6,7},{7,0},{8,9},{9,10},{10,1... | collective-permute-start | bytes 36872 | tf_op jit(solution)/shard_map/ppermute | solution.py:783
  71.0 8.0 %collective-permute-start.7 = (bf16[32,192]{1,0:T(8,128)(2,1)S(1)}, bf16[32,192]{1,0:T(8,128)(2,1)S(1)}, u32[]{:S(2)}, u32[]{:S(2)}) collective-permute-start(bf16[32,192]{1,0:T(8,128)(2,1)S(1)} %get-tuple-element.52), channel_id=1, source_target_pairs={{0,7},{1,0},{2,1},{3,2},{4,3},{5,4},{6,5},{7,6},{8,15},{9,8},{10,9... | collective-permute-start | bytes 36872 | tf_op jit(solution)/shard_map/ppermute | solution.py:783

commit v5 on v4

--- a/solution.py
+++ b/solution.py
@@ -8,10 +8,12 @@
 from jax.experimental.pallas import tpu as pltpu
 from jax.sharding import PartitionSpec as P
 
+
 HEADS = 3
 EPS = 1e-06
 NEG = -1e30
 AXES = ("lat", "lon")
+CHUNKS = 4
 F32 = jnp.float32
 BF16 = jnp.bfloat16
 VMEM = pltpu.VMEM
@@ -109,12 +111,19 @@
     return rank_col, rank_row, route_col
 
 
+def ends_of(cols):
+    row, lane = iota((16, cols), 0), iota((16, cols), 1)
+    return onehot(((row == 0) & (lane == 0)) | ((row == 1) & (lane == cols - 1)))
+
+
 def intro_kernel(
-    route_hbm, spot_hbm, x_hbm, slab_ref, top_ref, bot_ref, left_ref, right_ref, route_ref, spot_ref, x_ref, slab,
-    sem,
+    route_hbm, spot_hbm, x_hbm, slab_ref, top_ref, bot_ref, route_ref, spot_ref, first_ref, final_ref, slab, sem
 ):
-    rows, ch, cols = x_ref.shape
-    pairs = ((route_hbm, route_ref), (spot_hbm, spot_ref), (x_hbm, x_ref))
+    _, cols = first_ref.shape
+    rows = x_hbm.shape[0]
+    pairs = (
+        (route_hbm, route_ref), (spot_hbm, spot_ref), (x_hbm.at[0], first_ref), (x_hbm.at[rows - 1], final_ref)
+    )
     fetches = [pltpu.make_async_copy(a, b, sem.at[k]) for k, (a, b) in enumerate(pairs)]
     for fetch in fetches:
         fetch.start()
@@ -131,44 +140,55 @@
     slab[:, 0, :] = nn(jnp.where(member, high, 0.0).astype(BF16), ranked)
     slab[:, 1, :] = nn(jnp.where(member, low, 0.0).astype(BF16), ranked)
     fetches[2].wait()
-    eye = onehot(iota((cols, cols), 0) == iota((cols, cols), 1))
-    row, lane = iota((16, cols), 0), iota((16, cols), 1)
-    ends = onehot(((row == 0) & (lane == 0)) | ((row == 1) & (lane == cols - 1)))
-    pairs = [nt(ends, x_ref[r]) for r in range(rows)]
-    firsts = [p[0:1] for p in pairs]
-    lasts = [p[1:2] for p in pairs]
-    left_ref[...] = jnp.concatenate(lasts, axis=0).astype(BF16)
-    right_ref[...] = jnp.concatenate(firsts, axis=0).astype(BF16)
-    bot_ref[...] = nt(eye, x_ref[0]).astype(BF16)
-    top_ref[...] = nt(eye, x_ref[rows - 1]).astype(BF16)
-    mine = corner_tile([lasts[-1], firsts[-1], lasts[0], firsts[0]])
+    fetches[3].wait()
+    ends = ends_of(cols)
+    first, final = nt(ends, first_ref[...]), nt(ends, final_ref[...])
+    mine = corner_tile([final[1:2], final[0:1], first[1:2], first[0:1]])
     for k in range(6):
         slab[:, 2 + k, :] = jnp.broadcast_to(mine[k], (regions, 128))
     slab_ref[...] = slab[...].astype(BF16)
+    bot_ref[...] = first_ref[...].T
+    top_ref[...] = final_ref[...].T
 
 
 def intro(route, spot, x_t, regions):
-    rows, ch, cols = x_t.shape
+    _, ch, cols = x_t.shape
     return pl.pallas_call(
         intro_kernel,
-        out_shape=(
-            SDS((regions, 8, 128), BF16),
-            SDS((cols, ch), BF16),
-            SDS((cols, ch), BF16),
-            SDS((rows, ch), BF16),
-            SDS((rows, ch), BF16),
-        ),
+        out_shape=(pltpu.HBM((regions, 8, 128), BF16), VMEM((cols, ch), BF16), VMEM((cols, ch), BF16)),
         in_specs=in_hbm(3),
-        out_specs=tuple(whole(5)),
+        out_specs=tuple(whole(3)),
         scratch_shapes=[
             VMEM(route.shape, jnp.int32),
             VMEM(spot.shape, jnp.int32),
-            VMEM(x_t.shape, BF16),
+            VMEM((ch, cols), BF16),
+            VMEM((ch, cols), BF16),
             VMEM((regions, 8, 128), F32),
-            pltpu.SemaphoreType.DMA((3,)),
+            pltpu.SemaphoreType.DMA((4,)),
         ],
+        compiler_params=PARAMS,
         name="intro",
     )(hbm(route), hbm(spot), hbm(x_t))
+
+
+def sides_kernel(x_ref, left_ref, right_ref):
+    rows, _, cols = x_ref.shape
+    ends = ends_of(cols)
+    pairs = [nt(ends, x_ref[r]) for r in range(rows)]
+    left_ref[...] = jnp.concatenate([p[1:2] for p in pairs], axis=0).astype(BF16)
+    right_ref[...] = jnp.concatenate([p[0:1] for p in pairs], axis=0).astype(BF16)
+
+
+def side_columns(x_t):
+    rows, ch, _ = x_t.shape
+    return pl.pallas_call(
+        sides_kernel,
+        out_shape=(VMEM((rows, ch), BF16), VMEM((rows, ch), BF16)),
+        in_specs=whole(1),
+        out_specs=tuple(whole(2)),
+        compiler_params=PARAMS,
+        name="sides",
+    )(x_t)
 
 
 def conv_weights(w_ref, wc, back):
@@ -211,23 +231,15 @@
                 o_ref[r] = line + add_ref[r] if back else line
 
 
-def conv_core_kernel(parts, x_hbm, w_ref, o_ref, xs_ref, wc, x_ref, sem):
+def conv_core_kernel(x_ref, w_ref, o_ref, xs_ref, wc):
     rows, ch, cols = x_ref.shape
     deep = xs_ref.shape[2]
-    size = rows // parts
-    at = [pl.ds(k * size, size) for k in range(parts)]
-    fetches = [pltpu.make_async_copy(x_hbm.at[a], x_ref.at[a], sem.at[k]) for k, a in enumerate(at)]
-    for fetch in fetches:
-        fetch.start()
     conv_weights(w_ref, wc, False)
-    eye = onehot(iota((cols, cols), 0) == iota((cols, cols), 1))
     pad = jnp.zeros((cols, deep - ch), BF16)
     xs_ref[0] = jnp.zeros((cols, deep), BF16)
     xs_ref[rows + 1] = jnp.zeros((cols, deep), BF16)
     for r in range(rows):
-        if r % size == 0:
-            fetches[r // size].wait()
-        xs_ref[r + 1] = jnp.concatenate([nt(eye, x_ref[r]).astype(BF16), pad], axis=1)
+        xs_ref[r + 1] = jnp.concatenate([x_ref[r].T, pad], axis=1)
     conv_blocks(False, rows // 4, xs_ref, wc, None, o_ref)
 
 
@@ -236,26 +248,24 @@
     conv_blocks(True, o_ref.shape[0] // 4, xs_ref, wc, add_ref, o_ref)
 
 
-def conv_core(x_t, taps, parts=4):
+def conv_core(x_t, taps):
     rows, ch, cols = x_t.shape
     deep = up(ch, 128)
     return pl.pallas_call(
-        functools.partial(conv_core_kernel, parts),
+        conv_core_kernel,
         out_shape=(SDS((rows, cols, ch), F32), SDS((rows + 2, cols, deep), BF16)),
-        in_specs=in_hbm(1) + whole(1),
+        in_specs=whole(2),
         out_specs=tuple(whole(2)),
         scratch_shapes=[
             VMEM((12, deep, ch), BF16),
-            VMEM(x_t.shape, BF16),
-            pltpu.SemaphoreType.DMA((parts,)),
         ],
         compiler_params=PARAMS,
         name="conv_core",
-    )(hbm(x_t), taps)
+    )(x_t, taps)
 
 
 def conv_back(xs, taps, add):
-    rows, cols, ch = add.shape
+    _, _, ch = add.shape
     return pl.pallas_call(
         conv_back_kernel,
         out_shape=SDS(add.shape, F32),
@@ -501,11 +511,11 @@
         out_shape=(
             SDS(gate.shape, F32),
             SDS((rows + 2, cols, up(ch, 128)), BF16),
-            SDS((cols, ch), BF16),
-            SDS((cols, ch), BF16),
-            SDS((rows, ch), BF16),
-            SDS((rows, ch), BF16),
-            SDS((8, ch), F32),
+            VMEM((cols, ch), BF16),
+            VMEM((cols, ch), BF16),
+            VMEM((rows, ch), BF16),
+            VMEM((rows, ch), BF16),
+            VMEM((8, ch), F32),
         ),
         in_specs=in_hbm(3) + whole(1),
         out_specs=tuple(whole(7)),
@@ -524,7 +534,7 @@
 
 
 def finish_kernel(parts, g_ref, w_ref, top_ref, bot_ref, left_ref, right_ref, corner_ref, o_hbm, fix, o_ref, sem):
-    rows, cols, ch = g_ref.shape
+    rows, _, _ = g_ref.shape
     corners = corner_ref[...]
     above = inside(-1) * border_rows(top_ref[...], w_ref, 0, True)
     below = inside(1) * border_rows(bot_ref[...], w_ref, 2, True)
@@ -677,9 +687,13 @@
         copy.start()
     index_ref, part_ref, w_in, g1_ref, w_qkv, bias_ref, w_out, g2_ref, w_head, mask_ref, obs_ref, from_ref = here
     need = lambda first, last: [copy.wait() for copy in fetches[first:last]]
+    size = out_ref.shape[0] // CHUNKS
+    chunks = [pl.ds(k * size, size) for k in range(CHUNKS)]
     stores = [
         pltpu.make_async_copy(a, b, sem.at[12 + k])
-        for k, (a, b) in enumerate(((pred_ref, pred_hbm), (out_ref, out_hbm), (gates_ref, gates_hbm)))
+        for k, (a, b) in enumerate(
+            ((pred_ref, pred_hbm), *((out_ref.at[p], out_hbm.at[p]) for p in chunks), (gates_ref, gates_hbm))
+        )
     ]
     stations, ch = part_ref.shape
     packed = from_ref.shape[0]
@@ -690,7 +704,7 @@
 
     base = cap + cap // 2
     gates_ref[...] = jnp.concatenate(near_corners(ans_ref, base) + [jnp.zeros((4, ch), F32)], axis=0)
-    stores[2].start()
+    stores[-1].start()
     need(0, 3)
     at = iota_f((stations, packed), 1)
     to = onehot(at == index_ref[:, 0:1])
@@ -747,9 +761,13 @@
         jnp.concatenate([blank, extra], axis=1),
     ]
     need(11, 12)
-    out = nn(from_ref[...], jnp.concatenate(parts, axis=0).astype(BF16))
-    out_ref[...] = out.astype(BF16).reshape(out_ref.shape)
-    stores[1].start()
+    taken = jnp.concatenate(parts, axis=0).astype(BF16)
+    regions, deep, _ = out_ref.shape
+    size = regions // CHUNKS
+    for k in range(CHUNKS):
+        out = nn(from_ref[k * size * deep : (k + 1) * size * deep], taken)
+        out_ref[k * size : (k + 1) * size] = out.astype(BF16).reshape(size, deep, 128)
+        stores[1 + k].start()
     for store in stores:
         store.wait()
 
@@ -771,7 +789,7 @@
             VMEM((HEADS, n, n), F32),
             VMEM((n, 3 * ch), BF16),
             *[VMEM(o.shape, o.dtype) for o in outs],
-            pltpu.SemaphoreType.DMA((len(late) + len(outs),)),
+            pltpu.SemaphoreType.DMA((len(late) + len(outs) + CHUNKS,)),
         ],
         compiler_params=PARAMS,
         name="stations",
@@ -818,9 +836,9 @@
     w_in = in_weight.T
 
     x_t = jnp.swapaxes(grid_field, 1, 2)
-    asks, *sides = intro(route, spot, x_t, regions)
+    asks, top, bot = intro(route, spot, x_t, regions)
     asked = exchange(asks)
-    borders = halo(*sides)
+    borders = halo(top, bot, *side_columns(x_t))
     asked, x_in = lax.optimization_barrier((asked, x_t))
     y, xs = conv_core(x_in, conv_weight)
     answer, gate, spots = sample(y, xs, conv_weight, asked, *borders, cap)

time: 82.1 us -> 79.3 us (0.966)
  Pallas kernels: 37.2 us -> 34.7 us
  waiting for transfers between devices: 6.22 us -> 5.36 us
    pallas_call x2 -> x3, Pallas kernels: 9.79 us -> 7.48 us  [the longest x1 4.31 us: conv_core(): pl.pallas_call(conv_core_kernel, out_shape=(SDS((rows, cols, ch), F32), S...]
    all_to_all x2, waiting for transfers between devices: 6.19 us -> 5.34 us  [exchange(): return lax.all_to_all(x, AXES, split_axis=0, concat_axis=0, tiled=True)]
  transfers between devices with their start and end apart: 10 -> 10, of which waited for: 2 -> 1; matrix products, arithmetic and copies ran while one was open for 0% -> 0% of each run, Pallas kernels for 18% -> 17%
where the time goes in v5:
time: 79.3 us; the launch traced here: 78.9 us
  Pallas kernels  34.7 us (44%)
  starting transfers between devices  23.7 us (30%)
  blocking collectives  13.3 us (17%)
  waiting for transfers between devices  5.36 us (7%)
  between operations  1.74 us (2%)
    all_to_all x1, blocking collectives, exchange(): return lax.all_to_all(x, AXES, split_axis=0, concat_axis=0, tiled=True)  13.3 us
    ppermute x8, starting transfers between devices, shift(): return lax.ppermute(x, axis, [(i, (i + step) % n) for i in range(n)])  13.1 us
    all_to_all x2, starting transfers between devices, exchange(): return lax.all_to_all(x, AXES, split_axis=0, concat_axis=0, tiled=True)  10.7 us
    pallas_call x1, Pallas kernels, stations_pass(): pl.pallas_call(functools.partial(station_kernel, cap), out_shape=outs, in...  7.16 us
    pallas_call x1, Pallas kernels, sample(): pl.pallas_call(functools.partial(sample_kernel, cap), out_shape=(pltpu.HB...  5.66 us
    all_to_all x2, waiting for transfers between devices, exchange(): return lax.all_to_all(x, AXES, split_axis=0, concat_axis=0, tiled=True)  5.34 us
    pallas_call x1, Pallas kernels, conv_back(): pl.pallas_call(conv_back_kernel, out_shape=SDS(add.shape, F32), in_specs=...  4.64 us
    pallas_call x1, Pallas kernels, conv_core(): pl.pallas_call(conv_core_kernel, out_shape=(SDS((rows, cols, ch), F32), S...  4.31 us
  transfers between devices with their start and end apart: 10, of which 1 were waited for; matrix products, arithmetic and copies ran while one was open for 0% of the time, Pallas kernels for 17%

profile of v5, /device:TPU:0, one launch (start us, length us, event | category | flops | bytes accessed | tf_op | source)
XLA Modules:
  0.0 78.9 jit_solution(11651203560590184956)
XLA Ops:
  0.6 0.0 copy-start.1
  0.6 0.0 copy-start
  0.6 2.3 %intro.1 = (bf16[32,8,128]{2,1,0:T(8,128)(2,1)}, bf16[128,192]{1,0:T(8,128)(2,1)S(1)}, bf16[128,192]{1,0:T(8,128)(2,1)S(1)}) custom-call(s32[1,256]{1,0:T(1,128)} %bitcast.18, s32[1,256]{1,0:T(1,128)} %bitcast.20, bf16[32,192,128]{2,1,0:T(8,128)(2,1)} %bitcast.10), custom_call_target="tpu_custom_call" | custom-call | tf_op jit(solution)/shard_map/intro/pallas_call | solution.py:156
  2.9 7.3 %all-to-all-start = ((bf16[32,8,128]{2,1,0:T(8,128)(2,1)}), bf16[32,8,128]{2,1,0:T(8,128)(2,1)S(1)}, u32[]{:S(2)}, u32[]{:S(2)}) async-start(bf16[32,8,128]{2,1,0:T(8,128)(2,1)} %get-tuple-element.28), calls=%async_computation | async-start | bytes 131072 | tf_op jit(solution)/shard_map/all_to_all | solution.py:810
  10.3 1.8 %collective-permute-start = (bf16[128,192]{1,0:T(8,128)(2,1)S(1)}, bf16[128,192]{1,0:T(8,128)(2,1)S(1)}, u32[]{:S(2)}, u32[]{:S(2)}) collective-permute-start(bf16[128,192]{1,0:T(8,128)(2,1)S(1)} %get-tuple-element.33), channel_id=1, source_target_pairs={{0,8},{8,16},{16,24},{24,0},{1,9},{9,17},{17,25},{25,1},{2,10},{10... | collective-permute-start | bytes 147464 | tf_op jit(solution)/shard_map/ppermute | solution.py:801
  12.1 1.2 %collective-permute-start.1 = (bf16[128,192]{1,0:T(8,128)(2,1)S(1)}, bf16[128,192]{1,0:T(8,128)(2,1)S(1)}, u32[]{:S(2)}, u32[]{:S(2)}) collective-permute-start(bf16[128,192]{1,0:T(8,128)(2,1)S(1)} %get-tuple-element.34), channel_id=1, source_target_pairs={{0,24},{8,0},{16,8},{24,16},{1,25},{9,1},{17,9},{25,17},{2,26},{10... | collective-permute-start | bytes 147464 | tf_op jit(solution)/shard_map/ppermute | solution.py:801
  13.2 0.0 copy-done.1
  13.2 0.9 %sides.1 = (bf16[32,192]{1,0:T(8,128)(2,1)S(1)}, bf16[32,192]{1,0:T(8,128)(2,1)S(1)}) custom-call(bf16[32,192,128]{2,1,0:T(8,128)(2,1)S(1)} %bitcast.11), custom_call_target="tpu_custom_call" | custom-call | tf_op jit(solution)/shard_map/sides/pallas_call | solution.py:184
  14.1 0.0 collective-permute-start.2
  14.2 3.6 %collective-permute-start.3 = (bf16[32,192]{1,0:T(8,128)(2,1)S(1)}, bf16[32,192]{1,0:T(8,128)(2,1)S(1)}, u32[]{:S(2)}, u32[]{:S(2)}) collective-permute-start(bf16[32,192]{1,0:T(8,128)(2,1)S(1)} %get-tuple-element.36), channel_id=1, source_target_pairs={{0,7},{1,0},{2,1},{3,2},{4,3},{5,4},{6,5},{7,6},{8,15},{9,8},{10,9... | collective-permute-start | bytes 36872 | tf_op jit(solution)/shard_map/ppermute | solution.py:801
  17.7 0.0 all-to-all-done.asked_ref
  17.7 0.0 copy-done
  17.7 4.3 %conv_core.1 = (f32[32,128,192]{2,1,0:T(8,128)S(1)}, bf16[34,128,256]{2,1,0:T(8,128)(2,1)S(1)}) custom-call(bf16[32,192,128]{2,1,0:T(8,128)(2,1)S(1)} %bitcast.12, bf16[9,192,192]{2,1,0:T(8,128)(2,1)S(1)} %copy-done), custom_call_target="tpu_custom_call" | custom-call | tf_op jit(solution)/shard_map/conv_core/pallas_call | solution.py:254
  22.0 0.0 collective-permute-done.2.left_ref
  22.0 0.0 collective-permute-done.3.right_ref
  22.1 0.0 collective-permute-done.top_ref
  22.1 0.0 collective-permute-done.1.bot_ref
  22.1 5.7 %sample.1 = (bf16[32,32,128]{2,1,0:T(8,128)(2,1)}, bf16[32,128,192]{2,1,0:T(8,128)(2,1)}, f32[32,128]{1,0:T(8,128)}) custom-call(f32[32,128,192]{2,1,0:T(8,128)S(1)} %get-tuple-element.30.y_ref, bf16[34,128,256]{2,1,0:T(8,128)(2,1)S(1)} %get-tuple-element.31.xs_ref, bf16[9,192,192]{2,1,0:T(8,128)(2,1)S(1)} %copy-done, ...), custom_call_target="tpu_custom_call" | custom-call | tf_op jit(solution)/shard_map/sample/pallas_call | solution.py:423
  27.7 3.3 %all-to-all-start.1 = ((bf16[32,32,128]{2,1,0:T(8,128)(2,1)}), bf16[32,32,128]{2,1,0:T(8,128)(2,1)S(1)}, u32[]{:S(2)}, u32[]{:S(2)}) async-start(bf16[32,32,128]{2,1,0:T(8,128)(2,1)} %get-tuple-element.37), calls=%async_computation.1 | async-start | bytes 524288 | tf_op jit(solution)/shard_map/all_to_all | solution.py:810
  31.1 0.0 copy-start.2
  31.9 3.7 %prepare.1 = (bf16[1024,768]{1,0:T(8,128)(2,1)}, f32[256,256]{1,0:T(8,128)}, f32[256,192]{1,0:T(8,128)}, f32[256,128]{1,0:T(8,128)}) custom-call(s32[1]{0:T(128)S(6)} %copy.18.live_ref, s32[1,256]{1,0:T(1,128)} %bitcast.19, s32[1,256]{1,0:T(1,128)} %bitcast.21, s32[16,256]{1,0:T(8,128)} %bitcast.16, s32[1,256]{1,0:T(1,128)} %bitcast.24, f32[16,256]{1,0:T(8,128)} %bitcast.17, ...), custom_call_target="tpu_custom_call" | custom-call | tf_op jit(solution)/shard_map/prepare/pallas_call | solution.py:667
  35.6 5.3 %all-to-all-done.1.ans_ref = bf16[32,32,128]{2,1,0:T(8,128)(2,1)S(1)} async-done(((bf16[32,32,128]{2,1,0:T(8,128)(2,1)}), bf16[32,32,128]{2,1,0:T(8,128)(2,1)S(1)}, u32[]{:S(2)}, u32[]{:S(2)}) %all-to-all-start.1) | async-done | bytes 262176 | tf_op jit(solution)/shard_map/all_to_all | solution.py:810
  40.9 7.2 %stations.1 = (f32[256,128]{1,0:T(8,128)}, bf16[32,32,128]{2,1,0:T(8,128)(2,1)}, f32[8,192]{1,0:T(8,128)}) custom-call(s32[1]{0:T(128)S(6)} %copy.18.live_ref, bf16[32,32,128]{2,1,0:T(8,128)(2,1)S(1)} %all-to-all-done.1.ans_ref, f32[256,128]{1,0:T(8,128)} %get-tuple-element.38.refs_0_, f32[256,192]{1,0:T(8,128)} %get-tuple-element.39.refs_1_, ...), custom_call_target="tpu_custom_call" | custom-call | tf_op jit(solution)/shard_map/stations/pallas_call | solution.py:782
  48.1 13.3 %all_to_all.15.inc_hbm = bf16[32,32,128]{2,1,0:T(8,128)(2,1)} all-to-all(bf16[32,32,128]{2,1,0:T(8,128)(2,1)} %get-tuple-element.44), channel_id=1, replica_groups=mesh['lat'=4,'lon'=8] {'lat','lon'}, dimensions={0} | all-to-all | bytes 524288 | tf_op jit(solution)/shard_map/all_to_all | solution.py:810
  61.4 0.0 copy-done.2
  61.4 3.7 %spread.1 = (f32[32,128,192]{2,1,0:T(8,128)S(1)}, bf16[34,128,256]{2,1,0:T(8,128)(2,1)S(1)}, bf16[128,192]{1,0:T(8,128)(2,1)S(1)}, bf16[128,192]{1,0:T(8,128)(2,...) custom-call(f32[32,128]{1,0:T(8,128)} %get-tuple-element.43.spots_hbm, ...), custom_call_target="tpu_custom_call" | custom-call | tf_op jit(solution)/shard_map/spread/pallas_call | solution.py:509
  65.1 0.9 %collective-permute-start.4 = (bf16[128,192]{1,0:T(8,128)(2,1)S(1)}, bf16[128,192]{1,0:T(8,128)(2,1)S(1)}, u32[]{:S(2)}, u32[]{:S(2)}) collective-permute-start(bf16[128,192]{1,0:T(8,128)(2,1)S(1)} %get-tuple-element.49), channel_id=1, source_target_pairs={{0,8},{8,16},{16,24},{24,0},{1,9},{9,17},{17,25},{25,1},{2,10},{10... | collective-permute-start | bytes 147464 | tf_op jit(solution)/shard_map/ppermute | solution.py:801
  66.0 2.1 %collective-permute-start.5 = (bf16[128,192]{1,0:T(8,128)(2,1)S(1)}, bf16[128,192]{1,0:T(8,128)(2,1)S(1)}, u32[]{:S(2)}, u32[]{:S(2)}) collective-permute-start(bf16[128,192]{1,0:T(8,128)(2,1)S(1)} %get-tuple-element.50), channel_id=1, source_target_pairs={{0,24},{8,0},{16,8},{24,16},{1,25},{9,1},{17,9},{25,17},{2,26},{10... | collective-permute-start | bytes 147464 | tf_op jit(solution)/shard_map/ppermute | solution.py:801
  68.0 0.2 collective-permute-start.6
  68.2 3.3 %collective-permute-start.7 = (bf16[32,192]{1,0:T(8,128)(2,1)S(1)}, bf16[32,192]{1,0:T(8,128)(2,1)S(1)}, u32[]{:S(2)}, u32[]{:S(2)}) collective-permute-start(bf16[32,192]{1,0:T(8,128)(2,1)S(1)} %get-tuple-element.52), channel_id=1, source_target_pairs={{0,7},{1,0},{2,1},{3,2},{4,3},{5,4},{6,5},{7,6},{8,15},{9,8},{10,9... | collective-permute-start | bytes 36872 | tf_op jit(solution)/shard_map/ppermute | solution.py:801
  71.6 4.6 %conv_back.1.g_ref = f32[32,128,192]{2,1,0:T(8,128)S(1)} custom-call(bf16[34,128,256]{2,1,0:T(8,128)(2,1)S(1)} %get-tuple-element.47.xs_ref, bf16[9,192,192]{2,1,0:T(8,128)(2,1)S(1)} %copy-done, f32[32,128,192]{2,1,0:T(8,128)S(1)} %get-tuple-element.48.add_ref), custom_call_target="tpu_custom_call" | custom-call | tf_op jit(solution)/shard_map/conv_back/pallas_call | solution.py:269
  76.2 0.0 collective-permute-done.6.left_ref
  76.2 0.0 collective-permute-done.7.right_ref
  76.2 0.0 collective-permute-done.4.top_ref
  76.3 0.0 collective-permute-done.5.bot_ref
  76.3 2.4 %finish.1 = f32[32,192,128]{2,1,0:T(8,128)} custom-call(f32[32,128,192]{2,1,0:T(8,128)S(1)} %conv_back.1.g_ref, bf16[9,192,192]{2,1,0:T(8,128)(2,1)S(1)} %copy-done, bf16[128,192]{1,0:T(8,128)(2,1)S(1)} %collective-permute-done.4.top_ref, bf16[128,192]{1,0:T(8,128)(2,1)S(1)} %collective-permute-done.5.bot_ref, ...), custom_call_target="tpu_custom_call" | custom-call | tf_op jit(solution)/shard_map/finish/pallas_call | solution.py:563
Async XLA Ops:
  0.6 12.6 %copy-start.1 = (bf16[32,128,192]{1,2,0:T(8,128)(2,1)S(1)}, bf16[32,128,192]{1,2,0:T(8,128)(2,1)}, u32[]{:S(2)}) copy-start(bf16[32,128,192]{1,2,0:T(8,128)(2,1)} %param.16) | copy-start | bytes 4718596
  0.6 17.1 %copy-start = (bf16[9,192,192]{2,1,0:T(8,128)(2,1)S(1)}, bf16[9,192,192]{2,1,0:T(8,128)(2,1)}, u32[]{:S(2)}) copy-start(bf16[9,192,192]{2,1,0:T(8,128)(2,1)} %w_ref.7) | copy-start | bytes 1990660
  2.9 14.8 %all-to-all-start = ((bf16[32,8,128]{2,1,0:T(8,128)(2,1)}), bf16[32,8,128]{2,1,0:T(8,128)(2,1)S(1)}, u32[]{:S(2)}, u32[]{:S(2)}) async-start(bf16[32,8,128]{2,1,0:T(8,128)(2,1)} %get-tuple-element.28), calls=%async_computation | async-start | bytes 131072 | tf_op jit(solution)/shard_map/all_to_all | solution.py:810
  10.3 11.8 %collective-permute-start = (bf16[128,192]{1,0:T(8,128)(2,1)S(1)}, bf16[128,192]{1,0:T(8,128)(2,1)S(1)}, u32[]{:S(2)}, u32[]{:S(2)}) collective-permute-start(bf16[128,192]{1,0:T(8,128)(2,1)S(1)} %get-tuple-element.33), channel_id=1, source_target_pairs={{0,8},{8,16},{16,24},{24,0},{1,9},{9,17},{17,25},{25,1},{2,10},{10... | collective-permute-start | bytes 147464 | tf_op jit(solution)/shard_map/ppermute | solution.py:801
  12.1 10.0 %collective-permute-start.1 = (bf16[128,192]{1,0:T(8,128)(2,1)S(1)}, bf16[128,192]{1,0:T(8,128)(2,1)S(1)}, u32[]{:S(2)}, u32[]{:S(2)}) collective-permute-start(bf16[128,192]{1,0:T(8,128)(2,1)S(1)} %get-tuple-element.34), channel_id=1, source_target_pairs={{0,24},{8,0},{16,8},{24,16},{1,25},{9,1},{17,9},{25,17},{2,26},{10... | collective-permute-start | bytes 147464 | tf_op jit(solution)/shard_map/ppermute | solution.py:801
  14.1 7.9 %collective-permute-start.2 = (bf16[32,192]{1,0:T(8,128)(2,1)S(1)}, bf16[32,192]{1,0:T(8,128)(2,1)S(1)}, u32[]{:S(2)}, u32[]{:S(2)}) collective-permute-start(bf16[32,192]{1,0:T(8,128)(2,1)S(1)} %get-tuple-element.35), channel_id=1, source_target_pairs={{0,1},{1,2},{2,3},{3,4},{4,5},{5,6},{6,7},{7,0},{8,9},{9,10},{10,1... | collective-permute-start | bytes 36872 | tf_op jit(solution)/shard_map/ppermute | solution.py:801
  14.2 7.9 %collective-permute-start.3 = (bf16[32,192]{1,0:T(8,128)(2,1)S(1)}, bf16[32,192]{1,0:T(8,128)(2,1)S(1)}, u32[]{:S(2)}, u32[]{:S(2)}) collective-permute-start(bf16[32,192]{1,0:T(8,128)(2,1)S(1)} %get-tuple-element.36), channel_id=1, source_target_pairs={{0,7},{1,0},{2,1},{3,2},{4,3},{5,4},{6,5},{7,6},{8,15},{9,8},{10,9... | collective-permute-start | bytes 36872 | tf_op jit(solution)/shard_map/ppermute | solution.py:801
  27.7 13.2 %all-to-all-start.1 = ((bf16[32,32,128]{2,1,0:T(8,128)(2,1)}), bf16[32,32,128]{2,1,0:T(8,128)(2,1)S(1)}, u32[]{:S(2)}, u32[]{:S(2)}) async-start(bf16[32,32,128]{2,1,0:T(8,128)(2,1)} %get-tuple-element.37), calls=%async_computation.1 | async-start | bytes 524288 | tf_op jit(solution)/shard_map/all_to_all | solution.py:810
  31.1 30.3 %copy-start.2 = (bf16[32,128,192]{2,1,0:T(8,128)(2,1)S(1)}, bf16[32,128,192]{2,1,0:T(8,128)(2,1)}, u32[]{:S(2)}) copy-start(bf16[32,128,192]{2,1,0:T(8,128)(2,1)} %get-tuple-element.46.gate_ref) | copy-start | bytes 4718596
  65.1 11.2 %collective-permute-start.4 = (bf16[128,192]{1,0:T(8,128)(2,1)S(1)}, bf16[128,192]{1,0:T(8,128)(2,1)S(1)}, u32[]{:S(2)}, u32[]{:S(2)}) collective-permute-start(bf16[128,192]{1,0:T(8,128)(2,1)S(1)} %get-tuple-element.49), channel_id=1, source_target_pairs={{0,8},{8,16},{16,24},{24,0},{1,9},{9,17},{17,25},{25,1},{2,10},{10... | collective-permute-start | bytes 147464 | tf_op jit(solution)/shard_map/ppermute | solution.py:801
  66.0 10.3 %collective-permute-start.5 = (bf16[128,192]{1,0:T(8,128)(2,1)S(1)}, bf16[128,192]{1,0:T(8,128)(2,1)S(1)}, u32[]{:S(2)}, u32[]{:S(2)}) collective-permute-start(bf16[128,192]{1,0:T(8,128)(2,1)S(1)} %get-tuple-element.50), channel_id=1, source_target_pairs={{0,24},{8,0},{16,8},{24,16},{1,25},{9,1},{17,9},{25,17},{2,26},{10... | collective-permute-start | bytes 147464 | tf_op jit(solution)/shard_map/ppermute | solution.py:801
  68.0 8.2 %collective-permute-start.6 = (bf16[32,192]{1,0:T(8,128)(2,1)S(1)}, bf16[32,192]{1,0:T(8,128)(2,1)S(1)}, u32[]{:S(2)}, u32[]{:S(2)}) collective-permute-start(bf16[32,192]{1,0:T(8,128)(2,1)S(1)} %get-tuple-element.51), channel_id=1, source_target_pairs={{0,1},{1,2},{2,3},{3,4},{4,5},{5,6},{6,7},{7,0},{8,9},{9,10},{10,1... | collective-permute-start | bytes 36872 | tf_op jit(solution)/shard_map/ppermute | solution.py:801
  68.2 8.0 %collective-permute-start.7 = (bf16[32,192]{1,0:T(8,128)(2,1)S(1)}, bf16[32,192]{1,0:T(8,128)(2,1)S(1)}, u32[]{:S(2)}, u32[]{:S(2)}) collective-permute-start(bf16[32,192]{1,0:T(8,128)(2,1)S(1)} %get-tuple-element.52), channel_id=1, source_target_pairs={{0,7},{1,0},{2,1},{3,2},{4,3},{5,4},{6,5},{7,6},{8,15},{9,8},{10,9... | collective-permute-start | bytes 36872 | tf_op jit(solution)/shard_map/ppermute | solution.py:801

commit v6 on v5

--- a/solution.py
+++ b/solution.py
@@ -354,11 +354,16 @@
     return jnp.sum(jnp.where(k % capacity == c, both, 0.0), axis=0, keepdims=True)
 
 
+def slope(pre):
+    sg = 0.5 * jnp.tanh(0.5 * pre) + 0.5
+    return sg * (1.0 + pre * (1.0 - sg))
+
+
 def sample_kernel(
-    cap, y_ref, xs_ref, w_ref, asked_ref, top_ref, bot_ref, left_ref, right_ref, ans_hbm, gate_hbm, spots_hbm,
-    field, fix, edge, pack, gate_ref, ans_ref, spots_ref, sem,
+    cap, y_ref, xs_ref, w_ref, asked_ref, top_ref, bot_ref, left_ref, right_ref, ans_hbm, pre_hbm, spots_hbm,
+    field, fix, edge, pack, pre_ref, ans_ref, spots_ref, sem,
 ):
-    rows, cols, ch = gate_ref.shape
+    rows, cols, ch = pre_ref.shape
     regions = ans_ref.shape[0]
     slots = regions * cap
     half = cap // 2
@@ -370,22 +375,22 @@
 
     def gates(r, pre):
         pre = add_sides(pre, fix, r)
-        sg = 0.5 * jnp.tanh(0.5 * pre) + 0.5
-        field[pl.ds(r * cols, cols), :] = (xs_ref[r + 1, :, :ch].astype(F32) + pre * sg).astype(BF16)
-        gate_ref[r] = (sg * (1.0 + pre * (1.0 - sg))).astype(BF16)
+        half = 0.5 * pre
+        field[pl.ds(r * cols, cols), :] = (xs_ref[r + 1, :, :ch].astype(F32) + half + half * jnp.tanh(half)).astype(BF16)
+        pre_ref[r] = pre.astype(BF16)
 
     def inner(r, carry):
         gates(r, y_ref[r])
         return carry
 
     gates(0, y_ref[0] + edge[0])
-    lax.fori_loop(1, rows - 1, inner, 0)
+    lax.fori_loop(1, rows - 1, inner, 0, unroll=6 if rows % 6 == 2 else 1)
     gates(rows - 1, y_ref[rows - 1] + edge[1])
 
     asked = asked_ref[...].astype(F32)
     spots_ref[...] = 256.0 * asked[:, 0, :] + asked[:, 1, :]
-    gate_out = pltpu.make_async_copy(gate_ref, gate_hbm, sem.at[0])
-    gate_out.start()
+    pre_out = pltpu.make_async_copy(pre_ref, pre_hbm, sem.at[0])
+    pre_out.start()
     spots_out = pltpu.make_async_copy(spots_ref, spots_hbm, sem.at[2])
     spots_out.start()
     spot = spots_column(spots_ref[...], slots)
@@ -404,15 +409,15 @@
         pack[t, 0:cap, :] = total[at : at + cap, :128]
         pack[t, cap : cap + half, 0 : ch - 128] = total[at : at + half, 128:]
         pack[t, cap : cap + half, 64 : 64 + ch - 128] = total[at + half : at + cap, 128:]
-    first, final = gate_ref[0].astype(F32), gate_ref[rows - 1].astype(F32)
-    mine = corner_tile([final[cols - 1 :], final[0:1], first[cols - 1 :], first[0:1]])
+    first, final = pre_ref[0].astype(F32), pre_ref[rows - 1].astype(F32)
+    mine = corner_tile([slope(v) for v in (final[cols - 1 :], final[0:1], first[cols - 1 :], first[0:1])])
     for k in range(6):
         pack[:, cap + half + k, :] = jnp.broadcast_to(mine[k], (regions, 128))
     ans_ref[...] = pack[...].astype(BF16)
     ans_out = pltpu.make_async_copy(ans_ref, ans_hbm, sem.at[1])
     ans_out.start()
     spots_out.wait()
-    gate_out.wait()
+    pre_out.wait()
     ans_out.wait()
 
 
@@ -503,11 +508,11 @@
     corner_ref[...] = jnp.concatenate(corners + [jnp.zeros((4, ch), F32)], axis=0)
 
 
-def spread(spots, incoming, gates, gate, cap, block=4):
+def spread(spots, incoming, gates, gate, cap):
     rows, cols, ch = gate.shape
     slots = incoming.shape[0] * cap
     return pl.pallas_call(
-        functools.partial(spread_kernel, cap, block),
+        functools.partial(spread_kernel, cap, rows),
         out_shape=(
             SDS(gate.shape, F32),
             SDS((rows + 2, cols, up(ch, 128)), BF16),
@@ -577,8 +582,10 @@
 
 def prepare_kernel(
     cap, tile, n_lon, live_ref, route_ref, spot_ref, near_ref, count_ref, bias_ref, obs_ref, mask_ref, w_ref,
-    from_ref, bias_out, part_ref, index_ref,
+    pre_hbm, from_ref, bias_out, part_ref, index_ref, gate_hbm, pre_ref, gate_ref, sem,
 ):
+    fetch = pltpu.make_async_copy(pre_hbm, pre_ref, sem.at[0])
+    fetch.start()
     packed, stations = from_ref.shape[0], index_ref.shape[0]
     features = obs_ref.shape[1]
     deep = slab_rows(cap)
@@ -660,8 +667,23 @@
         mask.astype(BF16), w_ref[:, features : 2 * features]
     )
 
-
-def prepare(route, spot, near, count, bias, live, obs, mask, w_in, regions, cap, tile, n_lon):
+    fetch.wait()
+    size = rows // CHUNKS
+    stores = []
+    for k in range(CHUNKS):
+        def gates(r, carry):
+            gate_ref[r] = slope(pre_ref[r].astype(F32)).astype(BF16)
+            return carry
+
+        lax.fori_loop(k * size, (k + 1) * size, gates, 0, unroll=2)
+        at = pl.ds(k * size, size)
+        stores.append(pltpu.make_async_copy(gate_ref.at[at], gate_hbm.at[at], sem.at[1 + k]))
+        stores[-1].start()
+    for store in stores:
+        store.wait()
+
+
+def prepare(route, spot, near, count, bias, live, obs, mask, w_in, pre, regions, cap, tile, n_lon):
     stations = obs.shape[0]
     packed = regions * slab_rows(cap)
     return pl.pallas_call(
@@ -671,11 +693,13 @@
             SDS((stations, stations), F32),
             SDS((stations, w_in.shape[0]), F32),
             SDS((stations, 128), F32),
+            pltpu.HBM(pre.shape, BF16),
         ),
-        in_specs=SCALARS + whole(8),
-        out_specs=tuple(whole(4)),
+        in_specs=SCALARS + whole(8) + in_hbm(1),
+        out_specs=tuple(whole(4) + in_hbm(1)),
+        scratch_shapes=[VMEM(pre.shape, BF16), VMEM(pre.shape, BF16), pltpu.SemaphoreType.DMA((1 + CHUNKS,))],
         name="prepare",
-    )(live, route, spot, near, count.reshape(1, -1), bias, obs, mask, w_in)
+    )(live, route, spot, near, count.reshape(1, -1), bias, obs, mask, w_in, hbm(pre))
 
 
 def station_kernel(cap, live_ref, ans_ref, *refs):
@@ -841,10 +865,10 @@
     borders = halo(top, bot, *side_columns(x_t))
     asked, x_in = lax.optimization_barrier((asked, x_t))
     y, xs = conv_core(x_in, conv_weight)
-    answer, gate, spots = sample(y, xs, conv_weight, asked, *borders, cap)
+    answer, pre, spots = sample(y, xs, conv_weight, asked, *borders, cap)
     answer = exchange(answer)
-    prepared = prepare(
-        route, spot, neighbours.T, neighbour_count, edge_bias.T, live_count, observed, hidden_mask, w_in,
+    *prepared, gate = prepare(
+        route, spot, neighbours.T, neighbour_count, edge_bias.T, live_count, observed, hidden_mask, w_in, pre,
         regions, cap, tile, n_lon,
     )
     predicted, outgoing, gates = stations_pass(

time: 79.3 us -> 77.4 us (0.976)
  waiting for transfers between devices: 5.36 us -> 2.66 us
  Pallas kernels: 34.7 us -> 35.6 us
    pallas_call x1, Pallas kernels: 3.67 us -> 6.52 us  [prepare(): pl.pallas_call(functools.partial(prepare_kernel, cap, tile, n_lon), out_s...]
    all_to_all x2, waiting for transfers between devices: 5.34 us -> 2.64 us  [exchange(): return lax.all_to_all(x, AXES, split_axis=0, concat_axis=0, tiled=True)]
    pallas_call x1, Pallas kernels: 3.68 us -> 2.48 us  [spread(): pl.pallas_call(functools.partial(spread_kernel, cap, rows), out_shape=(SD...]
    pallas_call x1, Pallas kernels: 5.66 us -> 4.85 us  [sample(): pl.pallas_call(functools.partial(sample_kernel, cap), out_shape=(pltpu.HB...]
  transfers between devices with their start and end apart: 10 -> 10, of which waited for: 1 -> 1; matrix products, arithmetic and copies ran while one was open for 0% -> 0% of each run, Pallas kernels for 17% -> 21%
where the time goes in v6:
time: 77.4 us; the launch traced here: 76.9 us
  Pallas kernels  35.6 us (46%)
  starting transfers between devices  23.7 us (31%)
  blocking collectives  13.3 us (17%)
  waiting for transfers between devices  2.66 us (3%)
  between operations  1.62 us (2%)
    all_to_all x1, blocking collectives, exchange(): return lax.all_to_all(x, AXES, split_axis=0, concat_axis=0, tiled=True)  13.3 us
    ppermute x8, starting transfers between devices, shift(): return lax.ppermute(x, axis, [(i, (i + step) % n) for i in range(n)])  13.1 us
    all_to_all x2, starting transfers between devices, exchange(): return lax.all_to_all(x, AXES, split_axis=0, concat_axis=0, tiled=True)  10.7 us
    pallas_call x1, Pallas kernels, stations_pass(): pl.pallas_call(functools.partial(station_kernel, cap), out_shape=outs, in...  7.18 us
    pallas_call x1, Pallas kernels, prepare(): pl.pallas_call(functools.partial(prepare_kernel, cap, tile, n_lon), out_s...  6.52 us
    pallas_call x1, Pallas kernels, sample(): pl.pallas_call(functools.partial(sample_kernel, cap), out_shape=(pltpu.HB...  4.85 us
    pallas_call x1, Pallas kernels, conv_back(): pl.pallas_call(conv_back_kernel, out_shape=SDS(add.shape, F32), in_specs=...  4.64 us
    pallas_call x1, Pallas kernels, conv_core(): pl.pallas_call(conv_core_kernel, out_shape=(SDS((rows, cols, ch), F32), S...  4.31 us
  transfers between devices with their start and end apart: 10, of which 1 were waited for; matrix products, arithmetic and copies ran while one was open for 0% of the time, Pallas kernels for 21%

profile of v6, /device:TPU:0, one launch (start us, length us, event | category | flops | bytes accessed | tf_op | source)
XLA Modules:
  0.0 76.9 jit_solution(5047916977206169769)
XLA Ops:
  0.6 0.0 copy-start.1
  0.6 0.0 copy-start
  0.6 2.3 %intro.1 = (bf16[32,8,128]{2,1,0:T(8,128)(2,1)}, bf16[128,192]{1,0:T(8,128)(2,1)S(1)}, bf16[128,192]{1,0:T(8,128)(2,1)S(1)}) custom-call(s32[1,256]{1,0:T(1,128)} %bitcast.18, s32[1,256]{1,0:T(1,128)} %bitcast.20, bf16[32,192,128]{2,1,0:T(8,128)(2,1)} %bitcast.10), custom_call_target="tpu_custom_call" | custom-call | tf_op jit(solution)/shard_map/intro/pallas_call | solution.py:156
  2.9 7.3 %all-to-all-start = ((bf16[32,8,128]{2,1,0:T(8,128)(2,1)}), bf16[32,8,128]{2,1,0:T(8,128)(2,1)S(1)}, u32[]{:S(2)}, u32[]{:S(2)}) async-start(bf16[32,8,128]{2,1,0:T(8,128)(2,1)} %get-tuple-element.29), calls=%async_computation | async-start | bytes 131072 | tf_op jit(solution)/shard_map/all_to_all | solution.py:834
  10.3 1.8 %collective-permute-start = (bf16[128,192]{1,0:T(8,128)(2,1)S(1)}, bf16[128,192]{1,0:T(8,128)(2,1)S(1)}, u32[]{:S(2)}, u32[]{:S(2)}) collective-permute-start(bf16[128,192]{1,0:T(8,128)(2,1)S(1)} %get-tuple-element.34), channel_id=1, source_target_pairs={{0,8},{8,16},{16,24},{24,0},{1,9},{9,17},{17,25},{25,1},{2,10},{10... | collective-permute-start | bytes 147464 | tf_op jit(solution)/shard_map/ppermute | solution.py:825
  12.1 1.2 %collective-permute-start.1 = (bf16[128,192]{1,0:T(8,128)(2,1)S(1)}, bf16[128,192]{1,0:T(8,128)(2,1)S(1)}, u32[]{:S(2)}, u32[]{:S(2)}) collective-permute-start(bf16[128,192]{1,0:T(8,128)(2,1)S(1)} %get-tuple-element.35), channel_id=1, source_target_pairs={{0,24},{8,0},{16,8},{24,16},{1,25},{9,1},{17,9},{25,17},{2,26},{10... | collective-permute-start | bytes 147464 | tf_op jit(solution)/shard_map/ppermute | solution.py:825
  13.2 0.0 copy-done.1
  13.2 0.9 %sides.1 = (bf16[32,192]{1,0:T(8,128)(2,1)S(1)}, bf16[32,192]{1,0:T(8,128)(2,1)S(1)}) custom-call(bf16[32,192,128]{2,1,0:T(8,128)(2,1)S(1)} %bitcast.11), custom_call_target="tpu_custom_call" | custom-call | tf_op jit(solution)/shard_map/sides/pallas_call | solution.py:184
  14.1 0.0 collective-permute-start.2
  14.2 3.6 %collective-permute-start.3 = (bf16[32,192]{1,0:T(8,128)(2,1)S(1)}, bf16[32,192]{1,0:T(8,128)(2,1)S(1)}, u32[]{:S(2)}, u32[]{:S(2)}) collective-permute-start(bf16[32,192]{1,0:T(8,128)(2,1)S(1)} %get-tuple-element.37), channel_id=1, source_target_pairs={{0,7},{1,0},{2,1},{3,2},{4,3},{5,4},{6,5},{7,6},{8,15},{9,8},{10,9... | collective-permute-start | bytes 36872 | tf_op jit(solution)/shard_map/ppermute | solution.py:825
  17.7 0.0 all-to-all-done.asked_ref
  17.7 0.0 copy-done
  17.7 4.3 %conv_core.1 = (f32[32,128,192]{2,1,0:T(8,128)S(1)}, bf16[34,128,256]{2,1,0:T(8,128)(2,1)S(1)}) custom-call(bf16[32,192,128]{2,1,0:T(8,128)(2,1)S(1)} %bitcast.12, bf16[9,192,192]{2,1,0:T(8,128)(2,1)S(1)} %copy-done), custom_call_target="tpu_custom_call" | custom-call | tf_op jit(solution)/shard_map/conv_core/pallas_call | solution.py:254
  22.0 0.0 collective-permute-done.2.left_ref
  22.0 0.0 collective-permute-done.3.right_ref
  22.1 0.0 collective-permute-done.top_ref
  22.1 0.0 collective-permute-done.1.bot_ref
  22.1 4.9 %sample.1 = (bf16[32,32,128]{2,1,0:T(8,128)(2,1)}, bf16[32,128,192]{2,1,0:T(8,128)(2,1)}, f32[32,128]{1,0:T(8,128)}) custom-call(f32[32,128,192]{2,1,0:T(8,128)S(1)} %get-tuple-element.31.y_ref, bf16[34,128,256]{2,1,0:T(8,128)(2,1)S(1)} %get-tuple-element.32.xs_ref, bf16[9,192,192]{2,1,0:T(8,128)(2,1)S(1)} %copy-done, ...), custom_call_target="tpu_custom_call" | custom-call | tf_op jit(solution)/shard_map/sample/pallas_call | solution.py:428
  26.9 3.3 %all-to-all-start.1 = ((bf16[32,32,128]{2,1,0:T(8,128)(2,1)}), bf16[32,32,128]{2,1,0:T(8,128)(2,1)S(1)}, u32[]{:S(2)}, u32[]{:S(2)}) async-start(bf16[32,32,128]{2,1,0:T(8,128)(2,1)} %get-tuple-element.38), calls=%async_computation.1 | async-start | bytes 524288 | tf_op jit(solution)/shard_map/all_to_all | solution.py:834
  30.9 6.5 %prepare.1 = (bf16[1024,768]{1,0:T(8,128)(2,1)}, f32[256,256]{1,0:T(8,128)}, f32[256,192]{1,0:T(8,128)}, f32[256,128]{1,0:T(8,128)}, bf16[32,128,192]{2,1,0:T(8,128)(2,1)}) custom-call(s32[1]{0:T(128)S(6)} %copy.18.live_ref, s32[1,256]{1,0:T(1,128)} %bitcast.19, s32[1,256]{1,0:T(1,128)} %bitcast.21, s32[16,256]{1,0:T(8,128)} %bitcast.16, s32[1,256]{1,0:T(1,128)} %bitcast.24, ...), custom_call_target="tpu_custom_call" | custom-call | tf_op jit(solution)/shard_map/prepare/pallas_call | solution.py:689
  37.5 0.0 copy-start.2
  37.5 2.6 %all-to-all-done.1.ans_ref = bf16[32,32,128]{2,1,0:T(8,128)(2,1)S(1)} async-done(((bf16[32,32,128]{2,1,0:T(8,128)(2,1)}), bf16[32,32,128]{2,1,0:T(8,128)(2,1)S(1)}, u32[]{:S(2)}, u32[]{:S(2)}) %all-to-all-start.1) | async-done | bytes 262176 | tf_op jit(solution)/shard_map/all_to_all | solution.py:834
  40.1 7.2 %stations.1 = (f32[256,128]{1,0:T(8,128)}, bf16[32,32,128]{2,1,0:T(8,128)(2,1)}, f32[8,192]{1,0:T(8,128)}) custom-call(s32[1]{0:T(128)S(6)} %copy.18.live_ref, bf16[32,32,128]{2,1,0:T(8,128)(2,1)S(1)} %all-to-all-done.1.ans_ref, f32[256,128]{1,0:T(8,128)} %get-tuple-element.40.refs_0_, f32[256,192]{1,0:T(8,128)} %get-tuple-element.41.refs_1_, ...), custom_call_target="tpu_custom_call" | custom-call | tf_op jit(solution)/shard_map/stations/pallas_call | solution.py:806
  47.3 13.3 %all_to_all.15.inc_hbm = bf16[32,32,128]{2,1,0:T(8,128)(2,1)} all-to-all(bf16[32,32,128]{2,1,0:T(8,128)(2,1)} %get-tuple-element.46), channel_id=1, replica_groups=mesh['lat'=4,'lon'=8] {'lat','lon'}, dimensions={0} | all-to-all | bytes 524288 | tf_op jit(solution)/shard_map/all_to_all | solution.py:834
  60.6 0.0 copy-done.2
  60.6 2.5 %spread.1 = (f32[32,128,192]{2,1,0:T(8,128)S(1)}, bf16[34,128,256]{2,1,0:T(8,128)(2,1)S(1)}, bf16[128,192]{1,0:T(8,128)(2,1)S(1)}, bf16[128,192]{1,0:T(8,128)(2,...) custom-call(f32[32,128]{1,0:T(8,128)} %get-tuple-element.45.spots_hbm, ...), custom_call_target="tpu_custom_call" | custom-call | tf_op jit(solution)/shard_map/spread/pallas_call | solution.py:514
  63.1 0.9 %collective-permute-start.4 = (bf16[128,192]{1,0:T(8,128)(2,1)S(1)}, bf16[128,192]{1,0:T(8,128)(2,1)S(1)}, u32[]{:S(2)}, u32[]{:S(2)}) collective-permute-start(bf16[128,192]{1,0:T(8,128)(2,1)S(1)} %get-tuple-element.51), channel_id=1, source_target_pairs={{0,8},{8,16},{16,24},{24,0},{1,9},{9,17},{17,25},{25,1},{2,10},{10... | collective-permute-start | bytes 147464 | tf_op jit(solution)/shard_map/ppermute | solution.py:825
  64.0 2.1 %collective-permute-start.5 = (bf16[128,192]{1,0:T(8,128)(2,1)S(1)}, bf16[128,192]{1,0:T(8,128)(2,1)S(1)}, u32[]{:S(2)}, u32[]{:S(2)}) collective-permute-start(bf16[128,192]{1,0:T(8,128)(2,1)S(1)} %get-tuple-element.52), channel_id=1, source_target_pairs={{0,24},{8,0},{16,8},{24,16},{1,25},{9,1},{17,9},{25,17},{2,26},{10... | collective-permute-start | bytes 147464 | tf_op jit(solution)/shard_map/ppermute | solution.py:825
  66.1 0.2 collective-permute-start.6
  66.3 3.4 %collective-permute-start.7 = (bf16[32,192]{1,0:T(8,128)(2,1)S(1)}, bf16[32,192]{1,0:T(8,128)(2,1)S(1)}, u32[]{:S(2)}, u32[]{:S(2)}) collective-permute-start(bf16[32,192]{1,0:T(8,128)(2,1)S(1)} %get-tuple-element.54), channel_id=1, source_target_pairs={{0,7},{1,0},{2,1},{3,2},{4,3},{5,4},{6,5},{7,6},{8,15},{9,8},{10,9... | collective-permute-start | bytes 36872 | tf_op jit(solution)/shard_map/ppermute | solution.py:825
  69.6 4.6 %conv_back.1.g_ref = f32[32,128,192]{2,1,0:T(8,128)S(1)} custom-call(bf16[34,128,256]{2,1,0:T(8,128)(2,1)S(1)} %get-tuple-element.49.xs_ref, bf16[9,192,192]{2,1,0:T(8,128)(2,1)S(1)} %copy-done, f32[32,128,192]{2,1,0:T(8,128)S(1)} %get-tuple-element.50.add_ref), custom_call_target="tpu_custom_call" | custom-call | tf_op jit(solution)/shard_map/conv_back/pallas_call | solution.py:269
  74.3 0.0 collective-permute-done.6.left_ref
  74.3 0.0 collective-permute-done.7.right_ref
  74.3 0.0 collective-permute-done.4.top_ref
  74.3 0.0 collective-permute-done.5.bot_ref
  74.3 2.4 %finish.1 = f32[32,192,128]{2,1,0:T(8,128)} custom-call(f32[32,128,192]{2,1,0:T(8,128)S(1)} %conv_back.1.g_ref, bf16[9,192,192]{2,1,0:T(8,128)(2,1)S(1)} %copy-done, bf16[128,192]{1,0:T(8,128)(2,1)S(1)} %collective-permute-done.4.top_ref, bf16[128,192]{1,0:T(8,128)(2,1)S(1)} %collective-permute-done.5.bot_ref, ...), custom_call_target="tpu_custom_call" | custom-call | tf_op jit(solution)/shard_map/finish/pallas_call | solution.py:568
Async XLA Ops:
  0.6 12.6 %copy-start.1 = (bf16[32,128,192]{1,2,0:T(8,128)(2,1)S(1)}, bf16[32,128,192]{1,2,0:T(8,128)(2,1)}, u32[]{:S(2)}) copy-start(bf16[32,128,192]{1,2,0:T(8,128)(2,1)} %param.16) | copy-start | bytes 4718596
  0.6 17.1 %copy-start = (bf16[9,192,192]{2,1,0:T(8,128)(2,1)S(1)}, bf16[9,192,192]{2,1,0:T(8,128)(2,1)}, u32[]{:S(2)}) copy-start(bf16[9,192,192]{2,1,0:T(8,128)(2,1)} %w_ref.7) | copy-start | bytes 1990660
  2.9 14.8 %all-to-all-start = ((bf16[32,8,128]{2,1,0:T(8,128)(2,1)}), bf16[32,8,128]{2,1,0:T(8,128)(2,1)S(1)}, u32[]{:S(2)}, u32[]{:S(2)}) async-start(bf16[32,8,128]{2,1,0:T(8,128)(2,1)} %get-tuple-element.29), calls=%async_computation | async-start | bytes 131072 | tf_op jit(solution)/shard_map/all_to_all | solution.py:834
  10.3 11.8 %collective-permute-start = (bf16[128,192]{1,0:T(8,128)(2,1)S(1)}, bf16[128,192]{1,0:T(8,128)(2,1)S(1)}, u32[]{:S(2)}, u32[]{:S(2)}) collective-permute-start(bf16[128,192]{1,0:T(8,128)(2,1)S(1)} %get-tuple-element.34), channel_id=1, source_target_pairs={{0,8},{8,16},{16,24},{24,0},{1,9},{9,17},{17,25},{25,1},{2,10},{10... | collective-permute-start | bytes 147464 | tf_op jit(solution)/shard_map/ppermute | solution.py:825
  12.1 10.0 %collective-permute-start.1 = (bf16[128,192]{1,0:T(8,128)(2,1)S(1)}, bf16[128,192]{1,0:T(8,128)(2,1)S(1)}, u32[]{:S(2)}, u32[]{:S(2)}) collective-permute-start(bf16[128,192]{1,0:T(8,128)(2,1)S(1)} %get-tuple-element.35), channel_id=1, source_target_pairs={{0,24},{8,0},{16,8},{24,16},{1,25},{9,1},{17,9},{25,17},{2,26},{10... | collective-permute-start | bytes 147464 | tf_op jit(solution)/shard_map/ppermute | solution.py:825
  14.1 7.9 %collective-permute-start.2 = (bf16[32,192]{1,0:T(8,128)(2,1)S(1)}, bf16[32,192]{1,0:T(8,128)(2,1)S(1)}, u32[]{:S(2)}, u32[]{:S(2)}) collective-permute-start(bf16[32,192]{1,0:T(8,128)(2,1)S(1)} %get-tuple-element.36), channel_id=1, source_target_pairs={{0,1},{1,2},{2,3},{3,4},{4,5},{5,6},{6,7},{7,0},{8,9},{9,10},{10,1... | collective-permute-start | bytes 36872 | tf_op jit(solution)/shard_map/ppermute | solution.py:825
  14.2 7.9 %collective-permute-start.3 = (bf16[32,192]{1,0:T(8,128)(2,1)S(1)}, bf16[32,192]{1,0:T(8,128)(2,1)S(1)}, u32[]{:S(2)}, u32[]{:S(2)}) collective-permute-start(bf16[32,192]{1,0:T(8,128)(2,1)S(1)} %get-tuple-element.37), channel_id=1, source_target_pairs={{0,7},{1,0},{2,1},{3,2},{4,3},{5,4},{6,5},{7,6},{8,15},{9,8},{10,9... | collective-permute-start | bytes 36872 | tf_op jit(solution)/shard_map/ppermute | solution.py:825
  26.9 13.2 %all-to-all-start.1 = ((bf16[32,32,128]{2,1,0:T(8,128)(2,1)}), bf16[32,32,128]{2,1,0:T(8,128)(2,1)S(1)}, u32[]{:S(2)}, u32[]{:S(2)}) async-start(bf16[32,32,128]{2,1,0:T(8,128)(2,1)} %get-tuple-element.38), calls=%async_computation.1 | async-start | bytes 524288 | tf_op jit(solution)/shard_map/all_to_all | solution.py:834
  37.5 23.1 %copy-start.2 = (bf16[32,128,192]{2,1,0:T(8,128)(2,1)S(1)}, bf16[32,128,192]{2,1,0:T(8,128)(2,1)}, u32[]{:S(2)}) copy-start(bf16[32,128,192]{2,1,0:T(8,128)(2,1)} %get-tuple-element.48.gate_ref) | copy-start | bytes 4718596
  63.1 11.2 %collective-permute-start.4 = (bf16[128,192]{1,0:T(8,128)(2,1)S(1)}, bf16[128,192]{1,0:T(8,128)(2,1)S(1)}, u32[]{:S(2)}, u32[]{:S(2)}) collective-permute-start(bf16[128,192]{1,0:T(8,128)(2,1)S(1)} %get-tuple-element.51), channel_id=1, source_target_pairs={{0,8},{8,16},{16,24},{24,0},{1,9},{9,17},{17,25},{25,1},{2,10},{10... | collective-permute-start | bytes 147464 | tf_op jit(solution)/shard_map/ppermute | solution.py:825
  64.0 10.3 %collective-permute-start.5 = (bf16[128,192]{1,0:T(8,128)(2,1)S(1)}, bf16[128,192]{1,0:T(8,128)(2,1)S(1)}, u32[]{:S(2)}, u32[]{:S(2)}) collective-permute-start(bf16[128,192]{1,0:T(8,128)(2,1)S(1)} %get-tuple-element.52), channel_id=1, source_target_pairs={{0,24},{8,0},{16,8},{24,16},{1,25},{9,1},{17,9},{25,17},{2,26},{10... | collective-permute-start | bytes 147464 | tf_op jit(solution)/shard_map/ppermute | solution.py:825
  66.1 8.2 %collective-permute-start.6 = (bf16[32,192]{1,0:T(8,128)(2,1)S(1)}, bf16[32,192]{1,0:T(8,128)(2,1)S(1)}, u32[]{:S(2)}, u32[]{:S(2)}) collective-permute-start(bf16[32,192]{1,0:T(8,128)(2,1)S(1)} %get-tuple-element.53), channel_id=1, source_target_pairs={{0,1},{1,2},{2,3},{3,4},{4,5},{5,6},{6,7},{7,0},{8,9},{9,10},{10,1... | collective-permute-start | bytes 36872 | tf_op jit(solution)/shard_map/ppermute | solution.py:825
  66.3 8.0 %collective-permute-start.7 = (bf16[32,192]{1,0:T(8,128)(2,1)S(1)}, bf16[32,192]{1,0:T(8,128)(2,1)S(1)}, u32[]{:S(2)}, u32[]{:S(2)}) collective-permute-start(bf16[32,192]{1,0:T(8,128)(2,1)S(1)} %get-tuple-element.54), channel_id=1, source_target_pairs={{0,7},{1,0},{2,1},{3,2},{4,3},{5,4},{6,5},{7,6},{8,15},{9,8},{10,9... | collective-permute-start | bytes 36872 | tf_op jit(solution)/shard_map/ppermute | solution.py:825

commit v7 on v6

--- a/solution.py
+++ b/solution.py
@@ -582,11 +582,11 @@
 
 def prepare_kernel(
     cap, tile, n_lon, live_ref, route_ref, spot_ref, near_ref, count_ref, bias_ref, obs_ref, mask_ref, w_ref,
-    pre_hbm, from_ref, bias_out, part_ref, index_ref, gate_hbm, pre_ref, gate_ref, sem,
+    pre_hbm, from_ref, bias_out, part_ref, gate_hbm, pre_ref, gate_ref, sem,
 ):
     fetch = pltpu.make_async_copy(pre_hbm, pre_ref, sem.at[0])
     fetch.start()
-    packed, stations = from_ref.shape[0], index_ref.shape[0]
+    packed, stations = from_ref.shape[0], part_ref.shape[0]
     features = obs_ref.shape[1]
     deep = slab_rows(cap)
     regions = packed // deep
@@ -595,10 +595,10 @@
     route = route_ref[...]
     rank_col, rank_row, route_col = route_parts(route, up(regions, 128))
     upper = jnp.where(rank_col >= half, 1.0, 0.0)
-    lane = iota((stations, 128), 1)
+    lane = iota((stations, part_ref.shape[1] - w_ref.shape[0]), 1)
     main_at = route_col * deep + rank_col
     rest_at = route_col * deep + cap + rank_col - half * upper
-    index_ref[...] = jnp.where(lane == 0, main_at, jnp.where(lane == 1, rest_at, upper))
+    part_ref[:, w_ref.shape[0] :] = jnp.where(lane == 0, main_at, jnp.where(lane == 1, rest_at, upper))
 
     row, col, a, b = fine_cell(spot_ref[...].astype(F32), cols)
     share = []
@@ -663,7 +663,7 @@
     bias_out[...] = jnp.where(key == iota_f((stations, stations), 1), own_bias, table)
 
     mask = mask_ref[...].astype(F32)
-    part_ref[...] = nt((obs_ref[...] * (1.0 - mask)).astype(BF16), w_ref[:, :features]) + nt(
+    part_ref[:, : w_ref.shape[0]] = nt((obs_ref[...] * (1.0 - mask)).astype(BF16), w_ref[:, :features]) + nt(
         mask.astype(BF16), w_ref[:, features : 2 * features]
     )
 
@@ -691,35 +691,34 @@
         out_shape=(
             SDS((packed, 3 * stations), BF16),
             SDS((stations, stations), F32),
-            SDS((stations, w_in.shape[0]), F32),
-            SDS((stations, 128), F32),
+            SDS((stations, up(w_in.shape[0], 128)), F32),
             pltpu.HBM(pre.shape, BF16),
         ),
         in_specs=SCALARS + whole(8) + in_hbm(1),
-        out_specs=tuple(whole(4) + in_hbm(1)),
+        out_specs=tuple(whole(3) + in_hbm(1)),
         scratch_shapes=[VMEM(pre.shape, BF16), VMEM(pre.shape, BF16), pltpu.SemaphoreType.DMA((1 + CHUNKS,))],
         name="prepare",
     )(live, route, spot, near, count.reshape(1, -1), bias, obs, mask, w_in, hbm(pre))
 
 
 def station_kernel(cap, live_ref, ans_ref, *refs):
-    there, (pred_hbm, out_hbm, gates_hbm) = refs[:12], refs[12:15]
-    here = refs[15:27]
-    prob, d_qkv, pred_ref, out_ref, gates_ref, sem = refs[27:]
+    there, (pred_hbm, out_hbm, gates_hbm) = refs[:11], refs[11:14]
+    here = refs[14:25]
+    prob, d_qkv, pred_ref, out_ref, gates_ref, sem = refs[25:]
     fetches = [pltpu.make_async_copy(a, b, sem.at[k]) for k, (a, b) in enumerate(zip(there, here))]
-    for copy in fetches:
+    for copy in fetches[:10]:
         copy.start()
-    index_ref, part_ref, w_in, g1_ref, w_qkv, bias_ref, w_out, g2_ref, w_head, mask_ref, obs_ref, from_ref = here
+    part_ref, w_in, g1_ref, w_qkv, bias_ref, w_out, g2_ref, w_head, mask_ref, obs_ref, from_ref = here
     need = lambda first, last: [copy.wait() for copy in fetches[first:last]]
     size = out_ref.shape[0] // CHUNKS
     chunks = [pl.ds(k * size, size) for k in range(CHUNKS)]
     stores = [
-        pltpu.make_async_copy(a, b, sem.at[12 + k])
+        pltpu.make_async_copy(a, b, sem.at[11 + k])
         for k, (a, b) in enumerate(
             ((pred_ref, pred_hbm), *((out_ref.at[p], out_hbm.at[p]) for p in chunks), (gates_ref, gates_hbm))
         )
     ]
-    stations, ch = part_ref.shape
+    stations, ch = part_ref.shape[0], w_in.shape[0]
     packed = from_ref.shape[0]
     dim = ch // HEADS
     scale = 1.0 / math.sqrt(dim)
@@ -729,31 +728,37 @@
     base = cap + cap // 2
     gates_ref[...] = jnp.concatenate(near_corners(ans_ref, base) + [jnp.zeros((4, ch), F32)], axis=0)
     stores[-1].start()
-    need(0, 3)
+    need(0, 2)
+    fetches[10].start()
     at = iota_f((stations, packed), 1)
-    to = onehot(at == index_ref[:, 0:1])
-    to_rest = onehot(at == index_ref[:, 1:2])
+    to = onehot(at == part_ref[:, ch : ch + 1])
+    to_rest = onehot(at == part_ref[:, ch + 1 : ch + 2])
     flat = ans_ref[...].reshape(packed, 128)
     main = nn(to, flat).astype(BF16)
     rest = nn(to_rest, flat)
-    rest = jnp.where(index_ref[:, 2:3] > 0.0, pltpu.roll(rest, 64, 1), rest)[:, : ch - 128].astype(BF16)
-    embedded = part_ref[...] + nt(jnp.concatenate([main, rest], axis=1), w_in[:, below:])
+    rest = jnp.where(part_ref[:, ch + 2 : ch + 3] > 0.0, pltpu.roll(rest, 64, 1), rest)[:, : ch - 128].astype(BF16)
+    embedded = part_ref[:, :ch] + nt(jnp.concatenate([main, rest], axis=1), w_in[:, below:])
     r1 = lax.rsqrt(jnp.sum(embedded * embedded, axis=1, keepdims=True) * inv + EPS)
     unit1 = embedded * r1
-    need(3, 6)
+    need(2, 5)
     g1 = g1_ref[...]
     projected = nn((unit1 * g1).astype(BF16), w_qkv[...]).astype(BF16)
-    cut = lambda block, h: projected[:, block * ch + h * dim : block * ch + (h + 1) * dim]
-    need(6, 11)
+    query, key, value = projected[:, :ch], projected[:, ch : 2 * ch], projected[:, 2 * ch :]
+    lane = iota((1, ch), 1) // dim
+    apart = lambda v: jnp.concatenate([v * onehot(lane == h) for h in range(HEADS)], axis=0)
+    keys, values = apart(key), apart(value)
+    scores = nt(keys, query) * scale
+    need(5, 10)
     g2 = g2_ref[...]
-    residual = embedded
+    probs = []
     for h in range(HEADS):
-        score = nt(cut(1, h), cut(0, h)) * scale + bias_ref[...]
+        score = scores[h * stations : (h + 1) * stations] + bias_ref[...]
         weight = jnp.exp(score - jnp.max(score, axis=0, keepdims=True))
         p = weight * (1.0 / jnp.sum(weight, axis=0, keepdims=True))
         prob[h] = p
-        mixed = tn(p.astype(BF16), cut(2, h))
-        residual = residual + nn(mixed.astype(BF16), w_out[h * dim : (h + 1) * dim])
+        probs.append(p.astype(BF16))
+    mixed = tn(jnp.concatenate(probs, axis=0), values).astype(BF16)
+    residual = embedded + nn(mixed, w_out[...])
     r2 = lax.rsqrt(jnp.sum(residual * residual, axis=1, keepdims=True) * inv + EPS)
     unit2 = residual * r2
     alive = jnp.where(iota((stations, 1), 0) < live_ref[0], 1.0, 0.0)
@@ -765,15 +770,16 @@
     u2 = nt(d_pred.astype(BF16), w_head[...]).astype(BF16).astype(F32) * g2
     d_res = r2 * (u2 - unit2 * (jnp.sum(u2 * unit2, axis=1, keepdims=True) * inv))
     d_res_b = d_res.astype(BF16)
+    d_mixed = nt(d_res_b, w_out[...]).astype(BF16)
+    d_probs = nt(values, d_mixed)
+    d_scores = []
     for h in range(HEADS):
-        p = prob[h]
-        d_mixed = nt(d_res_b, w_out[h * dim : (h + 1) * dim]).astype(BF16)
-        d_p = nt(cut(2, h), d_mixed)
+        p, d_p = prob[h], d_probs[h * stations : (h + 1) * stations]
         d_score = p * (d_p - jnp.sum(p * d_p, axis=0, keepdims=True))
-        d_score = (d_score * scale).astype(BF16)
-        d_qkv[:, h * dim : (h + 1) * dim] = tn(d_score, cut(1, h)).astype(BF16)
-        d_qkv[:, ch + h * dim : ch + (h + 1) * dim] = nn(d_score, cut(0, h)).astype(BF16)
-        d_qkv[:, 2 * ch + h * dim : 2 * ch + (h + 1) * dim] = nn(p.astype(BF16), d_mixed).astype(BF16)
+        d_scores.append((d_score * scale).astype(BF16))
+    d_qkv[:, :ch] = tn(jnp.concatenate(d_scores, axis=0), keys).astype(BF16)
+    d_qkv[:, ch : 2 * ch] = nn(jnp.concatenate(d_scores, axis=1), apart(query)).astype(BF16)
+    d_qkv[:, 2 * ch :] = nn(jnp.concatenate(probs, axis=1), apart(d_mixed)).astype(BF16)
     u1 = nt(d_qkv[...], w_qkv[...]).astype(BF16).astype(F32) * g1
     d_emb = d_res + r1 * (u1 - unit1 * (jnp.sum(u1 * unit1, axis=1, keepdims=True) * inv))
     d_interp = nn(d_emb.astype(BF16), w_in[:, below:]).astype(BF16).astype(F32)
@@ -784,7 +790,7 @@
         jnp.concatenate([extra, blank], axis=1),
         jnp.concatenate([blank, extra], axis=1),
     ]
-    need(11, 12)
+    need(10, 11)
     taken = jnp.concatenate(parts, axis=0).astype(BF16)
     regions, deep, _ = out_ref.shape
     size = regions // CHUNKS
@@ -797,10 +803,10 @@
 
 
 def stations_pass(live, answer, prepared, obs, mask, w_in, g1, w_qkv, w_out, g2, w_head, cap):
-    outgoing, table, part, index = prepared
-    n, ch = part.shape
+    outgoing, table, part = prepared
+    n, ch = part.shape[0], w_in.shape[0]
     late = (
-        index, part, w_in, g1.reshape(1, -1), w_qkv, table, w_out, g2.reshape(1, -1), w_head, mask, obs, outgoing
+        part, w_in, g1.reshape(1, -1), w_qkv, table, w_out, g2.reshape(1, -1), w_head, mask, obs, outgoing
     )
     outs = (pltpu.HBM(obs.shape, F32), pltpu.HBM(answer.shape, BF16), pltpu.HBM((8, ch), F32))
     return pl.pallas_call(

time: 77.4 us -> 76.5 us (0.988)
  Pallas kernels: 35.6 us -> 34.7 us
    pallas_call x1, Pallas kernels: 7.18 us -> 6.27 us  [stations_pass(): pl.pallas_call(functools.partial(station_kernel, cap), out_shape=outs, in...]
  transfers between devices with their start and end apart: 10 -> 10, of which waited for: 1 -> 1; matrix products, arithmetic and copies ran while one was open for 0% -> 0% of each run, Pallas kernels for 21% -> 22%
where the time goes in v7:
time: 76.5 us; the launch traced here: 76 us
  Pallas kernels  34.7 us (45%)
  starting transfers between devices  23.7 us (31%)
  blocking collectives  13.3 us (17%)
  waiting for transfers between devices  2.63 us (3%)
  between operations  1.62 us (2%)
    all_to_all x1, blocking collectives, exchange(): return lax.all_to_all(x, AXES, split_axis=0, concat_axis=0, tiled=True)  13.3 us
    ppermute x8, starting transfers between devices, shift(): return lax.ppermute(x, axis, [(i, (i + step) % n) for i in range(n)])  13.1 us
    all_to_all x2, starting transfers between devices, exchange(): return lax.all_to_all(x, AXES, split_axis=0, concat_axis=0, tiled=True)  10.7 us
    pallas_call x1, Pallas kernels, prepare(): pl.pallas_call(functools.partial(prepare_kernel, cap, tile, n_lon), out_s...  6.55 us
    pallas_call x1, Pallas kernels, stations_pass(): pl.pallas_call(functools.partial(station_kernel, cap), out_shape=outs, in...  6.27 us
    pallas_call x1, Pallas kernels, sample(): pl.pallas_call(functools.partial(sample_kernel, cap), out_shape=(pltpu.HB...  4.85 us
    pallas_call x1, Pallas kernels, conv_back(): pl.pallas_call(conv_back_kernel, out_shape=SDS(add.shape, F32), in_specs=...  4.64 us
    pallas_call x1, Pallas kernels, conv_core(): pl.pallas_call(conv_core_kernel, out_shape=(SDS((rows, cols, ch), F32), S...  4.31 us
  transfers between devices with their start and end apart: 10, of which 1 were waited for; matrix products, arithmetic and copies ran while one was open for 0% of the time, Pallas kernels for 22%

profile of v7, /device:TPU:0, one launch (start us, length us, event | category | flops | bytes accessed | tf_op | source)
XLA Modules:
  0.0 76.0 jit_solution(8989644412918422474)
XLA Ops:
  0.6 0.0 copy-start.1
  0.6 0.0 copy-start
  0.6 2.3 %intro.1 = (bf16[32,8,128]{2,1,0:T(8,128)(2,1)}, bf16[128,192]{1,0:T(8,128)(2,1)S(1)}, bf16[128,192]{1,0:T(8,128)(2,1)S(1)}) custom-call(s32[1,256]{1,0:T(1,128)} %bitcast.18, s32[1,256]{1,0:T(1,128)} %bitcast.20, bf16[32,192,128]{2,1,0:T(8,128)(2,1)} %bitcast.10), custom_call_target="tpu_custom_call" | custom-call | tf_op jit(solution)/shard_map/intro/pallas_call | solution.py:156
  2.9 7.3 %all-to-all-start = ((bf16[32,8,128]{2,1,0:T(8,128)(2,1)}), bf16[32,8,128]{2,1,0:T(8,128)(2,1)S(1)}, u32[]{:S(2)}, u32[]{:S(2)}) async-start(bf16[32,8,128]{2,1,0:T(8,128)(2,1)} %get-tuple-element.28), calls=%async_computation | async-start | bytes 131072 | tf_op jit(solution)/shard_map/all_to_all | solution.py:840
  10.3 1.8 %collective-permute-start = (bf16[128,192]{1,0:T(8,128)(2,1)S(1)}, bf16[128,192]{1,0:T(8,128)(2,1)S(1)}, u32[]{:S(2)}, u32[]{:S(2)}) collective-permute-start(bf16[128,192]{1,0:T(8,128)(2,1)S(1)} %get-tuple-element.33), channel_id=1, source_target_pairs={{0,8},{8,16},{16,24},{24,0},{1,9},{9,17},{17,25},{25,1},{2,10},{10... | collective-permute-start | bytes 147464 | tf_op jit(solution)/shard_map/ppermute | solution.py:831
  12.1 1.2 %collective-permute-start.1 = (bf16[128,192]{1,0:T(8,128)(2,1)S(1)}, bf16[128,192]{1,0:T(8,128)(2,1)S(1)}, u32[]{:S(2)}, u32[]{:S(2)}) collective-permute-start(bf16[128,192]{1,0:T(8,128)(2,1)S(1)} %get-tuple-element.34), channel_id=1, source_target_pairs={{0,24},{8,0},{16,8},{24,16},{1,25},{9,1},{17,9},{25,17},{2,26},{10... | collective-permute-start | bytes 147464 | tf_op jit(solution)/shard_map/ppermute | solution.py:831
  13.2 0.0 copy-done.1
  13.2 0.9 %sides.1 = (bf16[32,192]{1,0:T(8,128)(2,1)S(1)}, bf16[32,192]{1,0:T(8,128)(2,1)S(1)}) custom-call(bf16[32,192,128]{2,1,0:T(8,128)(2,1)S(1)} %bitcast.11), custom_call_target="tpu_custom_call" | custom-call | tf_op jit(solution)/shard_map/sides/pallas_call | solution.py:184
  14.1 0.0 collective-permute-start.2
  14.2 3.6 %collective-permute-start.3 = (bf16[32,192]{1,0:T(8,128)(2,1)S(1)}, bf16[32,192]{1,0:T(8,128)(2,1)S(1)}, u32[]{:S(2)}, u32[]{:S(2)}) collective-permute-start(bf16[32,192]{1,0:T(8,128)(2,1)S(1)} %get-tuple-element.36), channel_id=1, source_target_pairs={{0,7},{1,0},{2,1},{3,2},{4,3},{5,4},{6,5},{7,6},{8,15},{9,8},{10,9... | collective-permute-start | bytes 36872 | tf_op jit(solution)/shard_map/ppermute | solution.py:831
  17.7 0.0 all-to-all-done.asked_ref
  17.7 0.0 copy-done
  17.7 4.3 %conv_core.1 = (f32[32,128,192]{2,1,0:T(8,128)S(1)}, bf16[34,128,256]{2,1,0:T(8,128)(2,1)S(1)}) custom-call(bf16[32,192,128]{2,1,0:T(8,128)(2,1)S(1)} %bitcast.12, bf16[9,192,192]{2,1,0:T(8,128)(2,1)S(1)} %copy-done), custom_call_target="tpu_custom_call" | custom-call | tf_op jit(solution)/shard_map/conv_core/pallas_call | solution.py:254
  22.0 0.0 collective-permute-done.2.left_ref
  22.0 0.0 collective-permute-done.3.right_ref
  22.1 0.0 collective-permute-done.top_ref
  22.1 0.0 collective-permute-done.1.bot_ref
  22.1 4.9 %sample.1 = (bf16[32,32,128]{2,1,0:T(8,128)(2,1)}, bf16[32,128,192]{2,1,0:T(8,128)(2,1)}, f32[32,128]{1,0:T(8,128)}) custom-call(f32[32,128,192]{2,1,0:T(8,128)S(1)} %get-tuple-element.30.y_ref, bf16[34,128,256]{2,1,0:T(8,128)(2,1)S(1)} %get-tuple-element.31.xs_ref, bf16[9,192,192]{2,1,0:T(8,128)(2,1)S(1)} %copy-done, ...), custom_call_target="tpu_custom_call" | custom-call | tf_op jit(solution)/shard_map/sample/pallas_call | solution.py:428
  26.9 3.3 %all-to-all-start.1 = ((bf16[32,32,128]{2,1,0:T(8,128)(2,1)}), bf16[32,32,128]{2,1,0:T(8,128)(2,1)S(1)}, u32[]{:S(2)}, u32[]{:S(2)}) async-start(bf16[32,32,128]{2,1,0:T(8,128)(2,1)} %get-tuple-element.37), calls=%async_computation.1 | async-start | bytes 524288 | tf_op jit(solution)/shard_map/all_to_all | solution.py:840
  30.9 6.5 %prepare.1 = (bf16[1024,768]{1,0:T(8,128)(2,1)}, f32[256,256]{1,0:T(8,128)}, f32[256,256]{1,0:T(8,128)}, bf16[32,128,192]{2,1,0:T(8,128)(2,1)}) custom-call(s32[1]{0:T(128)S(6)} %copy.18.live_ref, s32[1,256]{1,0:T(1,128)} %bitcast.19, s32[1,256]{1,0:T(1,128)} %bitcast.21, s32[16,256]{1,0:T(8,128)} %bitcast.16, s32[1,256]{1,0:T(1,128)} %bitcast.22, ...), custom_call_target="tpu_custom_call" | custom-call | tf_op jit(solution)/shard_map/prepare/pallas_call | solution.py:689
  37.5 0.0 copy-start.2
  37.5 2.6 %all-to-all-done.1.ans_ref = bf16[32,32,128]{2,1,0:T(8,128)(2,1)S(1)} async-done(((bf16[32,32,128]{2,1,0:T(8,128)(2,1)}), bf16[32,32,128]{2,1,0:T(8,128)(2,1)S(1)}, u32[]{:S(2)}, u32[]{:S(2)}) %all-to-all-start.1) | async-done | bytes 262176 | tf_op jit(solution)/shard_map/all_to_all | solution.py:840
  40.1 6.3 %stations.1 = (f32[256,128]{1,0:T(8,128)}, bf16[32,32,128]{2,1,0:T(8,128)(2,1)}, f32[8,192]{1,0:T(8,128)}) custom-call(s32[1]{0:T(128)S(6)} %copy.18.live_ref, bf16[32,32,128]{2,1,0:T(8,128)(2,1)S(1)} %all-to-all-done.1.ans_ref, f32[256,256]{1,0:T(8,128)} %get-tuple-element.39.refs_0_, bf16[192,448]{1,0:T(8,128)(2,1)} %bitcast.15, f32[1,192]{1,0:T(1,128)} %bitcast.23, ...), custom_call_target="tpu_custom_call" | custom-call | tf_op jit(solution)/shard_map/stations/pallas_call | solution.py:812
  46.4 13.3 %all_to_all.15.inc_hbm = bf16[32,32,128]{2,1,0:T(8,128)(2,1)} all-to-all(bf16[32,32,128]{2,1,0:T(8,128)(2,1)} %get-tuple-element.44), channel_id=1, replica_groups=mesh['lat'=4,'lon'=8] {'lat','lon'}, dimensions={0} | all-to-all | bytes 524288 | tf_op jit(solution)/shard_map/all_to_all | solution.py:840
  59.7 0.0 copy-done.2
  59.7 2.5 %spread.1 = (f32[32,128,192]{2,1,0:T(8,128)S(1)}, bf16[34,128,256]{2,1,0:T(8,128)(2,1)S(1)}, bf16[128,192]{1,0:T(8,128)(2,1)S(1)}, bf16[128,192]{1,0:T(8,128)(2,...) custom-call(f32[32,128]{1,0:T(8,128)} %get-tuple-element.43.spots_hbm, ...), custom_call_target="tpu_custom_call" | custom-call | tf_op jit(solution)/shard_map/spread/pallas_call | solution.py:514
  62.2 0.9 %collective-permute-start.4 = (bf16[128,192]{1,0:T(8,128)(2,1)S(1)}, bf16[128,192]{1,0:T(8,128)(2,1)S(1)}, u32[]{:S(2)}, u32[]{:S(2)}) collective-permute-start(bf16[128,192]{1,0:T(8,128)(2,1)S(1)} %get-tuple-element.49), channel_id=1, source_target_pairs={{0,8},{8,16},{16,24},{24,0},{1,9},{9,17},{17,25},{25,1},{2,10},{10... | collective-permute-start | bytes 147464 | tf_op jit(solution)/shard_map/ppermute | solution.py:831
  63.1 2.1 %collective-permute-start.5 = (bf16[128,192]{1,0:T(8,128)(2,1)S(1)}, bf16[128,192]{1,0:T(8,128)(2,1)S(1)}, u32[]{:S(2)}, u32[]{:S(2)}) collective-permute-start(bf16[128,192]{1,0:T(8,128)(2,1)S(1)} %get-tuple-element.50), channel_id=1, source_target_pairs={{0,24},{8,0},{16,8},{24,16},{1,25},{9,1},{17,9},{25,17},{2,26},{10... | collective-permute-start | bytes 147464 | tf_op jit(solution)/shard_map/ppermute | solution.py:831
  65.2 0.2 collective-permute-start.6
  65.4 3.4 %collective-permute-start.7 = (bf16[32,192]{1,0:T(8,128)(2,1)S(1)}, bf16[32,192]{1,0:T(8,128)(2,1)S(1)}, u32[]{:S(2)}, u32[]{:S(2)}) collective-permute-start(bf16[32,192]{1,0:T(8,128)(2,1)S(1)} %get-tuple-element.52), channel_id=1, source_target_pairs={{0,7},{1,0},{2,1},{3,2},{4,3},{5,4},{6,5},{7,6},{8,15},{9,8},{10,9... | collective-permute-start | bytes 36872 | tf_op jit(solution)/shard_map/ppermute | solution.py:831
  68.7 4.6 %conv_back.1.g_ref = f32[32,128,192]{2,1,0:T(8,128)S(1)} custom-call(bf16[34,128,256]{2,1,0:T(8,128)(2,1)S(1)} %get-tuple-element.47.xs_ref, bf16[9,192,192]{2,1,0:T(8,128)(2,1)S(1)} %copy-done, f32[32,128,192]{2,1,0:T(8,128)S(1)} %get-tuple-element.48.add_ref), custom_call_target="tpu_custom_call" | custom-call | tf_op jit(solution)/shard_map/conv_back/pallas_call | solution.py:269
  73.4 0.0 collective-permute-done.6.left_ref
  73.4 0.0 collective-permute-done.7.right_ref
  73.4 0.0 collective-permute-done.4.top_ref
  73.4 0.0 collective-permute-done.5.bot_ref
  73.4 2.4 %finish.1 = f32[32,192,128]{2,1,0:T(8,128)} custom-call(f32[32,128,192]{2,1,0:T(8,128)S(1)} %conv_back.1.g_ref, bf16[9,192,192]{2,1,0:T(8,128)(2,1)S(1)} %copy-done, bf16[128,192]{1,0:T(8,128)(2,1)S(1)} %collective-permute-done.4.top_ref, bf16[128,192]{1,0:T(8,128)(2,1)S(1)} %collective-permute-done.5.bot_ref, ...), custom_call_target="tpu_custom_call" | custom-call | tf_op jit(solution)/shard_map/finish/pallas_call | solution.py:568
Async XLA Ops:
  0.6 12.6 %copy-start.1 = (bf16[32,128,192]{1,2,0:T(8,128)(2,1)S(1)}, bf16[32,128,192]{1,2,0:T(8,128)(2,1)}, u32[]{:S(2)}) copy-start(bf16[32,128,192]{1,2,0:T(8,128)(2,1)} %param.16) | copy-start | bytes 4718596
  0.6 17.1 %copy-start = (bf16[9,192,192]{2,1,0:T(8,128)(2,1)S(1)}, bf16[9,192,192]{2,1,0:T(8,128)(2,1)}, u32[]{:S(2)}) copy-start(bf16[9,192,192]{2,1,0:T(8,128)(2,1)} %w_ref.7) | copy-start | bytes 1990660
  2.9 14.8 %all-to-all-start = ((bf16[32,8,128]{2,1,0:T(8,128)(2,1)}), bf16[32,8,128]{2,1,0:T(8,128)(2,1)S(1)}, u32[]{:S(2)}, u32[]{:S(2)}) async-start(bf16[32,8,128]{2,1,0:T(8,128)(2,1)} %get-tuple-element.28), calls=%async_computation | async-start | bytes 131072 | tf_op jit(solution)/shard_map/all_to_all | solution.py:840
  10.3 11.8 %collective-permute-start = (bf16[128,192]{1,0:T(8,128)(2,1)S(1)}, bf16[128,192]{1,0:T(8,128)(2,1)S(1)}, u32[]{:S(2)}, u32[]{:S(2)}) collective-permute-start(bf16[128,192]{1,0:T(8,128)(2,1)S(1)} %get-tuple-element.33), channel_id=1, source_target_pairs={{0,8},{8,16},{16,24},{24,0},{1,9},{9,17},{17,25},{25,1},{2,10},{10... | collective-permute-start | bytes 147464 | tf_op jit(solution)/shard_map/ppermute | solution.py:831
  12.1 10.0 %collective-permute-start.1 = (bf16[128,192]{1,0:T(8,128)(2,1)S(1)}, bf16[128,192]{1,0:T(8,128)(2,1)S(1)}, u32[]{:S(2)}, u32[]{:S(2)}) collective-permute-start(bf16[128,192]{1,0:T(8,128)(2,1)S(1)} %get-tuple-element.34), channel_id=1, source_target_pairs={{0,24},{8,0},{16,8},{24,16},{1,25},{9,1},{17,9},{25,17},{2,26},{10... | collective-permute-start | bytes 147464 | tf_op jit(solution)/shard_map/ppermute | solution.py:831
  14.1 7.9 %collective-permute-start.2 = (bf16[32,192]{1,0:T(8,128)(2,1)S(1)}, bf16[32,192]{1,0:T(8,128)(2,1)S(1)}, u32[]{:S(2)}, u32[]{:S(2)}) collective-permute-start(bf16[32,192]{1,0:T(8,128)(2,1)S(1)} %get-tuple-element.35), channel_id=1, source_target_pairs={{0,1},{1,2},{2,3},{3,4},{4,5},{5,6},{6,7},{7,0},{8,9},{9,10},{10,1... | collective-permute-start | bytes 36872 | tf_op jit(solution)/shard_map/ppermute | solution.py:831
  14.2 7.9 %collective-permute-start.3 = (bf16[32,192]{1,0:T(8,128)(2,1)S(1)}, bf16[32,192]{1,0:T(8,128)(2,1)S(1)}, u32[]{:S(2)}, u32[]{:S(2)}) collective-permute-start(bf16[32,192]{1,0:T(8,128)(2,1)S(1)} %get-tuple-element.36), channel_id=1, source_target_pairs={{0,7},{1,0},{2,1},{3,2},{4,3},{5,4},{6,5},{7,6},{8,15},{9,8},{10,9... | collective-permute-start | bytes 36872 | tf_op jit(solution)/shard_map/ppermute | solution.py:831
  26.9 13.2 %all-to-all-start.1 = ((bf16[32,32,128]{2,1,0:T(8,128)(2,1)}), bf16[32,32,128]{2,1,0:T(8,128)(2,1)S(1)}, u32[]{:S(2)}, u32[]{:S(2)}) async-start(bf16[32,32,128]{2,1,0:T(8,128)(2,1)} %get-tuple-element.37), calls=%async_computation.1 | async-start | bytes 524288 | tf_op jit(solution)/shard_map/all_to_all | solution.py:840
  37.5 22.2 %copy-start.2 = (bf16[32,128,192]{2,1,0:T(8,128)(2,1)S(1)}, bf16[32,128,192]{2,1,0:T(8,128)(2,1)}, u32[]{:S(2)}) copy-start(bf16[32,128,192]{2,1,0:T(8,128)(2,1)} %get-tuple-element.46.gate_ref) | copy-start | bytes 4718596
  62.2 11.2 %collective-permute-start.4 = (bf16[128,192]{1,0:T(8,128)(2,1)S(1)}, bf16[128,192]{1,0:T(8,128)(2,1)S(1)}, u32[]{:S(2)}, u32[]{:S(2)}) collective-permute-start(bf16[128,192]{1,0:T(8,128)(2,1)S(1)} %get-tuple-element.49), channel_id=1, source_target_pairs={{0,8},{8,16},{16,24},{24,0},{1,9},{9,17},{17,25},{25,1},{2,10},{10... | collective-permute-start | bytes 147464 | tf_op jit(solution)/shard_map/ppermute | solution.py:831
  63.1 10.3 %collective-permute-start.5 = (bf16[128,192]{1,0:T(8,128)(2,1)S(1)}, bf16[128,192]{1,0:T(8,128)(2,1)S(1)}, u32[]{:S(2)}, u32[]{:S(2)}) collective-permute-start(bf16[128,192]{1,0:T(8,128)(2,1)S(1)} %get-tuple-element.50), channel_id=1, source_target_pairs={{0,24},{8,0},{16,8},{24,16},{1,25},{9,1},{17,9},{25,17},{2,26},{10... | collective-permute-start | bytes 147464 | tf_op jit(solution)/shard_map/ppermute | solution.py:831
  65.2 8.2 %collective-permute-start.6 = (bf16[32,192]{1,0:T(8,128)(2,1)S(1)}, bf16[32,192]{1,0:T(8,128)(2,1)S(1)}, u32[]{:S(2)}, u32[]{:S(2)}) collective-permute-start(bf16[32,192]{1,0:T(8,128)(2,1)S(1)} %get-tuple-element.51), channel_id=1, source_target_pairs={{0,1},{1,2},{2,3},{3,4},{4,5},{5,6},{6,7},{7,0},{8,9},{9,10},{10,1... | collective-permute-start | bytes 36872 | tf_op jit(solution)/shard_map/ppermute | solution.py:831
  65.4 8.0 %collective-permute-start.7 = (bf16[32,192]{1,0:T(8,128)(2,1)S(1)}, bf16[32,192]{1,0:T(8,128)(2,1)S(1)}, u32[]{:S(2)}, u32[]{:S(2)}) collective-permute-start(bf16[32,192]{1,0:T(8,128)(2,1)S(1)} %get-tuple-element.52), channel_id=1, source_target_pairs={{0,7},{1,0},{2,1},{3,2},{4,3},{5,4},{6,5},{7,6},{8,15},{9,8},{10,9... | collective-permute-start | bytes 36872 | tf_op jit(solution)/shard_map/ppermute | solution.py:831

commit v8 on v7

--- a/solution.py
+++ b/solution.py
@@ -413,12 +413,17 @@
     mine = corner_tile([slope(v) for v in (final[cols - 1 :], final[0:1], first[cols - 1 :], first[0:1])])
     for k in range(6):
         pack[:, cap + half + k, :] = jnp.broadcast_to(mine[k], (regions, 128))
-    ans_ref[...] = pack[...].astype(BF16)
-    ans_out = pltpu.make_async_copy(ans_ref, ans_hbm, sem.at[1])
-    ans_out.start()
+    size = regions // CHUNKS
+    outs = []
+    for k in range(CHUNKS):
+        at = pl.ds(k * size, size)
+        ans_ref[at] = pack[at].astype(BF16)
+        outs.append(pltpu.make_async_copy(ans_ref.at[at], ans_hbm.at[at], sem.at[3 + k]))
+        outs[-1].start()
     spots_out.wait()
     pre_out.wait()
-    ans_out.wait()
+    for out in outs:
+        out.wait()
 
 
 def sample(y, xs, taps, asked, top, bot, left, right, cap):
@@ -442,7 +447,7 @@
             VMEM((rows, cols, ch), BF16),
             VMEM((regions, deep, 128), BF16),
             VMEM((regions, 128), F32),
-            pltpu.SemaphoreType.DMA((3,)),
+            pltpu.SemaphoreType.DMA((3 + CHUNKS,)),
         ],
         compiler_params=PARAMS,
         name="sample",
@@ -596,8 +601,9 @@
     rank_col, rank_row, route_col = route_parts(route, up(regions, 128))
     upper = jnp.where(rank_col >= half, 1.0, 0.0)
     lane = iota((stations, part_ref.shape[1] - w_ref.shape[0]), 1)
-    main_at = route_col * deep + rank_col
-    rest_at = route_col * deep + cap + rank_col - half * upper
+    dense = cap == 16
+    main_at = route_col * (cap if dense else deep) + rank_col
+    rest_at = route_col * (half if dense else deep) + (0 if dense else cap) + rank_col - half * upper
     part_ref[:, w_ref.shape[0] :] = jnp.where(lane == 0, main_at, jnp.where(lane == 1, rest_at, upper))
 
     row, col, a, b = fine_cell(spot_ref[...].astype(F32), cols)
@@ -730,12 +736,17 @@
     stores[-1].start()
     need(0, 2)
     fetches[10].start()
-    at = iota_f((stations, packed), 1)
-    to = onehot(at == part_ref[:, ch : ch + 1])
-    to_rest = onehot(at == part_ref[:, ch + 1 : ch + 2])
-    flat = ans_ref[...].reshape(packed, 128)
+    if cap == 16:
+        regions, half = ans_ref.shape[0], cap // 2
+        slab = ans_ref[:, cap : cap + 16].astype(F32)
+        flat = ans_ref[:, :cap].reshape(regions * cap, 128)
+        flat_rest = slab[:, :half].reshape(regions * half, 128).astype(BF16)
+    else:
+        flat = flat_rest = ans_ref[...].reshape(packed, 128)
+    to = onehot(iota_f((stations, flat.shape[0]), 1) == part_ref[:, ch : ch + 1])
+    to_rest = onehot(iota_f((stations, flat_rest.shape[0]), 1) == part_ref[:, ch + 1 : ch + 2])
     main = nn(to, flat).astype(BF16)
-    rest = nn(to_rest, flat)
+    rest = nn(to_rest, flat_rest)
     rest = jnp.where(part_ref[:, ch + 2 : ch + 3] > 0.0, pltpu.roll(rest, 64, 1), rest)[:, : ch - 128].astype(BF16)
     embedded = part_ref[:, :ch] + nt(jnp.concatenate([main, rest], axis=1), w_in[:, below:])
     r1 = lax.rsqrt(jnp.sum(embedded * embedded, axis=1, keepdims=True) * inv + EPS)

time: 76.5 us -> 76.3 us (level)
  no operation moved by 1% of the time
where the time goes in v8:
time: 76.3 us; the launch traced here: 75.9 us
  Pallas kernels  34.6 us (45%)
  starting transfers between devices  23.7 us (31%)
  blocking collectives  13.3 us (17%)
  waiting for transfers between devices  2.63 us (3%)
  between operations  1.62 us (2%)
    all_to_all x1, blocking collectives, exchange(): return lax.all_to_all(x, AXES, split_axis=0, concat_axis=0, tiled=True)  13.3 us
    ppermute x8, starting transfers between devices, shift(): return lax.ppermute(x, axis, [(i, (i + step) % n) for i in range(n)])  13.1 us
    all_to_all x2, starting transfers between devices, exchange(): return lax.all_to_all(x, AXES, split_axis=0, concat_axis=0, tiled=True)  10.7 us
    pallas_call x1, Pallas kernels, prepare(): pl.pallas_call(functools.partial(prepare_kernel, cap, tile, n_lon), out_s...  6.55 us
    pallas_call x1, Pallas kernels, stations_pass(): pl.pallas_call(functools.partial(station_kernel, cap), out_shape=outs, in...  6.09 us
    pallas_call x1, Pallas kernels, sample(): pl.pallas_call(functools.partial(sample_kernel, cap), out_shape=(pltpu.HB...  4.9 us
    pallas_call x1, Pallas kernels, conv_back(): pl.pallas_call(conv_back_kernel, out_shape=SDS(add.shape, F32), in_specs=...  4.64 us
    pallas_call x1, Pallas kernels, conv_core(): pl.pallas_call(conv_core_kernel, out_shape=(SDS((rows, cols, ch), F32), S...  4.31 us
  transfers between devices with their start and end apart: 10, of which 1 were waited for; matrix products, arithmetic and copies ran while one was open for 0% of the time, Pallas kernels for 22%

profile of v8, /device:TPU:0, one launch (start us, length us, event | category | flops | bytes accessed | tf_op | source)
XLA Modules:
  0.0 75.9 jit_solution(16681521355869168165)
XLA Ops:
  0.6 0.0 copy-start.1
  0.6 0.0 copy-start
  0.6 2.3 %intro.1 = (bf16[32,8,128]{2,1,0:T(8,128)(2,1)}, bf16[128,192]{1,0:T(8,128)(2,1)S(1)}, bf16[128,192]{1,0:T(8,128)(2,1)S(1)}) custom-call(s32[1,256]{1,0:T(1,128)} %bitcast.18, s32[1,256]{1,0:T(1,128)} %bitcast.20, bf16[32,192,128]{2,1,0:T(8,128)(2,1)} %bitcast.10), custom_call_target="tpu_custom_call" | custom-call | tf_op jit(solution)/shard_map/intro/pallas_call | solution.py:156
  2.9 7.3 %all-to-all-start = ((bf16[32,8,128]{2,1,0:T(8,128)(2,1)}), bf16[32,8,128]{2,1,0:T(8,128)(2,1)S(1)}, u32[]{:S(2)}, u32[]{:S(2)}) async-start(bf16[32,8,128]{2,1,0:T(8,128)(2,1)} %get-tuple-element.28), calls=%async_computation | async-start | bytes 131072 | tf_op jit(solution)/shard_map/all_to_all | solution.py:851
  10.3 1.8 %collective-permute-start = (bf16[128,192]{1,0:T(8,128)(2,1)S(1)}, bf16[128,192]{1,0:T(8,128)(2,1)S(1)}, u32[]{:S(2)}, u32[]{:S(2)}) collective-permute-start(bf16[128,192]{1,0:T(8,128)(2,1)S(1)} %get-tuple-element.33), channel_id=1, source_target_pairs={{0,8},{8,16},{16,24},{24,0},{1,9},{9,17},{17,25},{25,1},{2,10},{10... | collective-permute-start | bytes 147464 | tf_op jit(solution)/shard_map/ppermute | solution.py:842
  12.1 1.2 %collective-permute-start.1 = (bf16[128,192]{1,0:T(8,128)(2,1)S(1)}, bf16[128,192]{1,0:T(8,128)(2,1)S(1)}, u32[]{:S(2)}, u32[]{:S(2)}) collective-permute-start(bf16[128,192]{1,0:T(8,128)(2,1)S(1)} %get-tuple-element.34), channel_id=1, source_target_pairs={{0,24},{8,0},{16,8},{24,16},{1,25},{9,1},{17,9},{25,17},{2,26},{10... | collective-permute-start | bytes 147464 | tf_op jit(solution)/shard_map/ppermute | solution.py:842
  13.2 0.0 copy-done.1
  13.2 0.9 %sides.1 = (bf16[32,192]{1,0:T(8,128)(2,1)S(1)}, bf16[32,192]{1,0:T(8,128)(2,1)S(1)}) custom-call(bf16[32,192,128]{2,1,0:T(8,128)(2,1)S(1)} %bitcast.11), custom_call_target="tpu_custom_call" | custom-call | tf_op jit(solution)/shard_map/sides/pallas_call | solution.py:184
  14.1 0.0 collective-permute-start.2
  14.2 3.6 %collective-permute-start.3 = (bf16[32,192]{1,0:T(8,128)(2,1)S(1)}, bf16[32,192]{1,0:T(8,128)(2,1)S(1)}, u32[]{:S(2)}, u32[]{:S(2)}) collective-permute-start(bf16[32,192]{1,0:T(8,128)(2,1)S(1)} %get-tuple-element.36), channel_id=1, source_target_pairs={{0,7},{1,0},{2,1},{3,2},{4,3},{5,4},{6,5},{7,6},{8,15},{9,8},{10,9... | collective-permute-start | bytes 36872 | tf_op jit(solution)/shard_map/ppermute | solution.py:842
  17.7 0.0 all-to-all-done.asked_ref
  17.7 0.0 copy-done
  17.7 4.3 %conv_core.1 = (f32[32,128,192]{2,1,0:T(8,128)S(1)}, bf16[34,128,256]{2,1,0:T(8,128)(2,1)S(1)}) custom-call(bf16[32,192,128]{2,1,0:T(8,128)(2,1)S(1)} %bitcast.12, bf16[9,192,192]{2,1,0:T(8,128)(2,1)S(1)} %copy-done), custom_call_target="tpu_custom_call" | custom-call | tf_op jit(solution)/shard_map/conv_core/pallas_call | solution.py:254
  22.0 0.0 collective-permute-done.2.left_ref
  22.0 0.0 collective-permute-done.3.right_ref
  22.1 0.0 collective-permute-done.top_ref
  22.1 0.0 collective-permute-done.1.bot_ref
  22.1 4.9 %sample.1 = (bf16[32,32,128]{2,1,0:T(8,128)(2,1)}, bf16[32,128,192]{2,1,0:T(8,128)(2,1)}, f32[32,128]{1,0:T(8,128)}) custom-call(f32[32,128,192]{2,1,0:T(8,128)S(1)} %get-tuple-element.30.y_ref, bf16[34,128,256]{2,1,0:T(8,128)(2,1)S(1)} %get-tuple-element.31.xs_ref, bf16[9,192,192]{2,1,0:T(8,128)(2,1)S(1)} %copy-done, ...), custom_call_target="tpu_custom_call" | custom-call | tf_op jit(solution)/shard_map/sample/pallas_call | solution.py:433
  27.0 3.3 %all-to-all-start.1 = ((bf16[32,32,128]{2,1,0:T(8,128)(2,1)}), bf16[32,32,128]{2,1,0:T(8,128)(2,1)S(1)}, u32[]{:S(2)}, u32[]{:S(2)}) async-start(bf16[32,32,128]{2,1,0:T(8,128)(2,1)} %get-tuple-element.37), calls=%async_computation.1 | async-start | bytes 524288 | tf_op jit(solution)/shard_map/all_to_all | solution.py:851
  31.0 6.5 %prepare.1 = (bf16[1024,768]{1,0:T(8,128)(2,1)}, f32[256,256]{1,0:T(8,128)}, f32[256,256]{1,0:T(8,128)}, bf16[32,128,192]{2,1,0:T(8,128)(2,1)}) custom-call(s32[1]{0:T(128)S(6)} %copy.18.live_ref, s32[1,256]{1,0:T(1,128)} %bitcast.19, s32[1,256]{1,0:T(1,128)} %bitcast.21, s32[16,256]{1,0:T(8,128)} %bitcast.16, s32[1,256]{1,0:T(1,128)} %bitcast.22, ...), custom_call_target="tpu_custom_call" | custom-call | tf_op jit(solution)/shard_map/prepare/pallas_call | solution.py:695
  37.5 0.0 copy-start.2
  37.5 2.6 %all-to-all-done.1.ans_ref = bf16[32,32,128]{2,1,0:T(8,128)(2,1)S(1)} async-done(((bf16[32,32,128]{2,1,0:T(8,128)(2,1)}), bf16[32,32,128]{2,1,0:T(8,128)(2,1)S(1)}, u32[]{:S(2)}, u32[]{:S(2)}) %all-to-all-start.1) | async-done | bytes 262176 | tf_op jit(solution)/shard_map/all_to_all | solution.py:851
  40.1 6.1 %stations.1 = (f32[256,128]{1,0:T(8,128)}, bf16[32,32,128]{2,1,0:T(8,128)(2,1)}, f32[8,192]{1,0:T(8,128)}) custom-call(s32[1]{0:T(128)S(6)} %copy.18.live_ref, bf16[32,32,128]{2,1,0:T(8,128)(2,1)S(1)} %all-to-all-done.1.ans_ref, f32[256,256]{1,0:T(8,128)} %get-tuple-element.39.refs_0_, bf16[192,448]{1,0:T(8,128)(2,1)} %bitcast.15, f32[1,192]{1,0:T(1,128)} %bitcast.23, ...), custom_call_target="tpu_custom_call" | custom-call | tf_op jit(solution)/shard_map/stations/pallas_call | solution.py:823
  46.2 13.3 %all_to_all.15.inc_hbm = bf16[32,32,128]{2,1,0:T(8,128)(2,1)} all-to-all(bf16[32,32,128]{2,1,0:T(8,128)(2,1)} %get-tuple-element.44), channel_id=1, replica_groups=mesh['lat'=4,'lon'=8] {'lat','lon'}, dimensions={0} | all-to-all | bytes 524288 | tf_op jit(solution)/shard_map/all_to_all | solution.py:851
  59.6 0.0 copy-done.2
  59.6 2.5 %spread.1 = (f32[32,128,192]{2,1,0:T(8,128)S(1)}, bf16[34,128,256]{2,1,0:T(8,128)(2,1)S(1)}, bf16[128,192]{1,0:T(8,128)(2,1)S(1)}, bf16[128,192]{1,0:T(8,128)(2,...) custom-call(f32[32,128]{1,0:T(8,128)} %get-tuple-element.43.spots_hbm, ...), custom_call_target="tpu_custom_call" | custom-call | tf_op jit(solution)/shard_map/spread/pallas_call | solution.py:519
  62.1 0.9 %collective-permute-start.4 = (bf16[128,192]{1,0:T(8,128)(2,1)S(1)}, bf16[128,192]{1,0:T(8,128)(2,1)S(1)}, u32[]{:S(2)}, u32[]{:S(2)}) collective-permute-start(bf16[128,192]{1,0:T(8,128)(2,1)S(1)} %get-tuple-element.49), channel_id=1, source_target_pairs={{0,8},{8,16},{16,24},{24,0},{1,9},{9,17},{17,25},{25,1},{2,10},{10... | collective-permute-start | bytes 147464 | tf_op jit(solution)/shard_map/ppermute | solution.py:842
  63.0 2.1 %collective-permute-start.5 = (bf16[128,192]{1,0:T(8,128)(2,1)S(1)}, bf16[128,192]{1,0:T(8,128)(2,1)S(1)}, u32[]{:S(2)}, u32[]{:S(2)}) collective-permute-start(bf16[128,192]{1,0:T(8,128)(2,1)S(1)} %get-tuple-element.50), channel_id=1, source_target_pairs={{0,24},{8,0},{16,8},{24,16},{1,25},{9,1},{17,9},{25,17},{2,26},{10... | collective-permute-start | bytes 147464 | tf_op jit(solution)/shard_map/ppermute | solution.py:842
  65.0 0.2 collective-permute-start.6
  65.2 3.4 %collective-permute-start.7 = (bf16[32,192]{1,0:T(8,128)(2,1)S(1)}, bf16[32,192]{1,0:T(8,128)(2,1)S(1)}, u32[]{:S(2)}, u32[]{:S(2)}) collective-permute-start(bf16[32,192]{1,0:T(8,128)(2,1)S(1)} %get-tuple-element.52), channel_id=1, source_target_pairs={{0,7},{1,0},{2,1},{3,2},{4,3},{5,4},{6,5},{7,6},{8,15},{9,8},{10,9... | collective-permute-start | bytes 36872 | tf_op jit(solution)/shard_map/ppermute | solution.py:842
  68.6 4.6 %conv_back.1.g_ref = f32[32,128,192]{2,1,0:T(8,128)S(1)} custom-call(bf16[34,128,256]{2,1,0:T(8,128)(2,1)S(1)} %get-tuple-element.47.xs_ref, bf16[9,192,192]{2,1,0:T(8,128)(2,1)S(1)} %copy-done, f32[32,128,192]{2,1,0:T(8,128)S(1)} %get-tuple-element.48.add_ref), custom_call_target="tpu_custom_call" | custom-call | tf_op jit(solution)/shard_map/conv_back/pallas_call | solution.py:269
  73.2 0.0 collective-permute-done.6.left_ref
  73.2 0.0 collective-permute-done.7.right_ref
  73.3 0.0 collective-permute-done.4.top_ref
  73.3 0.0 collective-permute-done.5.bot_ref
  73.3 2.4 %finish.1 = f32[32,192,128]{2,1,0:T(8,128)} custom-call(f32[32,128,192]{2,1,0:T(8,128)S(1)} %conv_back.1.g_ref, bf16[9,192,192]{2,1,0:T(8,128)(2,1)S(1)} %copy-done, bf16[128,192]{1,0:T(8,128)(2,1)S(1)} %collective-permute-done.4.top_ref, bf16[128,192]{1,0:T(8,128)(2,1)S(1)} %collective-permute-done.5.bot_ref, ...), custom_call_target="tpu_custom_call" | custom-call | tf_op jit(solution)/shard_map/finish/pallas_call | solution.py:573
Async XLA Ops:
  0.6 12.6 %copy-start.1 = (bf16[32,128,192]{1,2,0:T(8,128)(2,1)S(1)}, bf16[32,128,192]{1,2,0:T(8,128)(2,1)}, u32[]{:S(2)}) copy-start(bf16[32,128,192]{1,2,0:T(8,128)(2,1)} %param.16) | copy-start | bytes 4718596
  0.6 17.1 %copy-start = (bf16[9,192,192]{2,1,0:T(8,128)(2,1)S(1)}, bf16[9,192,192]{2,1,0:T(8,128)(2,1)}, u32[]{:S(2)}) copy-start(bf16[9,192,192]{2,1,0:T(8,128)(2,1)} %w_ref.7) | copy-start | bytes 1990660
  2.9 14.8 %all-to-all-start = ((bf16[32,8,128]{2,1,0:T(8,128)(2,1)}), bf16[32,8,128]{2,1,0:T(8,128)(2,1)S(1)}, u32[]{:S(2)}, u32[]{:S(2)}) async-start(bf16[32,8,128]{2,1,0:T(8,128)(2,1)} %get-tuple-element.28), calls=%async_computation | async-start | bytes 131072 | tf_op jit(solution)/shard_map/all_to_all | solution.py:851
  10.3 11.8 %collective-permute-start = (bf16[128,192]{1,0:T(8,128)(2,1)S(1)}, bf16[128,192]{1,0:T(8,128)(2,1)S(1)}, u32[]{:S(2)}, u32[]{:S(2)}) collective-permute-start(bf16[128,192]{1,0:T(8,128)(2,1)S(1)} %get-tuple-element.33), channel_id=1, source_target_pairs={{0,8},{8,16},{16,24},{24,0},{1,9},{9,17},{17,25},{25,1},{2,10},{10... | collective-permute-start | bytes 147464 | tf_op jit(solution)/shard_map/ppermute | solution.py:842
  12.1 10.0 %collective-permute-start.1 = (bf16[128,192]{1,0:T(8,128)(2,1)S(1)}, bf16[128,192]{1,0:T(8,128)(2,1)S(1)}, u32[]{:S(2)}, u32[]{:S(2)}) collective-permute-start(bf16[128,192]{1,0:T(8,128)(2,1)S(1)} %get-tuple-element.34), channel_id=1, source_target_pairs={{0,24},{8,0},{16,8},{24,16},{1,25},{9,1},{17,9},{25,17},{2,26},{10... | collective-permute-start | bytes 147464 | tf_op jit(solution)/shard_map/ppermute | solution.py:842
  14.1 7.9 %collective-permute-start.2 = (bf16[32,192]{1,0:T(8,128)(2,1)S(1)}, bf16[32,192]{1,0:T(8,128)(2,1)S(1)}, u32[]{:S(2)}, u32[]{:S(2)}) collective-permute-start(bf16[32,192]{1,0:T(8,128)(2,1)S(1)} %get-tuple-element.35), channel_id=1, source_target_pairs={{0,1},{1,2},{2,3},{3,4},{4,5},{5,6},{6,7},{7,0},{8,9},{9,10},{10,1... | collective-permute-start | bytes 36872 | tf_op jit(solution)/shard_map/ppermute | solution.py:842
  14.2 7.9 %collective-permute-start.3 = (bf16[32,192]{1,0:T(8,128)(2,1)S(1)}, bf16[32,192]{1,0:T(8,128)(2,1)S(1)}, u32[]{:S(2)}, u32[]{:S(2)}) collective-permute-start(bf16[32,192]{1,0:T(8,128)(2,1)S(1)} %get-tuple-element.36), channel_id=1, source_target_pairs={{0,7},{1,0},{2,1},{3,2},{4,3},{5,4},{6,5},{7,6},{8,15},{9,8},{10,9... | collective-permute-start | bytes 36872 | tf_op jit(solution)/shard_map/ppermute | solution.py:842
  27.0 13.2 %all-to-all-start.1 = ((bf16[32,32,128]{2,1,0:T(8,128)(2,1)}), bf16[32,32,128]{2,1,0:T(8,128)(2,1)S(1)}, u32[]{:S(2)}, u32[]{:S(2)}) async-start(bf16[32,32,128]{2,1,0:T(8,128)(2,1)} %get-tuple-element.37), calls=%async_computation.1 | async-start | bytes 524288 | tf_op jit(solution)/shard_map/all_to_all | solution.py:851
  37.5 22.1 %copy-start.2 = (bf16[32,128,192]{2,1,0:T(8,128)(2,1)S(1)}, bf16[32,128,192]{2,1,0:T(8,128)(2,1)}, u32[]{:S(2)}) copy-start(bf16[32,128,192]{2,1,0:T(8,128)(2,1)} %get-tuple-element.46.gate_ref) | copy-start | bytes 4718596
  62.1 11.2 %collective-permute-start.4 = (bf16[128,192]{1,0:T(8,128)(2,1)S(1)}, bf16[128,192]{1,0:T(8,128)(2,1)S(1)}, u32[]{:S(2)}, u32[]{:S(2)}) collective-permute-start(bf16[128,192]{1,0:T(8,128)(2,1)S(1)} %get-tuple-element.49), channel_id=1, source_target_pairs={{0,8},{8,16},{16,24},{24,0},{1,9},{9,17},{17,25},{25,1},{2,10},{10... | collective-permute-start | bytes 147464 | tf_op jit(solution)/shard_map/ppermute | solution.py:842
  63.0 10.3 %collective-permute-start.5 = (bf16[128,192]{1,0:T(8,128)(2,1)S(1)}, bf16[128,192]{1,0:T(8,128)(2,1)S(1)}, u32[]{:S(2)}, u32[]{:S(2)}) collective-permute-start(bf16[128,192]{1,0:T(8,128)(2,1)S(1)} %get-tuple-element.50), channel_id=1, source_target_pairs={{0,24},{8,0},{16,8},{24,16},{1,25},{9,1},{17,9},{25,17},{2,26},{10... | collective-permute-start | bytes 147464 | tf_op jit(solution)/shard_map/ppermute | solution.py:842
  65.0 8.2 %collective-permute-start.6 = (bf16[32,192]{1,0:T(8,128)(2,1)S(1)}, bf16[32,192]{1,0:T(8,128)(2,1)S(1)}, u32[]{:S(2)}, u32[]{:S(2)}) collective-permute-start(bf16[32,192]{1,0:T(8,128)(2,1)S(1)} %get-tuple-element.51), channel_id=1, source_target_pairs={{0,1},{1,2},{2,3},{3,4},{4,5},{5,6},{6,7},{7,0},{8,9},{9,10},{10,1... | collective-permute-start | bytes 36872 | tf_op jit(solution)/shard_map/ppermute | solution.py:842
  65.2 8.0 %collective-permute-start.7 = (bf16[32,192]{1,0:T(8,128)(2,1)S(1)}, bf16[32,192]{1,0:T(8,128)(2,1)S(1)}, u32[]{:S(2)}, u32[]{:S(2)}) collective-permute-start(bf16[32,192]{1,0:T(8,128)(2,1)S(1)} %get-tuple-element.52), channel_id=1, source_target_pairs={{0,7},{1,0},{2,1},{3,2},{4,3},{5,4},{6,5},{7,6},{8,15},{9,8},{10,9... | collective-permute-start | bytes 36872 | tf_op jit(solution)/shard_map/ppermute | solution.py:842
